TPU v7x, 256 devices: a whole 4x4x8 slice. The times are simulated.
256 devices in a mesh: span: 32 (over z_hi, x, core), chord: 8 (over z_lo, y).
Axes of the slice: x: 4, y: 4, z: 8 (z_hi: 4, z_lo: 2; z = z_hi * 2 + z_lo), core: 2. Of those that a mesh axis runs over, the one named last changes fastest.
Arguments:
- flow_state: float32 [3, 1024, 64, 1024], P(None, 'span', None, 'chord'), may hold values from -6 to 6
- vel_span: bfloat16 [1024, 64, 1024], P('span', None, 'chord'), may hold values from -1 to 1
- vel_chord: bfloat16 [1024, 64, 1024], P('span', None, 'chord'), may hold values from -1 to 2.5
- viscosity: bfloat16 [1024, 64, 1024], P('span', None, 'chord'), may hold values from 0.0099487305 to 0.119628906
- mixing: float32 [3, 3], replicated, may hold values from -0.5 to 0.5
- te_index: int32 [1024], P('span'), may hold values from 0 to 1023
- band_response: float32 [64, 2, 64], replicated, may hold values from -0.75 to 0.75
- spectra: bfloat16 [1024, 64, 128], P('span', 'chord'), may hold values from -6 to 6
- offsets: int32 [16], replicated, may hold values from 0 to 63
- prior_gram_blocks: float32 [2, 64, 1024, 1024], P(None, 'chord', 'span'), may hold values from -6 to 6
Outputs:
- flow_next: float32 [3, 1024, 64, 1024], P(None, 'span', None, 'chord')
- gram_next: float32 [2, 64, 1024, 1024], P(None, 'chord', 'span')
All inputs are finite; a program needn't handle non-finite values.
Results may differ from a plain program's by a relative error of at most 0.0025.
Values may be sent and summed in bfloat16 or wider, within the bound.
No kernel may reach another device: no remote copies, remote signals or barrier semaphores. Data moves between devices by JAX's collectives and lax.ppermute only.
A program may use at most 128 MiB of HBM per device.

v0:
```python
import jax
import jax.numpy as jnp
from jax import lax
from jax.sharding import PartitionSpec as P

first_coeffs = (0.75, -0.15, 1.0 / 60.0)
second_coeffs = (1.5, -0.15, 1.0 / 90.0)
centre_coeff = -49.0 / 18.0
time_step = 0.6
decay_factor = 0.9


def padded_2(block, sides, width, periodic):
    for axis, dim in sides:
        count = lax.axis_size(axis)
        forward = [(i, i + 1) for i in range(count - 1)]
        if periodic:
            forward.append((count - 1, 0))
        backward = [(target, source) for source, target in forward]
        low = lax.ppermute(
            lax.slice_in_dim(block, block.shape[dim] - width, None, axis=dim), axis, forward
        )
        high = lax.ppermute(lax.slice_in_dim(block, 0, width, axis=dim), axis, backward)
        block = jnp.concatenate([low, block, high], axis=dim)
    return block


def window(padded, axis_pos, length, offset):
    return lax.slice_in_dim(padded, 3 + offset, 3 + offset + length, axis=axis_pos)


def first_diff(padded, axis_pos, length):
    result = first_coeffs[0] * (
        window(padded, axis_pos, length, 1) - window(padded, axis_pos, length, -1)
    )
    for reach in (2, 3):
        result = result + first_coeffs[reach - 1] * (
            window(padded, axis_pos, length, reach) - window(padded, axis_pos, length, -reach)
        )
    return result


def second_diff(padded, axis_pos, length):
    result = centre_coeff * window(padded, axis_pos, length, 0)
    for reach in (1, 2, 3):
        result = result + second_coeffs[reach - 1] * (
            window(padded, axis_pos, length, reach) + window(padded, axis_pos, length, -reach)
        )
    return result


def padded_views(flow):
    span_padding = padded_2(flow, (("span", 1),), 3, True)
    chord_pad = padded_2(flow, (("chord", 3),), 3, False)
    return (span_padding, chord_pad)


def tendency(flow, speed_span, speed_chord, visc, mixing):
    span_len = flow.shape[1]
    normal_len = flow.shape[2]
    chord_len = flow.shape[3]
    span_padding, chord_pad = padded_views(flow)
    normal_pad = jnp.pad(flow, ((0, 0), (0, 0), (3, 3), (0, 0)))
    diffusion = (
        second_diff(span_padding, 1, span_len)
        + second_diff(chord_pad, 3, chord_len)
        + second_diff(normal_pad, 2, normal_len)
    )
    cross_coupling = jnp.einsum("qe,esnc->qsnc", mixing, flow, precision=lax.Precision.HIGHEST)
    return (
        -speed_span * first_diff(span_padding, 1, span_len)
        - speed_chord * first_diff(chord_pad, 3, chord_len)
        + visc * diffusion
        + cross_coupling
    )


def segment_weights(seg_count):
    ramp = (lax.iota(jnp.int32, seg_count + 1) + 1).astype(jnp.float32) / seg_count
    ramp = jnp.minimum(ramp, jnp.float32(1.0))
    return jnp.concatenate([ramp, ramp])


def shards(
    flow_state,
    vel_span,
    vel_chord,
    viscosity,
    mixing,
    te_index,
    band_response,
    spectra,
    offsets,
    prior_gram_blocks,
):
    span_cells = flow_state.shape[1]
    chord_cells = flow_state.shape[3]
    band_count = spectra.shape[1]
    slot_count = spectra.shape[2] // 2
    seg_count = offsets.shape[0]
    chord_pos = lax.axis_index("chord")
    speed_span = vel_span.astype(jnp.float32)
    speed_chord = vel_chord.astype(jnp.float32)
    visc = viscosity.astype(jnp.float32)
    section_one = flow_state + time_step * tendency(
        flow_state, speed_span, speed_chord, visc, mixing
    )
    flow_next = 0.5 * (
        flow_state
        + section_one
        + time_step * tendency(section_one, speed_span, speed_chord, visc, mixing)
    )
    local_col = te_index - chord_pos * chord_cells
    onehot = (lax.iota(jnp.int32, chord_cells)[None, :] == local_col[:, None]).astype(jnp.float32)
    normal_profile = jnp.sum(flow_next[0] * onehot[:, None, :], axis=2)
    complete_profile = lax.psum(normal_profile, "chord")
    local_band_response = lax.dynamic_slice_in_dim(
        band_response, chord_pos * band_count, band_count, 2
    )
    band_magnitude = jnp.einsum(
        "vg,gkl->vlk", complete_profile, local_band_response, precision=lax.Precision.HIGHEST
    ).astype(jnp.bfloat16)
    stored = spectra.reshape(span_cells, band_count, 2, slot_count)
    picked = jnp.take(stored, offsets, axis=3)
    segments = jnp.concatenate([picked, band_magnitude[:, :, :, None]], axis=3)
    depth = 2 * segments.shape[3]
    weights = segment_weights(seg_count)
    own_flat = segments.reshape(span_cells, band_count, depth).astype(jnp.float32) * weights
    turned = (
        jnp.concatenate([segments[:, :, 1], -segments[:, :, 0]], axis=2).astype(jnp.float32)
        * weights
    )
    piece = lax.all_gather(segments, "span", axis=0, tiled=True)
    piece_flat = piece.reshape(piece.shape[0], band_count, depth).astype(jnp.float32)
    real_part = jnp.einsum("ibk,jbk->bij", own_flat, piece_flat, precision=lax.Precision.HIGHEST)
    imag_part = jnp.einsum("ibk,jbk->bij", turned, piece_flat, precision=lax.Precision.HIGHEST)
    gram_block = jnp.stack([real_part, imag_part])
    gram_next = decay_factor * prior_gram_blocks + gram_block
    return (flow_next, gram_next)


def solution(mesh):
    return jax.shard_map(
        shards,
        mesh=mesh,
        in_specs=(
            P(None, "span", None, "chord"),
            P("span", None, "chord"),
            P("span", None, "chord"),
            P("span", None, "chord"),
            P(),
            P("span"),
            P(),
            P("span", "chord", None),
            P(),
            P(None, "chord", "span", None),
        ),
        out_specs=(P(None, "span", None, "chord"), P(None, "chord", "span", None)),
        check_vma=False,
    )
```

profile of v0, /device:TPU:51, one launch (start us, length us, event | category | flops | bytes accessed | tf_op | source)
XLA Modules:
  0.0 320.1 jit_solution(15856583297987222747)
XLA Ops:
  0.6 0.0 copy-start
  0.6 0.0 copy-start.2
  0.7 4.6 %copy.67 = f32[3,32,64,128]{3,0,2,1:T(4,128)S(1)} copy(f32[3,32,64,128]{3,2,1,0:T(8,128)} %param.10) | data formatting | bytes 6291456 | tf_op args[0]
  5.3 2.1 copy-done.4
  7.3 1.0 fusion.41
  8.4 1.8 collective-permute-start.1
  10.1 0.0 collective-permute-start
  10.1 4.0 %fusion.42 = (f32[3,32,64,3]{3,2,1,0:T(8,128)}, f32[3,32,64,3]{3,2,1,0:T(8,128)}) fusion(f32[3,32,64,128]{3,2,1,0:T(8,128)S(1)} %copy-done.2), kind=kLoop, calls=%fused_computation.107 | loop fusion | bytes 294912 | tf_op jit(solution)/shard_map/slice | solution.py:21
  14.1 3.1 copy.84
  17.2 2.2 collective-permute-start.2
  19.4 3.1 copy.85
  22.5 4.0 %collective-permute-start.3 = (f32[3,32,64,3]{2,1,3,0:T(8,128)}, f32[3,32,64,3]{2,1,3,0:T(8,128)}, u32[]{:S(2)}, u32[]{:S(2)}) collective-permute-start(f32[3,32,64,3]{2,1,3,0:T(8,128)} %copy.85), channel_id=1, source_target_pairs={{0,1},{1,2},{2,3},{3,4},{4,5},{5,6},{6,7},{8,9},{9,10},{10,11},{11... | collective-permute-start | bytes 221192 | tf_op jit(solution)/shard_map/ppermute | solution.py:20
  26.6 0.0 copy-done.8
  26.6 2.1 convert_element_type.41
  28.7 2.1 convert_element_type.42
  30.9 2.1 convert_negate_fusion
  33.0 0.2 copy.72
  33.2 0.0 copy-done
  33.2 0.1 constant_dynamic-slice_fusion
  33.3 0.6 gather_fusion
  33.9 0.1 select_bitcast_fusion
  34.0 0.1 fusion.35
  34.1 0.0 collective-permute-done.2
  34.1 4.3 %copy.59 = f32[3,32,64,3]{3,0,2,1:T(4,128)} copy(f32[3,32,64,3]{2,1,3,0:T(8,128)} %collective-permute-done.2) | data formatting | bytes 147456 | tf_op jit(solution)/shard_map/ppermute | solution.py:23
  38.4 0.0 collective-permute-done.3
  38.4 4.4 %copy.61 = f32[3,32,64,3]{3,0,2,1:T(4,128)} copy(f32[3,32,64,3]{2,1,3,0:T(8,128)} %collective-permute-done.3) | data formatting | bytes 147456 | tf_op jit(solution)/shard_map/ppermute | solution.py:20
  42.8 0.0 collective-permute-done.1
  42.8 1.8 constant_dynamic-update-slice_fusion.1
  44.6 6.3 %copy_dynamic-update-slice_fusion.1 = (f32[3,35,64,128]{3,0,2,1:T(4,128)}, f32[3,35,64,128]{3,0,2,1:T(4,128)}) fusion(f32[3,32,64,128]{3,2,1,0:T(8,128)S(1)} %copy-done.2, f32[3,35,64,128]{3,0,2,1:T(4,128)} %constant_dynamic-update-slice_fusion.1), kind=kLoop, calls=%fused_computation.79 | loop fusion | bytes 11534336
  50.9 0.0 collective-permute-done
  50.9 1.8 constant_dynamic-update-slice_fusion
  52.7 50.3 %multiply_add_fusion = f32[3,32,64,128]{3,0,2,1:T(4,128)} fusion(f32[3,32,64,128]{3,0,2,1:T(4,128)} %copy-done.4, f32[3,32,64,3]{3,0,2,1:T(4,128)} %copy.59, f32[3,32,64,3]{3,0,2,1:T(4,128)} %copy.61, f32[3,35,64,128]{3,0,2,1:T(4,128)} %get-tuple-element.15, f32[3,35,64,128]{3,0,2,1:T(4,128)} %constant_dynamic-update-slice_fusion, ...), kind=kOutput, calls=%fused_computation.48 | convolution fusion | flops 75497472 | bytes 48234532 | tf_op jit(solution)/shard_map/qe,esnc->qsnc/dot_general | solution.py:69
  103.1 2.1 fusion.39
  105.2 1.2 collective-permute-start.4
  106.4 1.1 collective-permute-start.5
  107.5 10.0 %fusion.40 = (f32[3,32,64,3]{3,0,2,1:T(4,128)}, f32[3,32,64,3]{3,0,2,1:T(4,128)}) fusion(f32[3,32,64,128]{3,0,2,1:T(4,128)} %multiply_add_fusion), kind=kLoop, calls=%fused_computation.105 | loop fusion | bytes 294912 | tf_op jit(solution)/shard_map/slice | solution.py:21
  117.5 3.4 %copy.68 = f32[3,32,64,3]{2,1,3,0:T(8,128)S(1)} copy(f32[3,32,64,3]{3,0,2,1:T(4,128)} %get-tuple-element.11) | data formatting | bytes 147456 | tf_op jit(solution)/shard_map/slice | solution.py:23
  120.9 1.9 collective-permute-start.6
  122.8 4.3 %copy.70 = f32[3,32,64,3]{2,1,3,0:T(8,128)} copy(f32[3,32,64,3]{3,0,2,1:T(4,128)} %get-tuple-element.10) | data formatting | bytes 147456 | tf_op jit(solution)/shard_map/slice | solution.py:21
  127.2 4.0 %collective-permute-start.7 = (f32[3,32,64,3]{2,1,3,0:T(8,128)}, f32[3,32,64,3]{2,1,3,0:T(8,128)}, u32[]{:S(2)}, u32[]{:S(2)}) collective-permute-start(f32[3,32,64,3]{2,1,3,0:T(8,128)} %copy.70), channel_id=1, source_target_pairs={{0,1},{1,2},{2,3},{3,4},{4,5},{5,6},{6,7},{8,9},{9,10},{10,11},{11... | collective-permute-start | bytes 221192 | tf_op jit(solution)/shard_map/ppermute | solution.py:20
  131.2 0.1 pad_maximum_fusion.7
  131.3 0.0 collective-permute-done.6
  131.3 4.3 %copy.69 = f32[3,32,64,3]{3,0,2,1:T(4,128)} copy(f32[3,32,64,3]{2,1,3,0:T(8,128)} %collective-permute-done.6) | data formatting | bytes 147456 | tf_op jit(solution)/shard_map/ppermute | solution.py:23
  135.6 0.0 collective-permute-done.7
  135.6 4.3 %copy.71 = f32[3,32,64,3]{3,0,2,1:T(4,128)} copy(f32[3,32,64,3]{2,1,3,0:T(8,128)} %collective-permute-done.7) | data formatting | bytes 147456 | tf_op jit(solution)/shard_map/ppermute | solution.py:20
  139.9 0.0 collective-permute-done.4
  139.9 0.0 collective-permute-done.5
  139.9 56.4 %fusion.14 = f32[3,32,64,128]{3,0,2,1:T(4,128)S(1)} fusion(f32[3,32,64,128]{3,0,2,1:T(4,128)} %multiply_add_fusion, f32[3,32,64,3]{3,0,2,1:T(4,128)} %copy.69, f32[3,32,64,3]{3,0,2,1:T(4,128)} %copy.71, f32[3,3,64,128]{3,0,2,1:T(4,128)} %collective-permute-done.4, f32[3,3,64,128]{3,0,2,1:T(4,128)} %collective-permute-done.5, ...), kind=kOutput, calls=%fused_computation.46 | convolution fusion | flops 81788928 | bytes 27000868 | tf_op jit(solution)/shard_map/qe,esnc->qsnc/dot_general | solution.py:69
  196.4 1.9 copy-done.3
  198.3 0.8 slice.276
  199.1 0.3 multiply_reduce_fusion
  199.4 26.1 %psum.7 = f32[32,64]{1,0:T(8,128)S(1)} all-reduce(f32[32,64]{1,0:T(8,128)S(1)} %multiply_reduce_fusion), channel_id=1, replica_groups=mesh['span'=32,'chord'=8] {'chord'}, use_global_device_ids=true, to_apply=%region_1.2 | all-reduce | flops 2048 | bytes 16384 | tf_op jit(solution)/shard_map/psum | solution.py:116
  225.5 0.2 fusion.23
  225.8 0.1 fusion.38
  225.9 4.3 %copy.82 = f32[3,32,64,128]{3,2,1,0:T(8,128)} copy(f32[3,32,64,128]{3,0,2,1:T(4,128)} %copy-done.3) | data formatting | bytes 6291456
  230.2 0.2 copy.75
  230.4 80.2 %all_gather.3 = bf16[1024,8,2,17]{3,1,2,0:T(8,128)(2,1)} all-gather(bf16[32,8,2,17]{3,1,2,0:T(8,128)(2,1)S(1)} %copy.75), channel_id=1, replica_groups=mesh['span'=32,'chord'=8] {'span'}, dimensions={0}, use_global_device_ids=true | all-gather | bytes 574464 | tf_op jit(solution)/shard_map/all_gather | solution.py:133
  310.6 5.0 %copy.76 = bf16[1024,8,2,17]{0,1,3,2:T(8,128)(2,1)S(1)} copy(bf16[1024,8,2,17]{3,1,2,0:T(8,128)(2,1)} %all_gather.3) | data formatting | bytes 1114112 | tf_op jit(solution)/shard_map/all_gather | solution.py:133
  315.6 0.0 copy-start.5
  315.6 0.1 bitcast_multiply_fusion
  315.8 0.0 copy-start.1
  315.8 1.3 convolution_bitcast_fusion.1
  317.0 1.3 convolution_bitcast_fusion
  318.3 1.8 maximum_add_fusion
  (19 shorter events, 0.1 us)
Async XLA Ops:
  0.6 32.6 %copy-start = (f32[64,2,64]{2,1,0:T(2,128)S(1)}, f32[64,2,64]{2,1,0:T(2,128)}, u32[]{:S(2)}) copy-start(f32[64,2,64]{2,1,0:T(2,128)} %param.16) | copy-start | bytes 98308
  0.6 9.5 %copy-start.2 = (f32[3,32,64,128]{3,2,1,0:T(8,128)S(1)}, f32[3,32,64,128]{3,2,1,0:T(8,128)}, u32[]{:S(2)}) copy-start(f32[3,32,64,128]{3,2,1,0:T(8,128)} %param.10) | copy-start | bytes 9437188
  5.3 2.1 copy-start.4
  8.4 34.4 %collective-permute-start.1 = (f32[3,3,64,128]{3,0,2,1:T(4,128)}, f32[3,3,64,128]{3,0,2,1:T(4,128)}, u32[]{:S(2)}, u32[]{:S(2)}) collective-permute-start(f32[3,3,64,128]{3,0,2,1:T(4,128)} %get-tuple-element.13), channel_id=1, source_target_pairs={{0,8},{8,16},{16,24},{24,32},{32,40},{40,48},{48,56},{56,64},{64,7... | collective-permute-start | bytes 884744 | tf_op jit(solution)/shard_map/ppermute | solution.py:20
  10.1 40.8 %collective-permute-start = (f32[3,3,64,128]{3,0,2,1:T(4,128)}, f32[3,3,64,128]{3,0,2,1:T(4,128)}, u32[]{:S(2)}, u32[]{:S(2)}) collective-permute-start(f32[3,3,64,128]{3,0,2,1:T(4,128)} %get-tuple-element.12), channel_id=1, source_target_pairs={{8,0},{16,8},{24,16},{32,24},{40,32},{48,40},{56,48},{64,56},{72,6... | collective-permute-start | bytes 884744 | tf_op jit(solution)/shard_map/ppermute | solution.py:23
  14.1 12.4 %copy-start.8 = (s32[16]{0:T(128)S(1)}, s32[16]{0:T(128)}, u32[]{:S(2)}) copy-start(s32[16]{0:T(128)} %param.18) | copy-start | bytes 196
  17.2 15.7 %copy-start.6 = (bf16[32,8,128]{2,1,0:T(8,128)(2,1)S(1)}, bf16[32,8,128]{2,1,0:T(8,128)(2,1)}, u32[]{:S(2)}) copy-start(bf16[32,8,128]{2,1,0:T(8,128)(2,1)} %param.17) | copy-start | bytes 196612
  17.2 16.0 %copy-start.9 = (s32[32]{0:T(128)S(1)}, s32[32]{0:T(128)}, u32[]{:S(2)}) copy-start(s32[32]{0:T(128)} %param.15) | copy-start | bytes 388
  17.2 16.9 %collective-permute-start.2 = (f32[3,32,64,3]{2,1,3,0:T(8,128)}, f32[3,32,64,3]{2,1,3,0:T(8,128)}, u32[]{:S(2)}, u32[]{:S(2)}) collective-permute-start(f32[3,32,64,3]{2,1,3,0:T(8,128)} %copy.84), channel_id=1, source_target_pairs={{1,0},{2,1},{3,2},{4,3},{5,4},{6,5},{7,6},{9,8},{10,9},{11,10},{12... | collective-permute-start | bytes 221192 | tf_op jit(solution)/shard_map/ppermute | solution.py:23
  22.5 15.9 %collective-permute-start.3 = (f32[3,32,64,3]{2,1,3,0:T(8,128)}, f32[3,32,64,3]{2,1,3,0:T(8,128)}, u32[]{:S(2)}, u32[]{:S(2)}) collective-permute-start(f32[3,32,64,3]{2,1,3,0:T(8,128)} %copy.85), channel_id=1, source_target_pairs={{0,1},{1,2},{2,3},{3,4},{4,5},{5,6},{6,7},{8,9},{9,10},{10,11},{11... | collective-permute-start | bytes 221192 | tf_op jit(solution)/shard_map/ppermute | solution.py:20
  44.6 8.1 %copy-start.7 = (f32[3,3]{1,0:T(4,128)S(1)}, f32[3,3]{1,0:T(4,128)}, u32[]{:S(2)}) copy-start(f32[3,3]{1,0:T(4,128)} %param.14) | copy-start | bytes 112
  105.2 34.7 %collective-permute-start.4 = (f32[3,3,64,128]{3,0,2,1:T(4,128)}, f32[3,3,64,128]{3,0,2,1:T(4,128)}, u32[]{:S(2)}, u32[]{:S(2)}) collective-permute-start(f32[3,3,64,128]{3,0,2,1:T(4,128)} %get-tuple-element.9), channel_id=1, source_target_pairs={{8,0},{16,8},{24,16},{32,24},{40,32},{48,40},{56,48},{64,56},{72,6... | collective-permute-start | bytes 884744 | tf_op jit(solution)/shard_map/ppermute | solution.py:23
  106.4 33.5 %collective-permute-start.5 = (f32[3,3,64,128]{3,0,2,1:T(4,128)}, f32[3,3,64,128]{3,0,2,1:T(4,128)}, u32[]{:S(2)}, u32[]{:S(2)}) collective-permute-start(f32[3,3,64,128]{3,0,2,1:T(4,128)} %get-tuple-element.8), channel_id=1, source_target_pairs={{0,8},{8,16},{16,24},{24,32},{32,40},{40,48},{48,56},{56,64},{64,7... | collective-permute-start | bytes 884744 | tf_op jit(solution)/shard_map/ppermute | solution.py:20
  120.9 10.4 %collective-permute-start.6 = (f32[3,32,64,3]{2,1,3,0:T(8,128)S(1)}, f32[3,32,64,3]{2,1,3,0:T(8,128)}, u32[]{:S(2)}, u32[]{:S(2)}) collective-permute-start(f32[3,32,64,3]{2,1,3,0:T(8,128)S(1)} %copy.68), channel_id=1, source_target_pairs={{1,0},{2,1},{3,2},{4,3},{5,4},{6,5},{7,6},{9,8},{10,9},{11,10},{12... | collective-permute-start | bytes 221192 | tf_op jit(solution)/shard_map/ppermute | solution.py:23
  127.2 8.4 %collective-permute-start.7 = (f32[3,32,64,3]{2,1,3,0:T(8,128)}, f32[3,32,64,3]{2,1,3,0:T(8,128)}, u32[]{:S(2)}, u32[]{:S(2)}) collective-permute-start(f32[3,32,64,3]{2,1,3,0:T(8,128)} %copy.70), channel_id=1, source_target_pairs={{0,1},{1,2},{2,3},{3,4},{4,5},{5,6},{6,7},{8,9},{9,10},{10,11},{11... | collective-permute-start | bytes 221192 | tf_op jit(solution)/shard_map/ppermute | solution.py:20
  196.4 1.9 copy-start.3
  315.6 2.7 copy-start.5
  315.8 4.3 %copy-start.1 = (f32[64,2,64]{2,1,0:T(2,128)S(1)}, f32[64,2,64]{2,1,0:T(2,128)}, u32[]{:S(2)}) copy-start(f32[64,2,64]{2,1,0:T(2,128)} %param.16) | copy-start | bytes 98308
where the time goes:
time: 321 us; the launch traced here: 320 us
  matrix products  110 us (34%)
  blocking collectives  106 us (33%)
  local copies, waits for them, and re-layouts  78.2 us (24%)
  starting transfers between devices  16.2 us (5%)
  other arithmetic  8.9 us (3%)
    dot_general x2, matrix products, tendency(): jnp.einsum('qe,esnc->qsnc', mixing, flow, precision=lax.Precision.HIGHEST)  107 us
    all_gather x1, blocking collectives, shards(): piece = lax.all_gather(segments, 'span', axis=0, tiled=True)  80.2 us
    unnamed x27, local copies, waits for them, and re-layouts  27.5 us
    psum x1, blocking collectives, shards(): complete_profile = lax.psum(normal_profile, 'chord')  26.1 us
    slice x4, local copies, waits for them, and re-layouts, padded_2(): lax.slice_in_dim(block, block.shape[dim] - width, None, axis=dim)  20.4 us
    ppermute x4, starting transfers between devices, padded_2(): lax.ppermute(lax.slice_in_dim(block, block.shape[dim] - width, None, axis...  10.9 us
    ppermute x2, local copies, waits for them, and re-layouts, padded_2(): lax.ppermute(lax.slice_in_dim(block, block.shape[dim] - width, None, axis...  8.69 us
    ppermute x2, local copies, waits for them, and re-layouts, padded_2(): lax.ppermute(lax.slice_in_dim(block, 0, width, axis=dim), axis, backward)  8.61 us
  transfers between devices with their start and end apart: 8, of which 0 were waited for; matrix products, arithmetic and copies ran while one was open for 19% of the time, Pallas kernels for 0%

commit v1 on v0

v1 whole, which is shorter than its diff:
```python
import functools

import jax
import jax.numpy as jnp
import ml_dtypes
import numpy as np
from jax import lax
from jax.experimental import pallas as pl
from jax.experimental.pallas import tpu as pltpu
from jax.sharding import PartitionSpec as P

FIRST = (45, -9, 1)
SECOND = (270, -27, 2)
CENTRE = -490
TIME_STEP = 0.6
DECAY = 0.9
F32 = jnp.float32
BF16 = jnp.bfloat16
LANES = 128


def chord_matrices():
    inner = np.zeros((LANES, 2 * LANES), np.float32)
    halo = np.zeros((8, 2 * LANES), np.float32)

    def row(cell):
        if cell < 0:
            return halo, cell + 3
        if cell >= LANES:
            return halo, cell - LANES + 3
        return inner, cell

    for cell in range(LANES):
        inner[cell, LANES + cell] += CENTRE
        for reach in (1, 2, 3):
            for sign in (1, -1):
                table, index = row(cell + sign * reach)
                table[index, cell] += sign * FIRST[reach - 1]
                table[index, LANES + cell] += SECOND[reach - 1]
    edges = np.zeros((8, LANES), np.float32)
    for k in range(3):
        edges[k, LANES - 3 + k] = 1
        edges[3 + k, k] = 1
    bf = ml_dtypes.bfloat16
    return (
        np.concatenate([inner, inner]).astype(bf),
        halo.astype(bf),
        np.concatenate([edges, edges], axis=1).astype(bf),
    )


def split_two(x):
    high = x.astype(BF16)
    low = (x - high.astype(F32)).astype(BF16)
    return jnp.concatenate([high, low], axis=1)


def nt_dot(a, b):
    return lax.dot_general(a, b, (((1,), (1,)), ((), ())), preferred_element_type=F32)


def edges_kernel(flow_ref, pick_ref, right_ref, left_ref, *, pairs):
    quantities = flow_ref.shape[0]
    for q in range(quantities):
        for p in range(pairs):
            slab = flow_ref[q, 2 * p : 2 * p + 2].reshape(LANES, LANES)
            got = nt_dot(pick_ref[...], split_two(slab))
            for k in range(3):
                right_ref[0, k, q * pairs + p, :] = got[k, :]
                left_ref[0, k, q * pairs + p, :] = got[3 + k, :]


def section_kernel(
    *refs, quantities, second, profile, carried
):
    refs = list(refs)
    take = refs.pop
    state_hbm = take(0)
    span_low, span_high, chord_low, chord_high = (take(0) for _ in range(4))
    vs_hbm, vc_hbm, nu_hbm = (take(0) for _ in range(3))
    mix = take(0)
    inner_ref, halo_ref, pick_ref = (take(0) for _ in range(3))
    if second:
        flow_hbm = take(0)
    if profile:
        te_ref, band_ref = take(0), take(0)
    if carried:
        take(0)
    out_hbm = take(0)
    if not second:
        low_out, high_out, right_out, left_out = (take(0) for _ in range(4))
    if profile:
        amp_out = take(0)
    wide, result, chord, halos, vs, vc, nu, in_sem, out_sem = (take(0) for _ in range(9))
    if second:
        before, before_sem = take(0), take(0)
    if profile:
        columns, amps = take(0), take(0)

    count = len(quantities)
    first_q = quantities[0]
    stations, normal = vs.shape[0], vs.shape[1]
    chunks, pairs = 4, stations // 2
    per = stations // chunks

    def copies(c):
        rows = pl.ds(per * c, per)
        todo = [
            pltpu.make_async_copy(
                state_hbm.at[:, rows],
                wide.at[:, pl.ds(3 + per * c, per), pl.ds(8, normal), :],
                in_sem.at[0, c],
            ),
            pltpu.make_async_copy(vs_hbm.at[rows], vs.at[rows], in_sem.at[1, c]),
            pltpu.make_async_copy(vc_hbm.at[rows], vc.at[rows], in_sem.at[2, c]),
            pltpu.make_async_copy(nu_hbm.at[rows], nu.at[rows], in_sem.at[3, c]),
        ]
        if second:
            todo.append(
                pltpu.make_async_copy(
                    flow_hbm.at[pl.ds(first_q, count), rows], before.at[:, rows], before_sem.at[c]
                )
            )
        return todo

    for c in range(chunks):
        for copy in copies(c):
            copy.start()

    nothing = jnp.zeros(wide.shape[:2] + (8, LANES), F32)
    wide[:, :, 0:8, :] = nothing
    wide[:, :, 8 + normal : 16 + normal, :] = nothing
    wide[:, 0:3, 8 : 8 + normal, :] = span_low[...].astype(F32)
    wide[:, 3 + stations : 6 + stations, 8 : 8 + normal, :] = span_high[...].astype(F32)
    slabs = chord_low.shape[1]
    for k in range(3):
        halos[pl.ds(k, slabs, stride=8), :] = chord_low[k]
        halos[pl.ds(3 + k, slabs, stride=8), :] = chord_high[k]
    for k in (6, 7):
        halos[pl.ds(k, slabs, stride=8), :] = jnp.zeros((slabs, LANES), F32)
    if profile:
        columns[...] = jnp.zeros(columns.shape, F32)

    def matmuls(p):
        slot = p % 2
        for local, q in enumerate(quantities):
            slab = wide[q, pl.ds(3 + 2 * p, 2), 8 : 8 + normal, :].reshape(LANES, LANES)
            start = pl.multiple_of((q * pairs + p) * 8, 8)
            halo = halos[pl.ds(start, 8), :].T.astype(BF16)
            chord[slot, local] = jnp.dot(
                split_two(slab), inner_ref[...], preferred_element_type=F32
            ) + jnp.dot(halo, halo_ref[...], preferred_element_type=F32)

    def edge_cells(p):
        for q in quantities:
            slab = result[q - first_q, pl.ds(2 * p, 2)].reshape(LANES, LANES)
            got = nt_dot(pick_ref[...], split_two(slab))
            for k in range(3):
                right_out[k, pl.ds(q * pairs + p, 1), :] = got[k : k + 1, :]
                left_out[k, pl.ds(q * pairs + p, 1), :] = got[3 + k : 4 + k, :]

    scale = 0.5 if second else 1.0
    couple = [
        [
            scale * ((1.0 if q == e else 0.0) + TIME_STEP * mix[q, e])
            for e in range(wide.shape[0])
        ]
        for q in quantities
    ]
    lane = lax.broadcasted_iota(jnp.int32, (16, LANES), 1)

    def body(p, carry):
        matmuls(jnp.minimum(p + 1, pairs - 1))
        slot = p % 2
        for half in range(2):
            s = 2 * p + half
            for tile in range(normal // 16):
                rows = slice(16 * tile, 16 * tile + 16)
                a = vs[s, rows, :].astype(F32) * (-scale * TIME_STEP / 60)
                b = vc[s, rows, :].astype(F32) * (-scale * TIME_STEP / 60)
                g = nu[s, rows, :].astype(F32) * (scale * TIME_STEP / 180)
                centre = [
                    wide[e, 3 + s, 8 + 16 * tile : 24 + 16 * tile, :]
                    for e in range(wide.shape[0])
                ]
                for local, q in enumerate(quantities):

                    def at(ds, dn):
                        low = 8 + 16 * tile + dn
                        return wide[q, 3 + s + ds, low : low + 16, :]

                    first = None
                    both = None
                    for reach in (1, 2, 3):
                        up, down = at(reach, 0), at(-reach, 0)
                        diff = up - down
                        total = (up + down) + (at(0, reach) + at(0, -reach))
                        if FIRST[reach - 1] != 1:
                            diff = diff * float(FIRST[reach - 1])
                        total = total * float(SECOND[reach - 1])
                        first = diff if first is None else first + diff
                        both = total if both is None else both + total
                    crow = slice(64 * half + 16 * tile, 64 * half + 16 * tile + 16)
                    chord_first = chord[slot, local, crow, 0:LANES]
                    chord_second = chord[slot, local, crow, LANES : 2 * LANES]
                    both = both + (centre[q] * float(2 * CENTRE) + chord_second)
                    value = a * first + b * chord_first + g * both
                    for e in range(wide.shape[0]):
                        value = value + couple[local][e] * centre[e]
                    if second:
                        value = value + 0.5 * before[local, s, rows, :]
                    result[local, s, rows, :] = value
                    if profile:
                        hit = jnp.where(lane == te_ref[s], value, 0.0)
                        column = jnp.sum(hit, axis=1, keepdims=True)
                        columns[rows, :] += jnp.where(lane == s, column, 0.0)
        both_stations = pl.ds(2 * p, 2)
        pltpu.make_async_copy(
            result.at[:, both_stations],
            out_hbm.at[pl.ds(first_q, count), both_stations],
            out_sem.at[p],
        ).start()
        if not second:
            edge_cells(p)
        return carry

    def arrive(c):
        for copy in copies(c):
            copy.wait()

    arrive(0)
    matmuls(0)
    for c in range(chunks):
        if c + 1 < chunks:
            arrive(c + 1)
        lax.fori_loop(c * pairs // chunks, (c + 1) * pairs // chunks, body, 0)

    if not second:
        low_out[...] = result[:, 0:3].astype(BF16)
        high_out[...] = result[:, stations - 3 : stations].astype(BF16)
    if profile:
        amp = lax.dot_general(
            columns[...].T,
            band_ref[...],
            (((1,), (0,)), ((), ())),
            precision=lax.Precision.HIGHEST,
            preferred_element_type=F32,
        )
        amps[...] = amp[:stations].astype(BF16).astype(F32)
        lane4 = lax.broadcasted_iota(jnp.int32, (4, LANES), 1) // 16
        pieces = [jnp.zeros((4, LANES), F32) for _ in range(8)]
        for u in range(8):
            some = amps[pl.ds(u, 4, stride=8), :]
            for j in range(8):
                shift = (16 * (u - j)) % LANES
                moved = pltpu.roll(some, shift, 1) if shift else some
                pieces[j] = jnp.where(lane4 == u, moved, pieces[j])
        for j in range(8):
            amp_out[j] = pieces[j]

    def drain(p, carry):
        both_stations = pl.ds(2 * p, 2)
        pltpu.make_async_copy(
            result.at[:, both_stations],
            out_hbm.at[pl.ds(first_q, count), both_stations],
            out_sem.at[p],
        ).wait()
        return carry

    lax.fori_loop(0, pairs, drain, 0)


def section(
    state,
    halos,
    fields,
    mixing,
    tables,
    quantities,
    flow=None,
    te_local=None,
    band_table=None,
    onto=None,
):
    all_q, stations, normal, _ = state.shape
    second = flow is not None
    profile = te_local is not None
    carried = onto is not None
    count = len(quantities)
    pairs = stations // 2
    hbm = pl.BlockSpec(memory_space=pl.ANY)
    vmem = pl.BlockSpec(memory_space=pltpu.VMEM)
    smem = pl.BlockSpec(memory_space=pltpu.SMEM)
    args = [state, *halos, *fields, mixing, *tables]
    specs = [hbm] + [vmem] * 4 + [hbm] * 3 + [smem] + [vmem] * 3
    if second:
        args.append(flow)
        specs.append(hbm)
    if profile:
        args += [te_local, band_table]
        specs += [smem, vmem]
    aliases = {}
    if carried:
        aliases = {len(args): 0}
        args.append(onto)
        specs.append(hbm)
    shapes = [jax.ShapeDtypeStruct(state.shape, F32)]
    outs = [hbm]
    if not second:
        shapes += [jax.ShapeDtypeStruct((all_q, 3, normal, LANES), BF16)] * 2
        shapes += [jax.ShapeDtypeStruct((3, all_q * pairs, LANES), F32)] * 2
        outs += [vmem] * 4
    if profile:
        shapes.append(jax.ShapeDtypeStruct((8, 4, LANES), F32))
        outs.append(vmem)
    scratch = [
        pltpu.VMEM((all_q, stations + 6, normal + 16, LANES), F32),
        pltpu.VMEM((count, stations, normal, LANES), F32),
        pltpu.VMEM((2, count, LANES, 2 * LANES), F32),
        pltpu.VMEM((all_q * pairs * 8, LANES), F32),
        pltpu.VMEM((stations, normal, LANES), BF16),
        pltpu.VMEM((stations, normal, LANES), BF16),
        pltpu.VMEM((stations, normal, LANES), BF16),
        pltpu.SemaphoreType.DMA((4, 4)),
        pltpu.SemaphoreType.DMA((pairs,)),
    ]
    if second:
        scratch += [
            pltpu.VMEM((count, stations, normal, LANES), F32),
            pltpu.SemaphoreType.DMA((4,)),
        ]
    if profile:
        scratch += [pltpu.VMEM((normal, LANES), F32), pltpu.VMEM((stations, LANES), F32)]
    return pl.pallas_call(
        functools.partial(
            section_kernel,
            quantities=quantities,
            second=second,
            profile=profile,
            carried=carried,
        ),
        out_shape=tuple(shapes),
        in_specs=specs,
        out_specs=tuple(outs),
        scratch_shapes=scratch,
        input_output_aliases=aliases,
        compiler_params=pltpu.CompilerParams(vmem_limit_bytes=40 << 20),
        cost_estimate=pl.CostEstimate(
            flops=20000000 * count, transcendentals=0, bytes_accessed=5000000 * count
        ),
        name="section_" + ("two" if second else "one") + "_" + "".join(map(str, quantities)),
    )(*args)


def stored_kernel(prior_ref, left_ref, all_ref, out_ref, *, bands):
    step = pl.program_id(1)
    stations = left_ref.shape[2]
    lane_band = lax.broadcasted_iota(jnp.int32, (stations, 2 * LANES), 1) // 32
    parts = []
    for level in range(2):
        for b in range(bands):
            parts.append(jnp.where(lane_band == step * bands + b, left_ref[0, level], 0.0))
    left = jnp.concatenate(parts).astype(BF16)
    got = nt_dot(left, all_ref[...])
    half = bands * stations
    total = got[:half] + got[half:]
    out_ref[0] = DECAY * prior_ref[0] + total.reshape(bands, stations, -1)


def amplitude_kernel(known_ref, amp_ref, where_ref, rep_ref, out_ref, spread, left, *, bands):
    kind, step = pl.program_id(0), pl.program_id(1)
    stations = left.shape[1]
    rows = amp_ref.shape[0]

    @pl.when(jnp.logical_and(kind == 0, step == 0))
    def _():
        lane = lax.broadcasted_iota(jnp.int32, (8, LANES), 1) // 16
        own = lane == lax.broadcasted_iota(jnp.int32, (8, LANES), 0)
        for r in range(0, rows, 2):
            two = [
                jnp.where(own, jnp.broadcast_to(amp_ref[r + d : r + d + 1, :], (8, LANES)), 0.0)
                for d in range(2)
            ]
            spread[8 * r : 8 * r + 16, :] = jnp.concatenate(two).astype(BF16)
        first = pl.multiple_of(where_ref[0] * stations, stations)
        mine = spread[pl.ds(first, stations), :]
        for c in range(2):
            left[c] = jnp.dot(mine, rep_ref[c], preferred_element_type=F32)

    lane_band = lax.broadcasted_iota(jnp.int32, (stations, LANES), 1) % 8
    parts = [
        jnp.where(lane_band == step * bands + b, left[kind], 0.0) for b in range(bands)
    ]
    got = nt_dot(jnp.concatenate(parts).astype(BF16), spread[...])
    out_ref[0] = known_ref[0] + got.reshape(bands, stations, -1)


def amplitude_tables():
    index = np.arange(LANES)
    same = (index[:, None] % 16 == index[None, :] % 16).astype(np.float32)
    other = (index[:, None] % 8 == index[None, :] % 8) & (
        (index[:, None] % 16) // 8 != (index[None, :] % 16) // 8
    )
    sign = np.where((index % 16) // 8 == 0, 1.0, -1.0)
    return np.stack([same, other * sign[None, :]]).astype(ml_dtypes.bfloat16)


def shards(
    flow_state,
    vel_span,
    vel_chord,
    viscosity,
    mixing,
    te_index,
    band_response,
    spectra,
    offsets,
    prior_gram_blocks,
):
    quantities, stations, normal, cells = flow_state.shape
    bands, slots = spectra.shape[1], spectra.shape[2] // 2
    segs = offsets.shape[0]
    pairs = stations // 2
    span_n, chord_n = lax.axis_size("span"), lax.axis_size("chord")
    span_pos, chord_pos = lax.axis_index("span"), lax.axis_index("chord")
    tables = chord_matrices()
    fields = (vel_span, vel_chord, viscosity)

    def exchange(low, high, right, left):
        up = [(i, (i + 1) % span_n) for i in range(span_n)]
        down = [(b, a) for a, b in up]
        forward = [(i, i + 1) for i in range(chord_n - 1)]
        backward = [(b, a) for a, b in forward]
        return (
            lax.ppermute(high, "span", up),
            lax.ppermute(low, "span", down),
            lax.ppermute(right, "chord", forward),
            lax.ppermute(left, "chord", backward),
        )

    blocks = 8
    per = stations // blocks
    right, left = pl.pallas_call(
        functools.partial(edges_kernel, pairs=per // 2),
        grid=(blocks,),
        out_shape=(jax.ShapeDtypeStruct((blocks, 3, quantities * per // 2, LANES), F32),) * 2,
        in_specs=[
            pl.BlockSpec((quantities, per, normal, cells), lambda i: (0, i, 0, 0)),
            pl.BlockSpec(tables[2].shape, lambda i: (0, 0)),
        ],
        out_specs=(
            pl.BlockSpec((1, 3, quantities * per // 2, LANES), lambda i: (i, 0, 0, 0)),
        )
        * 2,
        name="edges",
    )(flow_state, tables[2])

    def slab_order(x):
        x = x.reshape(blocks, 3, quantities, per // 2, LANES)
        return x.transpose(1, 2, 0, 3, 4).reshape(3, quantities * pairs, LANES)

    halos = exchange(
        flow_state[:, :3].astype(BF16),
        flow_state[:, stations - 3 :].astype(BF16),
        slab_order(right),
        slab_order(left),
    )

    rows = lax.broadcasted_iota(jnp.int32, (2 * slots, 2 * segs), 0)
    cols = lax.broadcasted_iota(jnp.int32, (2 * slots, 2 * segs), 1)
    wanted = jnp.concatenate([offsets, offsets + slots])
    choose = (rows == wanted[None, :]).astype(BF16)
    picked = jnp.dot(
        spectra.reshape(stations * bands, 2 * slots), choose, preferred_element_type=F32
    )
    packed = picked.astype(BF16).reshape(stations, bands * 2 * segs)
    every = lax.all_to_all(
        jnp.broadcast_to(packed[None], (span_n,) + packed.shape), "span", 0, 0, tiled=True
    ).reshape(span_n * stations, bands * 2 * segs)
    ramp = (jnp.arange(segs, dtype=jnp.int32) + 1).astype(F32) / segs
    quad = packed.astype(F32).reshape(stations, bands, 2, segs) * ramp
    turned = jnp.stack([quad[:, :, 1], -quad[:, :, 0]], axis=2)
    lefts = jnp.stack([quad, turned]).reshape(2, stations, bands * 2 * segs)
    lefts_high = lefts.astype(BF16).astype(F32)
    lefts = jnp.stack([lefts_high, lefts - lefts_high], axis=1)

    section_one, low, high, right, left = section(
        flow_state, halos, fields, mixing, tables, (0, 1, 2)
    )
    halos = exchange(low, high, right, left)

    group = 4
    gram_block = pl.BlockSpec(
        (1, group, stations, span_n * stations), lambda c, g: (c, g, 0, 0)
    )
    known = pl.pallas_call(
        functools.partial(stored_kernel, bands=group),
        grid=(2, bands // group),
        out_shape=jax.ShapeDtypeStruct(prior_gram_blocks.shape, F32),
        in_specs=[
            gram_block,
            pl.BlockSpec((1, 2, stations, bands * 2 * segs), lambda c, g: (c, 0, 0, 0)),
            pl.BlockSpec((span_n * stations, bands * 2 * segs), lambda c, g: (0, 0)),
        ],
        out_specs=gram_block,
        name="gram_stored",
        cost_estimate=pl.CostEstimate(
            flops=20000000, transcendentals=0, bytes_accessed=5000000
        ),
    )(prior_gram_blocks, lefts, every)

    te_local = te_index - chord_pos * cells
    band_table = band_response.reshape(normal, 2, chord_n, bands).transpose(0, 2, 1, 3)
    band_table = band_table.reshape(normal, chord_n * 2 * bands)
    flow_next, amps = section(
        section_one,
        halos,
        fields,
        mixing,
        tables,
        (0,),
        flow=flow_state,
        te_local=te_local,
        band_table=band_table,
    )
    amps = jnp.broadcast_to(amps.astype(BF16)[None], (span_n,) + amps.shape)
    amps = lax.all_to_all(
        amps.reshape((span_n * chord_n,) + amps.shape[2:]), ("span", "chord"), 0, 0, tiled=True
    )
    (flow_next,) = section(
        section_one,
        halos,
        fields,
        mixing,
        tables,
        (1, 2),
        flow=flow_state,
        onto=flow_next,
    )
    amps = jnp.sum(amps.reshape((span_n, chord_n) + amps.shape[1:]).astype(F32), axis=1)
    amps = amps.reshape(span_n * 4, LANES)
    gram_next = pl.pallas_call(
        functools.partial(amplitude_kernel, bands=group),
        grid=(2, bands // group),
        out_shape=jax.ShapeDtypeStruct(prior_gram_blocks.shape, F32),
        in_specs=[
            gram_block,
            pl.BlockSpec(amps.shape, lambda c, g: (0, 0)),
            pl.BlockSpec(memory_space=pltpu.SMEM),
            pl.BlockSpec((2, LANES, LANES), lambda c, g: (0, 0, 0)),
        ],
        out_specs=gram_block,
        scratch_shapes=[
            pltpu.VMEM((span_n * stations, LANES), BF16),
            pltpu.VMEM((2, stations, LANES), F32),
        ],
        name="gram_amplitudes",
    )(known, amps, span_pos.reshape(1), amplitude_tables())
    return (flow_next, gram_next)


def solution(mesh):
    return jax.shard_map(
        shards,
        mesh=mesh,
        in_specs=(
            P(None, "span", None, "chord"),
            P("span", None, "chord"),
            P("span", None, "chord"),
            P("span", None, "chord"),
            P(),
            P("span"),
            P(),
            P("span", "chord", None),
            P(),
            P(None, "chord", "span", None),
        ),
        out_specs=(P(None, "span", None, "chord"), P(None, "chord", "span", None)),
        check_vma=False,
    )
```

time: 321 us -> 164 us (0.51)
  the two profiles are of different devices: /device:TPU:51 before, /device:TPU:1 now
where the time goes in v1:
time: 164 us; the launch traced here: 162 us
  Pallas kernels  55.6 us (34%)
  starting transfers between devices  44.6 us (27%)
  local copies, waits for them, and re-layouts  36.6 us (22%)
  waiting for transfers between devices  14.9 us (9%)
  other arithmetic  9.03 us (6%)
    pallas_call x3, Pallas kernels, section(): pl.pallas_call(functools.partial(section_kernel, quantities=quantities, s...  40.5 us
    unnamed x54, local copies, waits for them, and re-layouts  20.1 us
    all_to_all x1, starting transfers between devices, shards(): lax.all_to_all(amps.reshape((span_n * chord_n,) + amps.shape[2:]), ('span...  19.7 us
    ppermute x2, waiting for transfers between devices, exchange(): lax.ppermute(left, 'chord', backward)  7.67 us
    all_to_all x1, waiting for transfers between devices, shards(): lax.all_to_all(amps.reshape((span_n * chord_n,) + amps.shape[2:]), ('span...  6.85 us
    pallas_call x1, Pallas kernels, shards(): pl.pallas_call(functools.partial(edges_kernel, pairs=per // 2), grid=(blo...  6.21 us
    ppermute x2, starting transfers between devices, exchange(): lax.ppermute(right, 'chord', forward)  5.78 us
    ppermute x2, starting transfers between devices, exchange(): lax.ppermute(high, 'span', up)  5.77 us
  transfers between devices with their start and end apart: 10, of which 4 were waited for; matrix products, arithmetic and copies ran while one was open for 14% of the time, Pallas kernels for 11%

profile of v1, /device:TPU:1, one launch (start us, length us, event | category | flops | bytes accessed | tf_op | source)
XLA Modules:
  0.0 161.8 jit_solution(9906496281314300431)
XLA Ops:
  0.6 2.3 %convert.7 = bf16[3,32,64,128]{3,2,1,0:T(8,128)(2,1)S(1)} convert(f32[3,32,64,128]{3,2,1,0:T(8,128)} %refs_12_.3) | non-fusion elementwise | flops 786432 | bytes 4718592 | tf_op jit(solution)/shard_map/convert.4
  3.0 0.7 fusion.8
  3.7 2.6 %collective-permute-start = (bf16[3,3,64,128]{3,2,1,0:T(8,128)(2,1)}, bf16[3,3,64,128]{3,2,1,0:T(8,128)(2,1)S(1)}, u32[]{:S(2)}, u32[]{:S(2)}) collective-permute-start(bf16[3,3,64,128]{3,2,1,0:T(8,128)(2,1)} %get-tuple-element.21), channel_id=1, source_target_pairs={{0,8},{8,16},{16,24},{24,32},{32,40},{40,48},{48,56},{56,64},{64,7... | collective-permute-start | bytes 442376 | tf_op jit(solution)/shard_map/ppermute | solution.py:435
  6.3 0.6 collective-permute-start.1
  7.0 6.2 %edges.1 = (f32[8,3,6,128]{3,2,1,0:T(8,128)}, f32[8,3,6,128]{3,2,1,0:T(8,128)}) custom-call(f32[3,32,64,128]{3,2,1,0:T(8,128)} %refs_12_.3, bf16[8,256]{1,0:T(8,128)(2,1)} %constant.28.clone.pick_ref.refs_11_), custom_call_target="tpu_custom_call" | custom-call | tf_op jit(solution)/shard_map/edges/pallas_call | solution.py:443
  13.2 0.9 copy.60
  14.1 0.7 copy.61
  14.8 3.2 %collective-permute-start.2 = (f32[3,48,128]{2,1,0:T(8,128)}, f32[3,48,128]{2,1,0:T(8,128)}, u32[]{:S(2)}, u32[]{:S(2)}) collective-permute-start(f32[3,48,128]{2,1,0:T(8,128)} %bitcast.2), channel_id=1, source_target_pairs={{0,1},{1,2},{2,3},{3,4},{4,5},{5,6},{6,7},{8,9},{9,10},{10,11},{11... | collective-permute-start | bytes 221192 | tf_op jit(solution)/shard_map/ppermute | solution.py:437
  17.9 0.9 copy.62
  18.9 0.7 copy.63
  19.5 1.3 collective-permute-start.3
  20.9 4.1 %collective-permute-done.3.refs_4_ = f32[3,48,128]{2,1,0:T(8,128)} collective-permute-done((f32[3,48,128]{2,1,0:T(8,128)}, f32[3,48,128]{2,1,0:T(8,128)}, u32[]{:S(2)}, u32[]{:S(2)}) %collective-permute-start.3) | collective-permute-done | bytes 73760 | tf_op jit(solution)/shard_map/ppermute | solution.py:438
  25.0 1.0 copy-done.5
  26.0 1.0 copy-done.8
  27.1 1.0 copy-done.11
  28.1 18.2 %section_one_012.1 = (f32[3,32,64,128]{3,2,1,0:T(8,128)S(1)}, bf16[3,3,64,128]{3,2,1,0:T(8,128)(2,1)}, bf16[3,3,64,128]{3,2,1,0:T(8,128)(2,1)}, f32[3,48,128]{2,1,0:T(8,128)S(1)}, f32[3,48,128]{2,1,0:T(8,128)S(1)}) custom-call(f32[3,32,64,128]{3,2,1,0:T(8,128)S(1)} %copy-done.1, bf16[3,3,64,128]{3,2,1,0:T(8,128)(2,1)S(1)} %collective-permute-done.refs_1_, ...), custom_call_target="tpu_custom_call" | custom-call | flops 60000000 | bytes 15000000 | tf_op jit(solution)/shard_map/section_one_012/pallas_call | solution.py:334
  46.3 1.6 %copy-done.2 = f32[3,32,64,128]{3,2,1,0:T(8,128)} copy-done((f32[3,32,64,128]{3,2,1,0:T(8,128)}, f32[3,32,64,128]{3,2,1,0:T(8,128)S(1)}, u32[]{:S(2)}) %copy-start.2) | copy-done | bytes 3145752
  47.9 0.6 copy-done.22
  48.6 0.6 copy-done.23
  49.2 3.2 %collective-permute-start.4 = (bf16[3,3,64,128]{3,2,1,0:T(8,128)(2,1)}, bf16[3,3,64,128]{3,2,1,0:T(8,128)(2,1)S(1)}, u32[]{:S(2)}, u32[]{:S(2)}) collective-permute-start(bf16[3,3,64,128]{3,2,1,0:T(8,128)(2,1)} %get-tuple-element.14), channel_id=1, source_target_pairs={{0,8},{8,16},{16,24},{24,32},{32,40},{40,48},{48,56},{56,64},{64,7... | collective-permute-start | bytes 442376 | tf_op jit(solution)/shard_map/ppermute | solution.py:435
  52.4 5.1 %collective-permute-start.5 = (bf16[3,3,64,128]{3,2,1,0:T(8,128)(2,1)}, bf16[3,3,64,128]{3,2,1,0:T(8,128)(2,1)}, u32[]{:S(2)}, u32[]{:S(2)}) collective-permute-start(bf16[3,3,64,128]{3,2,1,0:T(8,128)(2,1)} %get-tuple-element.15), channel_id=1, source_target_pairs={{8,0},{16,8},{24,16},{32,24},{40,32},{48,40},{56,48},{64,56},{72,6... | collective-permute-start | bytes 442376 | tf_op jit(solution)/shard_map/ppermute | solution.py:436
  57.5 1.5 copy.64
  59.0 1.5 copy.65
  60.5 0.9 copy.66.refs_14_
  61.4 2.6 %collective-permute-start.6 = (f32[3,48,128]{2,1,0:T(8,128)}, f32[3,48,128]{2,1,0:T(8,128)S(1)}, u32[]{:S(2)}, u32[]{:S(2)}) collective-permute-start(f32[3,48,128]{2,1,0:T(8,128)} %copy-done.23), channel_id=1, source_target_pairs={{0,1},{1,2},{2,3},{3,4},{4,5},{5,6},{6,7},{8,9},{9,10},{10,11},{11... | collective-permute-start | bytes 221192 | tf_op jit(solution)/shard_map/ppermute | solution.py:437
  64.0 1.3 collective-permute-start.7
  65.3 0.1 pad_add_fusion
  65.3 0.3 collective-permute-done.6.refs_3_
  65.7 3.6 %collective-permute-done.7.refs_4_ = f32[3,48,128]{2,1,0:T(8,128)S(1)} collective-permute-done((f32[3,48,128]{2,1,0:T(8,128)}, f32[3,48,128]{2,1,0:T(8,128)S(1)}, u32[]{:S(2)}, u32[]{:S(2)}) %collective-permute-start.7) | collective-permute-done | bytes 73760 | tf_op jit(solution)/shard_map/ppermute | solution.py:438
  69.3 1.9 %copy-done.3 = f32[3,32,64,128]{3,2,1,0:T(8,128)S(1)} copy-done((f32[3,32,64,128]{3,2,1,0:T(8,128)S(1)}, f32[3,32,64,128]{3,2,1,0:T(8,128)}, u32[]{:S(2)}) %copy-start.3) | copy-done | bytes 3145752
  71.2 1.0 copy-done.6
  72.2 1.0 copy-done.9
  73.3 1.0 copy-done.12
  74.3 11.2 %section_two_0.1 = (f32[3,32,64,128]{3,2,1,0:T(8,128)}, f32[8,4,128]{2,1,0:T(4,128)S(1)}) custom-call(f32[3,32,64,128]{3,2,1,0:T(8,128)S(1)} %copy-done.3, bf16[3,3,64,128]{3,2,1,0:T(8,128)(2,1)S(1)} %collective-permute-done.4.refs_1_, bf16[3,3,64,128]{3,2,1,0:T(8,128)(2,1)} %collective-permute-done.5.refs_2_, ...), custom_call_target="tpu_custom_call" | custom-call | flops 20000000 | bytes 5000000 | tf_op jit(solution)/shard_map/section_two_0/pallas_call | solution.py:334
  85.6 0.8 broadcast_in_dim.8
  86.3 19.7 %all-to-all-start.1 = ((bf16[256,4,128]{2,1,0:T(4,128)(2,1)}), bf16[256,4,128]{2,1,0:T(4,128)(2,1)}, u32[]{:S(2)}, u32[]{:S(2)}) async-start(bf16[256,4,128]{2,1,0:T(4,128)(2,1)} %bitcast.27), calls=%async_computation.1 | async-start | bytes 524288 | tf_op jit(solution)/shard_map/all_to_all | solution.py:527
  106.0 0.2 fusion
  106.2 0.8 copy.67
  107.0 1.8 %reshape.216 = f32[32,8,2,16]{3,2,1,0:T(2,128)} reshape(f32[256,32]{1,0:T(8,128)} %copy.67) | data formatting | bytes 65536 | tf_op jit(solution)/shard_map/convert_element_type | solution.py:481
  108.8 1.6 reshape.215
  110.4 0.7 copy.71
  111.1 1.0 broadcast_in_dim.6
  112.0 1.8 %broadcast_multiply_fusion = f32[32,8,2,16]{3,2,1,0:T(2,128)} fusion(f32[32,8,2,16]{3,2,1,0:T(2,128)} %reshape.216, f32[16]{0:T(128)S(1)} %convert_multiply_fusion), kind=kLoop, calls=%fused_computation.6 | loop fusion | flops 8192 | bytes 65600 | tf_op jit(solution)/shard_map/mul | solution.py:481
  113.8 6.8 %all-to-all-done.1 = bf16[256,4,128]{2,1,0:T(4,128)(2,1)} async-done(((bf16[256,4,128]{2,1,0:T(4,128)(2,1)}), bf16[256,4,128]{2,1,0:T(4,128)(2,1)}, u32[]{:S(2)}, u32[]{:S(2)}) %all-to-all-start.1) | async-done | bytes 262176 | tf_op jit(solution)/shard_map/all_to_all | solution.py:527
  120.7 0.9 broadcast_in_dim.7
  121.5 5.0 %all-to-all-start = ((bf16[32,32,256]{2,1,0:T(8,128)(2,1)}), bf16[32,32,256]{2,1,0:T(8,128)(2,1)}, u32[]{:S(2)}, u32[]{:S(2)}) async-start(bf16[32,32,256]{2,1,0:T(8,128)(2,1)} %broadcast_in_dim.7), calls=%async_computation | async-start | bytes 1048576 | tf_op jit(solution)/shard_map/all_to_all | solution.py:477
  126.6 1.3 fusion.9
  127.9 1.0 pad_maximum_fusion
  128.9 1.7 %copy.69 = f32[32,8,2,16]{0,3,2,1:T(8,128)} copy(f32[32,8,2,16]{3,2,1,0:T(2,128)} %pad_maximum_fusion) | data formatting | bytes 65536 | tf_op jit(solution)/shard_map/stack | solution.py:482
  130.6 1.0 copy.70
  131.6 0.1 mul.38
  131.7 0.8 multiply_bitcast_fusion
  132.5 0.7 pad_maximum_fusion.1.left_ref
  133.2 1.9 %copy-done.4 = f32[3,32,64,128]{3,2,1,0:T(8,128)S(1)} copy-done((f32[3,32,64,128]{3,2,1,0:T(8,128)S(1)}, f32[3,32,64,128]{3,2,1,0:T(8,128)}, u32[]{:S(2)}) %copy-start.4) | copy-done | bytes 3145752
  135.1 1.0 copy-done.7
  136.1 1.0 copy-done.10
  137.1 1.0 copy-done.13
  138.2 0.9 copy-done.16
  139.1 0.9 copy-done.18
  139.9 11.1 %section_two_12.1 = f32[3,32,64,128]{3,2,1,0:T(8,128)} custom-call(f32[3,32,64,128]{3,2,1,0:T(8,128)S(1)} %copy-done.4, bf16[3,3,64,128]{3,2,1,0:T(8,128)(2,1)S(1)} %collective-permute-done.4.refs_1_, bf16[3,3,64,128]{3,2,1,0:T(8,128)(2,1)} %collective-permute-done.5.refs_2_, f32[3,48,128]{2,1,0:T(8,128)S(1)} %copy-done.16, ...), custom_call_target="tpu_custom_call", output_to_operand_aliasing={{}: (13, {})} | custom-call | flops 40000000 | bytes 10000000 | tf_op jit(solution)/shard_map/section_two_12/pallas_call | solution.py:334
  151.1 1.1 convert_reduce_fusion
  152.2 0.7 copy.74
  152.9 4.6 %gram_stored.1.known_ref = f32[2,8,32,1024]{3,2,1,0:T(8,128)} custom-call(f32[2,8,32,1024]{3,2,1,0:T(8,128)} %prior_ref.1, f32[2,2,32,256]{3,2,1,0:T(8,128)} %pad_maximum_fusion.1.left_ref, bf16[1024,256]{1,0:T(8,128)(2,1)} %bitcast.13.all_ref), custom_call_target="tpu_custom_call" | custom-call | flops 20000000 | bytes 5000000 | tf_op jit(solution)/shard_map/gram_stored/pallas_call | solution.py:496
  157.5 4.3 %gram_amplitudes.1 = f32[2,8,32,1024]{3,2,1,0:T(8,128)} custom-call(f32[2,8,32,1024]{3,2,1,0:T(8,128)} %gram_stored.1.known_ref, f32[128,128]{1,0:T(8,128)} %bitcast.31, s32[1]{0:T(128)} %bitcast.17.where_ref, bf16[2,128,128]{2,1,0:T(8,128)(2,1)} %constant.31.clone.rep_ref), custom_call_target="tpu_custom_call" | custom-call | tf_op jit(solution)/shard_map/gram_amplitudes/pallas_call | solution.py:542
  (49 shorter events, 0.2 us)
Async XLA Ops:
  0.6 105.4 %copy-start = (bf16[32,8,128]{2,1,0:T(8,128)(2,1)S(1)}, bf16[32,8,128]{2,1,0:T(8,128)(2,1)}, u32[]{:S(2)}) copy-start(bf16[32,8,128]{2,1,0:T(8,128)(2,1)} %param.21) | copy-start | bytes 196612
  2.9 17.9 %copy-start.25 = (s32[16]{0:T(128)S(1)}, s32[16]{0:T(128)}, u32[]{:S(2)}) copy-start(s32[16]{0:T(128)} %param.22) | copy-start | bytes 196
  2.9 22.0 %copy-start.1 = (f32[3,32,64,128]{3,2,1,0:T(8,128)S(1)}, f32[3,32,64,128]{3,2,1,0:T(8,128)}, u32[]{:S(2)}) copy-start(f32[3,32,64,128]{3,2,1,0:T(8,128)} %refs_12_.3) | copy-start | bytes 9437188
  2.9 22.0 %copy-start.14 = (bf16[256,256]{1,0:T(8,128)(2,1)S(1)}, bf16[256,256]{1,0:T(8,128)(2,1)}, u32[]{:S(2)}) copy-start(bf16[256,256]{1,0:T(8,128)(2,1)} %constant.29.clone.refs_9_) | copy-start | bytes 393220
  3.0 22.0 %copy-start.19 = (bf16[8,256]{1,0:T(8,128)(2,1)S(1)}, bf16[8,256]{1,0:T(8,128)(2,1)}, u32[]{:S(2)}) copy-start(bf16[8,256]{1,0:T(8,128)(2,1)} %constant.28.clone.pick_ref.refs_11_) | copy-start | bytes 12292
  3.0 22.0 %copy-start.20 = (bf16[8,256]{1,0:T(8,128)(2,1)S(1)}, bf16[8,256]{1,0:T(8,128)(2,1)}, u32[]{:S(2)}) copy-start(bf16[8,256]{1,0:T(8,128)(2,1)} %constant.30.clone.refs_10_) | copy-start | bytes 12292
  3.0 22.0 %copy-start.21 = (f32[3,3]{1,0:T(4,128)S(1)}, f32[3,3]{1,0:T(4,128)}, u32[]{:S(2)}) copy-start(f32[3,3]{1,0:T(4,128)} %refs_8_.5) | copy-start | bytes 112
  3.7 21.2 %collective-permute-start = (bf16[3,3,64,128]{3,2,1,0:T(8,128)(2,1)}, bf16[3,3,64,128]{3,2,1,0:T(8,128)(2,1)S(1)}, u32[]{:S(2)}, u32[]{:S(2)}) collective-permute-start(bf16[3,3,64,128]{3,2,1,0:T(8,128)(2,1)} %get-tuple-element.21), channel_id=1, source_target_pairs={{0,8},{8,16},{16,24},{24,32},{32,40},{40,48},{48,56},{56,64},{64,7... | collective-permute-start | bytes 442376 | tf_op jit(solution)/shard_map/ppermute | solution.py:435
  6.3 18.6 %collective-permute-start.1 = (bf16[3,3,64,128]{3,2,1,0:T(8,128)(2,1)}, bf16[3,3,64,128]{3,2,1,0:T(8,128)(2,1)}, u32[]{:S(2)}, u32[]{:S(2)}) collective-permute-start(bf16[3,3,64,128]{3,2,1,0:T(8,128)(2,1)} %get-tuple-element.20), channel_id=1, source_target_pairs={{8,0},{16,8},{24,16},{32,24},{40,32},{48,40},{56,48},{64,56},{72,6... | collective-permute-start | bytes 442376 | tf_op jit(solution)/shard_map/ppermute | solution.py:436
  14.8 6.1 %collective-permute-start.2 = (f32[3,48,128]{2,1,0:T(8,128)}, f32[3,48,128]{2,1,0:T(8,128)}, u32[]{:S(2)}, u32[]{:S(2)}) collective-permute-start(f32[3,48,128]{2,1,0:T(8,128)} %bitcast.2), channel_id=1, source_target_pairs={{0,1},{1,2},{2,3},{3,4},{4,5},{5,6},{6,7},{8,9},{9,10},{10,11},{11... | collective-permute-start | bytes 221192 | tf_op jit(solution)/shard_map/ppermute | solution.py:437
  19.5 5.4 %collective-permute-start.3 = (f32[3,48,128]{2,1,0:T(8,128)}, f32[3,48,128]{2,1,0:T(8,128)}, u32[]{:S(2)}, u32[]{:S(2)}) collective-permute-start(f32[3,48,128]{2,1,0:T(8,128)} %bitcast.5), channel_id=1, source_target_pairs={{1,0},{2,1},{3,2},{4,3},{5,4},{6,5},{7,6},{9,8},{10,9},{11,10},{12... | collective-permute-start | bytes 221192 | tf_op jit(solution)/shard_map/ppermute | solution.py:438
  20.8 36.6 %copy-start.24 = (s32[32]{0:T(128)S(1)}, s32[32]{0:T(128)}, u32[]{:S(2)}) copy-start(s32[32]{0:T(128)} %param.19) | copy-start | bytes 388
  25.0 1.0 copy-start.5
  26.0 1.0 copy-start.8
  27.1 1.0 copy-start.11
  46.3 1.6 %copy-start.2 = (f32[3,32,64,128]{3,2,1,0:T(8,128)}, f32[3,32,64,128]{3,2,1,0:T(8,128)S(1)}, u32[]{:S(2)}) copy-start(f32[3,32,64,128]{3,2,1,0:T(8,128)S(1)} %get-tuple-element.13.refs_0_) | copy-start | bytes 9437188
  47.9 0.6 copy-start.22
  48.6 0.6 copy-start.23
  49.2 20.1 %collective-permute-start.4 = (bf16[3,3,64,128]{3,2,1,0:T(8,128)(2,1)}, bf16[3,3,64,128]{3,2,1,0:T(8,128)(2,1)S(1)}, u32[]{:S(2)}, u32[]{:S(2)}) collective-permute-start(bf16[3,3,64,128]{3,2,1,0:T(8,128)(2,1)} %get-tuple-element.14), channel_id=1, source_target_pairs={{0,8},{8,16},{16,24},{24,32},{32,40},{40,48},{48,56},{56,64},{64,7... | collective-permute-start | bytes 442376 | tf_op jit(solution)/shard_map/ppermute | solution.py:435
  52.4 16.9 %collective-permute-start.5 = (bf16[3,3,64,128]{3,2,1,0:T(8,128)(2,1)}, bf16[3,3,64,128]{3,2,1,0:T(8,128)(2,1)}, u32[]{:S(2)}, u32[]{:S(2)}) collective-permute-start(bf16[3,3,64,128]{3,2,1,0:T(8,128)(2,1)} %get-tuple-element.15), channel_id=1, source_target_pairs={{8,0},{16,8},{24,16},{32,24},{40,32},{48,40},{56,48},{64,56},{72,6... | collective-permute-start | bytes 442376 | tf_op jit(solution)/shard_map/ppermute | solution.py:436
  61.4 4.3 %collective-permute-start.6 = (f32[3,48,128]{2,1,0:T(8,128)}, f32[3,48,128]{2,1,0:T(8,128)S(1)}, u32[]{:S(2)}, u32[]{:S(2)}) collective-permute-start(f32[3,48,128]{2,1,0:T(8,128)} %copy-done.23), channel_id=1, source_target_pairs={{0,1},{1,2},{2,3},{3,4},{4,5},{5,6},{6,7},{8,9},{9,10},{10,11},{11... | collective-permute-start | bytes 221192 | tf_op jit(solution)/shard_map/ppermute | solution.py:437
  64.0 5.3 %collective-permute-start.7 = (f32[3,48,128]{2,1,0:T(8,128)}, f32[3,48,128]{2,1,0:T(8,128)S(1)}, u32[]{:S(2)}, u32[]{:S(2)}) collective-permute-start(f32[3,48,128]{2,1,0:T(8,128)} %copy-done.22), channel_id=1, source_target_pairs={{1,0},{2,1},{3,2},{4,3},{5,4},{6,5},{7,6},{9,8},{10,9},{11,10},{12... | collective-permute-start | bytes 221192 | tf_op jit(solution)/shard_map/ppermute | solution.py:438
  65.7 19.9 %copy-start.15 = (f32[3,48,128]{2,1,0:T(8,128)}, f32[3,48,128]{2,1,0:T(8,128)S(1)}, u32[]{:S(2)}) copy-start(f32[3,48,128]{2,1,0:T(8,128)S(1)} %collective-permute-done.6.refs_3_) | copy-start | bytes 221188
  69.3 16.3 %copy-start.17 = (f32[3,48,128]{2,1,0:T(8,128)}, f32[3,48,128]{2,1,0:T(8,128)S(1)}, u32[]{:S(2)}) copy-start(f32[3,48,128]{2,1,0:T(8,128)S(1)} %collective-permute-done.7.refs_4_) | copy-start | bytes 221188
  69.3 1.9 %copy-start.3 = (f32[3,32,64,128]{3,2,1,0:T(8,128)S(1)}, f32[3,32,64,128]{3,2,1,0:T(8,128)}, u32[]{:S(2)}) copy-start(f32[3,32,64,128]{3,2,1,0:T(8,128)} %copy-done.2) | copy-start | bytes 9437188
  71.2 1.0 copy-start.6
  72.2 1.0 copy-start.9
  73.3 1.0 copy-start.12
  86.3 34.3 %all-to-all-start.1 = ((bf16[256,4,128]{2,1,0:T(4,128)(2,1)}), bf16[256,4,128]{2,1,0:T(4,128)(2,1)}, u32[]{:S(2)}, u32[]{:S(2)}) async-start(bf16[256,4,128]{2,1,0:T(4,128)(2,1)} %bitcast.27), calls=%async_computation.1 | async-start | bytes 524288 | tf_op jit(solution)/shard_map/all_to_all | solution.py:527
  121.5 31.4 %all-to-all-start = ((bf16[32,32,256]{2,1,0:T(8,128)(2,1)}), bf16[32,32,256]{2,1,0:T(8,128)(2,1)}, u32[]{:S(2)}, u32[]{:S(2)}) async-start(bf16[32,32,256]{2,1,0:T(8,128)(2,1)} %broadcast_in_dim.7), calls=%async_computation | async-start | bytes 1048576 | tf_op jit(solution)/shard_map/all_to_all | solution.py:477
  133.2 1.9 %copy-start.4 = (f32[3,32,64,128]{3,2,1,0:T(8,128)S(1)}, f32[3,32,64,128]{3,2,1,0:T(8,128)}, u32[]{:S(2)}) copy-start(f32[3,32,64,128]{3,2,1,0:T(8,128)} %copy-done.2) | copy-start | bytes 9437188
  135.1 1.0 copy-start.7
  136.1 1.0 copy-start.10
  137.1 1.0 copy-start.13
  138.2 0.9 copy-start.16
  139.1 0.9 copy-start.18

commit v2 on v0

v2 whole, which is shorter than its diff:
```python
import functools

import jax
import jax.numpy as jnp
import ml_dtypes
import numpy as np
from jax import lax
from jax.experimental import pallas as pl
from jax.experimental.pallas import tpu as pltpu
from jax.sharding import PartitionSpec as P

FIRST = (45, -9, 1)
SECOND = (270, -27, 2)
CENTRE = -490
TIME_STEP = 0.6
DECAY = 0.9
F32 = jnp.float32
BF16 = jnp.bfloat16
LANES = 128


def chord_matrices():
    inner = np.zeros((LANES, 2 * LANES), np.float32)
    outer = np.zeros((LANES, 2 * LANES), np.float32)

    def row(cell):
        if cell < 0:
            return outer, cell + 3
        if cell >= LANES:
            return outer, cell - LANES + 3
        return inner, cell

    for cell in range(LANES):
        inner[cell, LANES + cell] += CENTRE
        for reach in (1, 2, 3):
            for sign in (1, -1):
                table, index = row(cell + sign * reach)
                table[index, cell] += sign * FIRST[reach - 1]
                table[index, LANES + cell] += SECOND[reach - 1]
    return np.concatenate([inner, inner, outer]).astype(ml_dtypes.bfloat16)


def nt_dot(a, b):
    return lax.dot_general(a, b, (((1,), (1,)), ((), ())), preferred_element_type=F32)


def fine_dot(a, b):
    def pieces(x):
        one = x.astype(BF16)
        x = x - one.astype(F32)
        two = x.astype(BF16)
        return one, two, (x - two.astype(F32)).astype(BF16)

    left, right = pieces(a), pieces(b)
    total = None
    for i, j in ((2, 0), (0, 2), (1, 1), (1, 0), (0, 1), (0, 0)):
        part = jnp.dot(left[i], right[j], preferred_element_type=F32)
        total = part if total is None else total + part
    return total


def edge_lanes(shape):
    return lax.div(lax.broadcasted_iota(jnp.int32, shape, len(shape) - 1), 8)


def edges_kernel(flow_ref, cells_ref, low_ref, high_ref):
    stations, normal = flow_ref.shape[1:3]
    lane = edge_lanes((16, LANES))
    for half in range(stations // 16):
        for tile in range(normal // 16):
            rows = slice(16 * tile, 16 * tile + 16)
            packed = jnp.zeros((16, LANES), F32)
            for s in range(16):
                moved = pltpu.roll(flow_ref[0, 16 * half + s, rows, :], (3 + 8 * s) % LANES, 1)
                packed = jnp.where(lane == s, moved, packed)
            cells_ref[0, half, rows, :] = packed.astype(BF16)
    low_ref[0] = flow_ref[0, 0:3].astype(BF16)
    high_ref[0] = flow_ref[0, stations - 3 : stations].astype(BF16)


def section_kernel(*refs, second):
    take = list(refs).pop
    refs = list(refs)
    take = refs.pop
    state_hbm = take(0)
    span_low, span_high, chord_low, chord_high = (take(0) for _ in range(4))
    vs_hbm, vc_hbm, nu_hbm = (take(0) for _ in range(3))
    mix, table_ref = take(0), take(0)
    if second:
        flow_hbm, te_ref, band_ref = (take(0) for _ in range(3))
    out_hbm = take(0)
    if second:
        amp_out = take(0)
    else:
        low_out, high_out, cells_out = (take(0) for _ in range(3))
    wide, result, chord, halos, cells, vs, vc, nu, in_sem, out_sem = (take(0) for _ in range(10))
    if second:
        before, before_sem, columns, amps = (take(0) for _ in range(4))

    count, stations, normal = wide.shape[0], vs.shape[0], vs.shape[1]
    chunks, pairs = 4, stations // 2
    per = stations // chunks

    def copies(c):
        rows = pl.ds(per * c, per)
        todo = [
            pltpu.make_async_copy(
                state_hbm.at[:, rows],
                wide.at[:, pl.ds(3 + per * c, per), pl.ds(8, normal), :],
                in_sem.at[0, c],
            ),
            pltpu.make_async_copy(vs_hbm.at[rows], vs.at[rows], in_sem.at[1, c]),
            pltpu.make_async_copy(vc_hbm.at[rows], vc.at[rows], in_sem.at[2, c]),
            pltpu.make_async_copy(nu_hbm.at[rows], nu.at[rows], in_sem.at[3, c]),
        ]
        if second:
            todo.append(
                pltpu.make_async_copy(flow_hbm.at[:, rows], before.at[:, rows], before_sem.at[c])
            )
        return todo

    for c in range(chunks):
        for copy in copies(c):
            copy.start()

    nothing = jnp.zeros((count, stations, 8, LANES), F32)
    wide[:, 3 : 3 + stations, 0:8, :] = nothing
    wide[:, 3 : 3 + stations, 8 + normal : 16 + normal, :] = nothing
    wide[:, 0:3, 8 : 8 + normal, :] = span_low[...].astype(F32)
    wide[:, 3 + stations : 6 + stations, 8 : 8 + normal, :] = span_high[...].astype(F32)
    place = lax.rem(lax.broadcasted_iota(jnp.int32, (normal, LANES), 1), 8)
    for q in range(count):
        for half in range(stations // 16):
            near = jnp.where(
                place < 3, chord_low[q, half].astype(F32), chord_high[q, half].astype(F32)
            )
            halos[q, half] = jnp.where(place < 6, near, 0.0)
    if second:
        columns[...] = jnp.zeros(columns.shape, F32)

    def matmuls(p):
        slot, half = lax.rem(p, 2), lax.div(p, 8)
        parts = []
        for q in range(count):
            for d in range(2):
                slab = wide[q, 3 + 2 * p + d, 8 : 8 + normal, :]
                high = slab.astype(BF16)
                low = (slab - high.astype(F32)).astype(BF16)
                shift = lax.rem(LANES - 8 * lax.rem(2 * p + d, 16), LANES)
                beyond = pltpu.roll(halos[q, half], shift, 1).astype(BF16)
                parts.append(jnp.concatenate([high, low, beyond], axis=1))
        chord[slot] = jnp.dot(
            jnp.concatenate(parts), table_ref[...], preferred_element_type=F32
        )

    scale = 0.5 if second else 1.0
    couple = [
        [scale * ((1.0 if q == e else 0.0) + TIME_STEP * mix[q, e]) for e in range(count)]
        for q in range(count)
    ]
    ROWS = 16
    lane = lax.broadcasted_iota(jnp.int32, (ROWS, LANES), 1)

    def body(p, carry):
        matmuls(jnp.minimum(p + 1, pairs - 1))
        slot = lax.rem(p, 2)
        for half in range(2):
            s = 2 * p + half
            for tile in range(normal // ROWS):
                rows = slice(ROWS * tile, ROWS * tile + ROWS)
                a = vs[s, rows, :].astype(F32) * (-scale * TIME_STEP / 60)
                b = vc[s, rows, :].astype(F32) * (-scale * TIME_STEP / 60)
                g = nu[s, rows, :].astype(F32) * (scale * TIME_STEP / 180)
                centre = [
                    wide[e, 3 + s, 8 + ROWS * tile : 8 + ROWS * tile + ROWS, :]
                    for e in range(count)
                ]
                for q in range(count):

                    def at(ds, dn):
                        low = 8 + ROWS * tile + dn
                        return wide[q, 3 + s + ds, low : low + ROWS, :]

                    first = None
                    both = None
                    for reach in (1, 2, 3):
                        up, down = at(reach, 0), at(-reach, 0)
                        diff = up - down
                        total = (up + down) + (at(0, reach) + at(0, -reach))
                        if FIRST[reach - 1] != 1:
                            diff = diff * float(FIRST[reach - 1])
                        total = total * float(SECOND[reach - 1])
                        first = diff if first is None else first + diff
                        both = total if both is None else both + total
                    start = (2 * q + half) * normal + ROWS * tile
                    crow = slice(start, start + ROWS)
                    chord_first = chord[slot, crow, 0:LANES]
                    chord_second = chord[slot, crow, LANES : 2 * LANES]
                    both = both + (centre[q] * float(2 * CENTRE) + chord_second)
                    value = a * first + b * chord_first + g * both
                    for e in range(count):
                        value = value + couple[q][e] * centre[e]
                    if second:
                        value = value + 0.5 * before[q, s, rows, :]
                    result[q, s, rows, :] = value
                    if second and q == 0:
                        hit = jnp.where(lane == te_ref[s], value, 0.0)
                        column = jnp.sum(hit, axis=1, keepdims=True)
                        columns[rows, :] += jnp.where(lane == s, column, 0.0)
                    if not second:
                        station = lax.rem(s, 16)
                        moved = pltpu.roll(value, lax.rem(3 + 8 * station, LANES), 1)
                        kept = cells[q, lax.div(p, 8), rows, :]
                        cells[q, lax.div(p, 8), rows, :] = jnp.where(
                            lax.div(lane, 8) == station, moved, kept
                        )
        out_copy(p).start()
        return carry

    def out_copy(p):
        two = pl.ds(2 * p, 2)
        return pltpu.make_async_copy(result.at[:, two], out_hbm.at[:, two], out_sem.at[p])

    def arrive(c):
        for copy in copies(c):
            copy.wait()

    arrive(0)
    matmuls(0)
    for c in range(chunks):
        if c + 1 < chunks:
            arrive(c + 1)
        lax.fori_loop(c * pairs // chunks, (c + 1) * pairs // chunks, body, 0)

    if second:
        amp = fine_dot(columns[...].T, band_ref[...])
        amps[...] = amp[:stations].astype(BF16).astype(F32)
        lane4 = lax.div(lax.broadcasted_iota(jnp.int32, (4, LANES), 1), 16)
        pieces = [jnp.zeros((4, LANES), F32) for _ in range(8)]
        for u in range(8):
            some = amps[pl.ds(u, 4, stride=8), :]
            for j in range(8):
                shift = (16 * (u - j)) % LANES
                moved = pltpu.roll(some, shift, 1) if shift else some
                pieces[j] = jnp.where(lane4 == u, moved, pieces[j])
        for j in range(8):
            amp_out[j] = pieces[j]
    else:
        cells_out[...] = cells[...].astype(BF16)
        low_out[...] = result[:, 0:3].astype(BF16)
        high_out[...] = result[:, stations - 3 : stations].astype(BF16)

    def drain(p, carry):
        out_copy(p).wait()
        return carry

    lax.fori_loop(0, pairs, drain, 0)


def section(state, halos, fields, mixing, table, flow=None, te_local=None, band_table=None):
    count, stations, normal, _ = state.shape
    second = flow is not None
    pairs = stations // 2
    hbm = pl.BlockSpec(memory_space=pltpu.HBM)
    vmem = pl.BlockSpec(memory_space=pltpu.VMEM)
    smem = pl.BlockSpec(memory_space=pltpu.SMEM)
    args = [state, *halos, *fields, mixing, table]
    specs = [hbm] + [vmem] * 4 + [hbm] * 3 + [smem, vmem]
    shapes = [jax.ShapeDtypeStruct(state.shape, F32)]
    if second:
        args += [flow, te_local, band_table]
        specs += [hbm, smem, vmem]
        shapes.append(jax.ShapeDtypeStruct((8, 4, LANES), F32))
    else:
        shapes += [jax.ShapeDtypeStruct((count, 3, normal, LANES), BF16)] * 2
        shapes.append(jax.ShapeDtypeStruct((count, stations // 16, normal, LANES), BF16))
    field = pltpu.VMEM((stations, normal, LANES), BF16)
    args = [
        pltpu.with_memory_space_constraint(x, pltpu.HBM) if spec is hbm else x
        for x, spec in zip(args, specs)
    ]
    scratch = [
        pltpu.VMEM((count, stations + 6, normal + 16, LANES), F32),
        pltpu.VMEM((count, stations, normal, LANES), F32),
        pltpu.VMEM((2, count * 2 * normal, 2 * LANES), F32),
        pltpu.VMEM((count, stations // 16, normal, LANES), F32),
        pltpu.VMEM((count, stations // 16, normal, LANES), F32),
        field,
        field,
        field,
        pltpu.SemaphoreType.DMA((4, 4)),
        pltpu.SemaphoreType.DMA((pairs,)),
    ]
    if second:
        scratch += [
            pltpu.VMEM((count, stations, normal, LANES), F32),
            pltpu.SemaphoreType.DMA((4,)),
            pltpu.VMEM((normal, LANES), F32),
            pltpu.VMEM((stations, LANES), F32),
        ]
    return pl.pallas_call(
        functools.partial(section_kernel, second=second),
        out_shape=tuple(shapes),
        in_specs=specs,
        out_specs=tuple([hbm] + [vmem] * (len(shapes) - 1)),
        scratch_shapes=scratch,
        compiler_params=pltpu.CompilerParams(vmem_limit_bytes=40 << 20),
        cost_estimate=pl.CostEstimate(
            flops=60000000, transcendentals=0, bytes_accessed=12000000
        ),
        name="section_two" if second else "section_one",
    )(*args)


def spectra_kernel(spectra_ref, wanted_ref, own_ref, send_ref):
    stations, bands, slots = spectra_ref.shape
    width = wanted_ref.shape[1]
    rows = spectra_ref[...].astype(F32).reshape(stations * bands, slots).astype(BF16)
    slot = lax.broadcasted_iota(jnp.int32, (slots, width), 0)
    choose = jnp.where(slot == wanted_ref[...], 1.0, 0.0).astype(BF16)
    got = jnp.dot(rows, choose, preferred_element_type=F32)
    row_band = lax.rem(lax.broadcasted_iota(jnp.int32, got.shape, 0), bands)
    lane_band = lax.div(lax.broadcasted_iota(jnp.int32, got.shape, 1), width // bands)
    got = jnp.where(row_band == lane_band, got, 0.0).reshape(stations, bands, width)
    packed = jnp.sum(got, axis=1).astype(BF16)
    own_ref[...] = packed
    for d in range(send_ref.shape[0]):
        send_ref[d] = packed


def gram_kernel(prior_ref, every_ref, own_ref, ramp_ref, amp_ref, where_ref, rep_ref, out_ref, left):
    step = pl.program_id(0)
    bands, stations, tile = prior_ref.shape[1:]
    width = own_ref.shape[1]
    sources = amp_ref.shape[0] // (tile // stations) // pl.num_programs(0)

    def spread(source):
        whole = amp_ref[pl.ds(source * sources, sources)].astype(F32)
        total = whole[0]
        for j in range(1, sources):
            total = total + whole[j]
        lane = lax.div(lax.broadcasted_iota(jnp.int32, (8, LANES), 1), 16)
        here = lane == lax.broadcasted_iota(jnp.int32, (8, LANES), 0)
        rows = [
            jnp.where(here, jnp.broadcast_to(total[t : t + 1, :], (8, LANES)), 0.0)
            for t in range(4)
        ]
        return jnp.concatenate(rows).astype(BF16)

    @pl.when(step == 0)
    def _():
        own = own_ref[...].astype(F32)
        ramp = ramp_ref[...]
        lane = lax.broadcasted_iota(jnp.int32, own.shape, 1)
        real = lax.rem(lane, 32) < 16
        turned = jnp.where(
            real, pltpu.roll(own, width - 16, 1), -pltpu.roll(own, 16, 1)
        )
        mine = spread(where_ref[0])
        place = lax.broadcasted_iota(jnp.int32, (stations, LANES), 1)
        for c, part in enumerate((own, turned)):
            part = part * ramp
            high = part.astype(BF16).astype(F32)
            low = part - high
            amp = jnp.dot(mine, rep_ref[c], preferred_element_type=F32)
            for b in range(bands):
                at = (c * bands + b) * stations
                keep = lax.div(lane, 32) == b
                rows = slice(at, at + stations)
                left[rows, 0:width] = jnp.where(keep, high, 0.0).astype(BF16)
                left[rows, width : 2 * width] = jnp.where(keep, low, 0.0).astype(BF16)
                left[rows, 2 * width : 2 * width + LANES] = jnp.where(
                    lax.rem(place, 8) == b, amp, 0.0
                ).astype(BF16)

    blocks = tile // stations
    right = jnp.concatenate([spread(step * blocks + i) for i in range(blocks)])
    stored = every_ref[...]
    got = nt_dot(left[...], jnp.concatenate([stored, stored, right], axis=1))
    out_ref[...] = DECAY * prior_ref[...] + got.reshape(2, bands, stations, tile)


def amplitude_tables():
    index = np.arange(LANES)
    same = (index[:, None] % 16 == index[None, :] % 16).astype(np.float32)
    other = (index[:, None] % 8 == index[None, :] % 8) & (
        (index[:, None] % 16) // 8 != (index[None, :] % 16) // 8
    )
    sign = np.where((index % 16) // 8 == 0, 1.0, -1.0)
    return np.stack([same, other * sign[None, :]]).astype(ml_dtypes.bfloat16)


def shards(
    flow_state,
    vel_span,
    vel_chord,
    viscosity,
    mixing,
    te_index,
    band_response,
    spectra,
    offsets,
    prior_gram_blocks,
):
    count, stations, normal, cells = flow_state.shape
    bands, slots = spectra.shape[1], spectra.shape[2] // 2
    segs = offsets.shape[0]
    span_n, chord_n = lax.axis_size("span"), lax.axis_size("chord")
    span_pos, chord_pos = lax.axis_index("span"), lax.axis_index("chord")
    table = chord_matrices()
    fields = (vel_span, vel_chord, viscosity)

    def exchange(low, high, edge):
        up = [(i, (i + 1) % span_n) for i in range(span_n)]
        down = [(b, a) for a, b in up]
        forward = [(i, i + 1) for i in range(chord_n - 1)]
        backward = [(b, a) for a, b in forward]
        return (
            lax.ppermute(high, "span", up),
            lax.ppermute(low, "span", down),
            lax.ppermute(edge, "chord", forward),
            lax.ppermute(edge, "chord", backward),
        )

    edge_shape = jax.ShapeDtypeStruct((count, stations // 16, normal, LANES), BF16)
    ends_shape = jax.ShapeDtypeStruct((count, 3, normal, LANES), BF16)

    def per_quantity(shape):
        return pl.BlockSpec((1,) + shape.shape[1:], lambda q: (q, 0, 0, 0))

    edge, low, high = pl.pallas_call(
        edges_kernel,
        grid=(count,),
        out_shape=(edge_shape, ends_shape, ends_shape),
        in_specs=[per_quantity(flow_state)],
        out_specs=(per_quantity(edge_shape), per_quantity(ends_shape), per_quantity(ends_shape)),
        name="edges",
    )(flow_state)
    halos = exchange(low, high, edge)

    width = bands * 2 * segs
    wanted = jnp.tile(jnp.concatenate([offsets, offsets + slots]), bands)[None]
    packed, send = pl.pallas_call(
        spectra_kernel,
        out_shape=(
            jax.ShapeDtypeStruct((stations, width), BF16),
            jax.ShapeDtypeStruct((span_n, stations, width), BF16),
        ),
        name="spectra",
    )(spectra, wanted)
    every = lax.all_to_all(send, "span", 0, 0, tiled=True).reshape(span_n * stations, width)

    (section_one, low, high, edge) = section(flow_state, halos, fields, mixing, table)
    halos = exchange(low, high, edge)

    te_local = te_index - chord_pos * cells
    band_table = band_response.reshape(normal, 2, chord_n, bands).transpose(0, 2, 1, 3)
    band_table = band_table.reshape(normal, chord_n * 2 * bands)
    flow_next, amps = section(
        section_one,
        halos,
        fields,
        mixing,
        table,
        flow=flow_state,
        te_local=te_local,
        band_table=band_table,
    )
    amps = jnp.broadcast_to(amps.astype(BF16)[None], (span_n,) + amps.shape)
    amps = lax.all_to_all(
        amps.reshape((span_n * chord_n,) + amps.shape[2:]), ("span", "chord"), 0, 0, tiled=True
    )

    ramp = np.tile((np.arange(segs, dtype=np.float32) + 1) / segs, 2 * bands)[None]
    tiles = 4
    tile = span_n * stations // tiles
    gram_block = pl.BlockSpec((2, bands, stations, tile), lambda t: (0, 0, 0, t))

    def whole(x):
        return pl.BlockSpec(x.shape, lambda t: (0,) * x.ndim)

    reps = amplitude_tables()
    gram_next = pl.pallas_call(
        gram_kernel,
        grid=(tiles,),
        out_shape=jax.ShapeDtypeStruct(prior_gram_blocks.shape, F32),
        in_specs=[
            gram_block,
            pl.BlockSpec((tile, width), lambda t: (t, 0)),
            whole(packed),
            whole(ramp),
            whole(amps),
            pl.BlockSpec(memory_space=pltpu.SMEM),
            whole(reps),
        ],
        out_specs=gram_block,
        scratch_shapes=[pltpu.VMEM((2 * bands * stations, 2 * width + LANES), BF16)],
        compiler_params=pltpu.CompilerParams(vmem_limit_bytes=32 << 20),
        name="gram",
    )(prior_gram_blocks, every, packed, ramp, amps, span_pos.reshape(1), reps)
    return (flow_next, gram_next)


def solution(mesh):
    return jax.shard_map(
        shards,
        mesh=mesh,
        in_specs=(
            P(None, "span", None, "chord"),
            P("span", None, "chord"),
            P("span", None, "chord"),
            P("span", None, "chord"),
            P(),
            P("span"),
            P(),
            P("span", "chord", None),
            P(),
            P(None, "chord", "span", None),
        ),
        out_specs=(P(None, "span", None, "chord"), P(None, "chord", "span", None)),
        check_vma=False,
    )
```

time: 321 us -> 124 us (0.39)
  the two profiles are of different devices: /device:TPU:51 before, /device:TPU:1 now
where the time goes in v2:
time: 124 us; the launch traced here: 123 us
  starting transfers between devices  47.1 us (38%)
  waiting for transfers between devices  36.8 us (30%)
  Pallas kernels  34.6 us (28%)
  local copies, waits for them, and re-layouts  3.92 us (3%)
    pallas_call x2, Pallas kernels, section(): pl.pallas_call(functools.partial(section_kernel, second=second), out_shap...  25.9 us
    all_to_all x1, starting transfers between devices, shards(): lax.all_to_all(amps.reshape((span_n * chord_n,) + amps.shape[2:]), ('span...  22.6 us
    all_to_all x1, waiting for transfers between devices, shards(): lax.all_to_all(send, 'span', 0, 0, tiled=True)  18.5 us
    all_to_all x1, waiting for transfers between devices, shards(): lax.all_to_all(amps.reshape((span_n * chord_n,) + amps.shape[2:]), ('span...  12.9 us
    ppermute x2, starting transfers between devices, exchange(): lax.ppermute(low, 'span', down)  6 us
    ppermute x2, starting transfers between devices, exchange(): lax.ppermute(high, 'span', up)  5.92 us
    ppermute x2, starting transfers between devices, exchange(): lax.ppermute(edge, 'chord', forward)  5.66 us
    all_to_all x1, starting transfers between devices, shards(): lax.all_to_all(send, 'span', 0, 0, tiled=True)  4.38 us
  transfers between devices with their start and end apart: 10, of which 6 were waited for; matrix products, arithmetic and copies ran while one was open for 1% of the time, Pallas kernels for 2%

profile of v2, /device:TPU:1, one launch (start us, length us, event | category | flops | bytes accessed | tf_op | source)
XLA Modules:
  0.0 123.3 jit_solution(8474647541301943700)
XLA Ops:
  0.6 0.0 copy-start.2
  0.6 0.0 copy-start.5
  0.7 3.6 %edges.1 = (bf16[3,2,64,128]{3,2,1,0:T(8,128)(2,1)}, bf16[3,3,64,128]{3,2,1,0:T(8,128)(2,1)}, bf16[3,3,64,128]{3,2,1,0:T(8,128)(2,1)}) custom-call(f32[3,32,64,128]{3,2,1,0:T(8,128)} %refs_10_.1), custom_call_target="tpu_custom_call" | custom-call | tf_op jit(solution)/shard_map/edges/pallas_call | solution.py:431
  4.3 0.0 copy-start.8
  4.3 0.0 copy-start.7
  4.3 2.7 %collective-permute-start = (bf16[3,3,64,128]{3,2,1,0:T(8,128)(2,1)}, bf16[3,3,64,128]{3,2,1,0:T(8,128)(2,1)S(1)}, u32[]{:S(2)}, u32[]{:S(2)}) collective-permute-start(bf16[3,3,64,128]{3,2,1,0:T(8,128)(2,1)} %get-tuple-element.13), channel_id=1, source_target_pairs={{0,8},{8,16},{16,24},{24,32},{32,40},{40,48},{48,56},{56,64},{64,7... | collective-permute-start | bytes 442376 | tf_op jit(solution)/shard_map/ppermute | solution.py:419
  6.9 0.7 collective-permute-start.1
  7.7 2.5 %collective-permute-start.2 = (bf16[3,2,64,128]{3,2,1,0:T(8,128)(2,1)}, bf16[3,2,64,128]{3,2,1,0:T(8,128)(2,1)S(1)}, u32[]{:S(2)}, u32[]{:S(2)}) collective-permute-start(bf16[3,2,64,128]{3,2,1,0:T(8,128)(2,1)} %get-tuple-element.15), channel_id=1, source_target_pairs={{0,1},{1,2},{2,3},{3,4},{4,5},{5,6},{6,7},{8,9},{9,10},{10,11},{11... | collective-permute-start | bytes 294920 | tf_op jit(solution)/shard_map/ppermute | solution.py:421
  10.2 1.3 %collective-permute-start.3 = (bf16[3,2,64,128]{3,2,1,0:T(8,128)(2,1)}, bf16[3,2,64,128]{3,2,1,0:T(8,128)(2,1)S(1)}, u32[]{:S(2)}, u32[]{:S(2)}) collective-permute-start(bf16[3,2,64,128]{3,2,1,0:T(8,128)(2,1)} %get-tuple-element.15), channel_id=1, source_target_pairs={{1,0},{2,1},{3,2},{4,3},{5,4},{6,5},{7,6},{9,8},{10,9},{11,10},{12... | collective-permute-start | bytes 294920 | tf_op jit(solution)/shard_map/ppermute | solution.py:422
  11.5 0.6 collective-permute-done.2.refs_3_
  12.1 3.9 %collective-permute-done.3.refs_4_ = bf16[3,2,64,128]{3,2,1,0:T(8,128)(2,1)S(1)} collective-permute-done((bf16[3,2,64,128]{3,2,1,0:T(8,128)(2,1)}, bf16[3,2,64,128]{3,2,1,0:T(8,128)(2,1)S(1)}, u32[]{:S(2)}, u32[]{:S(2)}) %collective-permute-start.3) | collective-permute-done | bytes 98336 | tf_op jit(solution)/shard_map/ppermute | solution.py:422
  16.0 0.0 collective-permute-done.refs_1_
  16.0 0.0 collective-permute-done.1.refs_2_
  16.0 0.0 copy-done.2
  16.0 0.0 copy-done.5
  16.0 13.6 %section_one.1 = (f32[3,32,64,128]{3,2,1,0:T(8,128)S(1)}, bf16[3,3,64,128]{3,2,1,0:T(8,128)(2,1)S(1)}, bf16[3,3,64,128]{3,2,1,0:T(8,128)(2,1)S(1)}, bf16[3,2,64,128]{3,2,1,0:T(8,128)(2,1)S(1)}) custom-call(f32[3,32,64,128]{3,2,1,0:T(8,128)} %refs_10_.1, bf16[3,3,64,128]{3,2,1,0:T(8,128)(2,1)S(1)} %collective-permute-done.refs_1_, ...), custom_call_target="tpu_custom_call" | custom-call | flops 60000000 | bytes 12000000 | tf_op jit(solution)/shard_map/section_one/pallas_call | solution.py:301
  29.6 0.0 copy-start
  29.7 1.6 %copy-done = f32[3,32,64,128]{3,2,1,0:T(8,128)} copy-done((f32[3,32,64,128]{3,2,1,0:T(8,128)}, f32[3,32,64,128]{3,2,1,0:T(8,128)S(1)}, u32[]{:S(2)}) %copy-start) | copy-done | bytes 3145752
  31.3 3.2 %collective-permute-start.6 = (bf16[3,2,64,128]{3,2,1,0:T(8,128)(2,1)S(1)}, bf16[3,2,64,128]{3,2,1,0:T(8,128)(2,1)S(1)}, u32[]{:S(2)}, u32[]{:S(2)}) collective-permute-start(bf16[3,2,64,128]{3,2,1,0:T(8,128)(2,1)S(1)} %get-tuple-element.19), channel_id=1, source_target_pairs={{0,1},{1,2},{2,3},{3,4},{4,5},{5,6},{6,7},{8,9},{9,10},{10,11},{11... | collective-permute-start | bytes 294920 | tf_op jit(solution)/shard_map/ppermute | solution.py:421
  34.5 1.3 %collective-permute-start.7 = (bf16[3,2,64,128]{3,2,1,0:T(8,128)(2,1)S(1)}, bf16[3,2,64,128]{3,2,1,0:T(8,128)(2,1)S(1)}, u32[]{:S(2)}, u32[]{:S(2)}) collective-permute-start(bf16[3,2,64,128]{3,2,1,0:T(8,128)(2,1)S(1)} %get-tuple-element.19), channel_id=1, source_target_pairs={{1,0},{2,1},{3,2},{4,3},{5,4},{6,5},{7,6},{9,8},{10,9},{11,10},{12... | collective-permute-start | bytes 294920 | tf_op jit(solution)/shard_map/ppermute | solution.py:422
  35.8 3.2 %collective-permute-start.4 = (bf16[3,3,64,128]{3,2,1,0:T(8,128)(2,1)S(1)}, bf16[3,3,64,128]{3,2,1,0:T(8,128)(2,1)S(1)}, u32[]{:S(2)}, u32[]{:S(2)}) collective-permute-start(bf16[3,3,64,128]{3,2,1,0:T(8,128)(2,1)S(1)} %get-tuple-element.17), channel_id=1, source_target_pairs={{0,8},{8,16},{16,24},{24,32},{32,40},{40,48},{48,56},{56,64},{64,7... | collective-permute-start | bytes 442376 | tf_op jit(solution)/shard_map/ppermute | solution.py:419
  39.0 5.3 %collective-permute-start.5 = (bf16[3,3,64,128]{3,2,1,0:T(8,128)(2,1)S(1)}, bf16[3,3,64,128]{3,2,1,0:T(8,128)(2,1)S(1)}, u32[]{:S(2)}, u32[]{:S(2)}) collective-permute-start(bf16[3,3,64,128]{3,2,1,0:T(8,128)(2,1)S(1)} %get-tuple-element.18), channel_id=1, source_target_pairs={{8,0},{16,8},{24,16},{32,24},{40,32},{48,40},{56,48},{64,56},{72,6... | collective-permute-start | bytes 442376 | tf_op jit(solution)/shard_map/ppermute | solution.py:420
  44.3 0.0 copy-done.8
  44.3 0.0 copy-done.7
  44.3 0.1 copy.16
  44.4 0.1 copy.18.refs_12_
  44.5 0.0 collective-permute-done.6.refs_3_
  44.5 0.0 collective-permute-done.7.refs_4_
  44.5 0.6 collective-permute-done.4.refs_1_
  45.1 0.2 collective-permute-done.5.refs_2_
  45.3 0.0 copy-start.9
  45.3 0.0 copy-start.1
  45.3 0.0 copy-start.3
  45.3 0.0 copy-start.6
  45.3 12.3 %section_two.1 = (f32[3,32,64,128]{3,2,1,0:T(8,128)}, f32[8,4,128]{2,1,0:T(4,128)S(1)}) custom-call(f32[3,32,64,128]{3,2,1,0:T(8,128)} %copy-done, bf16[3,3,64,128]{3,2,1,0:T(8,128)(2,1)S(1)} %collective-permute-done.4.refs_1_, bf16[3,3,64,128]{3,2,1,0:T(8,128)(2,1)S(1)} %collective-permute-done.5.refs_2_, ...), custom_call_target="tpu_custom_call" | custom-call | flops 60000000 | bytes 12000000 | tf_op jit(solution)/shard_map/section_two/pallas_call | solution.py:301
  57.7 0.8 broadcast_in_dim.2
  58.4 22.6 %all-to-all-start.1 = ((bf16[256,4,128]{2,1,0:T(4,128)(2,1)}), bf16[256,4,128]{2,1,0:T(4,128)(2,1)S(1)}, u32[]{:S(2)}, u32[]{:S(2)}) async-start(bf16[256,4,128]{2,1,0:T(4,128)(2,1)} %bitcast.4), calls=%async_computation.1 | async-start | bytes 524288 | tf_op jit(solution)/shard_map/all_to_all | solution.py:470
  81.0 0.0 copy-done.9
  81.0 0.1 pad_add_fusion
  81.1 0.6 broadcast_in_dim_tile.3.wanted_ref
  81.8 1.9 %spectra.1 = (bf16[32,256]{1,0:T(8,128)(2,1)}, bf16[32,32,256]{2,1,0:T(8,128)(2,1)}) custom-call(bf16[32,8,128]{2,1,0:T(8,128)(2,1)} %spectra_ref.1, s32[1,256]{1,0:T(1,128)} %broadcast_in_dim_tile.3.wanted_ref), custom_call_target="tpu_custom_call" | custom-call | tf_op jit(solution)/shard_map/spectra/pallas_call | solution.py:443
  83.7 12.9 %all-to-all-done.1.amp_ref = bf16[256,4,128]{2,1,0:T(4,128)(2,1)S(1)} async-done(((bf16[256,4,128]{2,1,0:T(4,128)(2,1)}), bf16[256,4,128]{2,1,0:T(4,128)(2,1)S(1)}, u32[]{:S(2)}, u32[]{:S(2)}) %all-to-all-start.1) | async-done | bytes 262176 | tf_op jit(solution)/shard_map/all_to_all | solution.py:470
  96.6 4.4 %all-to-all-start = ((bf16[32,32,256]{2,1,0:T(8,128)(2,1)}), bf16[32,32,256]{2,1,0:T(8,128)(2,1)S(1)}, u32[]{:S(2)}, u32[]{:S(2)}) async-start(bf16[32,32,256]{2,1,0:T(8,128)(2,1)} %get-tuple-element.21), calls=%async_computation | async-start | bytes 1048576 | tf_op jit(solution)/shard_map/all_to_all | solution.py:451
  101.0 18.5 %all-to-all-done = bf16[32,32,256]{2,1,0:T(8,128)(2,1)S(1)} async-done(((bf16[32,32,256]{2,1,0:T(8,128)(2,1)}), bf16[32,32,256]{2,1,0:T(8,128)(2,1)S(1)}, u32[]{:S(2)}, u32[]{:S(2)}) %all-to-all-start) | async-done | bytes 524320 | tf_op jit(solution)/shard_map/all_to_all | solution.py:451
  119.5 0.0 copy-done.1
  119.5 0.0 copy-done.3
  119.5 0.0 copy-done.6
  119.5 0.0 copy-start.4
  119.5 0.7 copy-done.4
  120.2 3.1 %gram.1 = f32[2,8,32,1024]{3,2,1,0:T(8,128)} custom-call(f32[2,8,32,1024]{3,2,1,0:T(8,128)S(1)} %copy-done.1, bf16[1024,256]{1,0:T(8,128)(2,1)S(1)} %bitcast.7, bf16[32,256]{1,0:T(8,128)(2,1)S(1)} %copy-done.4, f32[1,256]{1,0:T(1,128)S(1)} %copy-done.6, bf16[256,4,128]{2,1,0:T(4,128)(2,1)S(1)} %all-to-all-done.1.amp_ref, s32[1]{0:T(128)} %bitcast.5.where_ref, ...), custom_call_target="tpu_custom_call" | custom-call | tf_op jit(solution)/shard_map/gram/pallas_call | solution.py:483
  (5 shorter events, 0.0 us)
Async XLA Ops:
  0.6 15.4 %copy-start.2 = (bf16[384,256]{1,0:T(8,128)(2,1)S(1)}, bf16[384,256]{1,0:T(8,128)(2,1)}, u32[]{:S(2)}) copy-start(bf16[384,256]{1,0:T(8,128)(2,1)} %constant.19.clone.refs_9_) | copy-start | bytes 589828
  0.6 15.4 %copy-start.5 = (f32[3,3]{1,0:T(4,128)S(1)}, f32[3,3]{1,0:T(4,128)}, u32[]{:S(2)}) copy-start(f32[3,3]{1,0:T(4,128)} %refs_8_.3) | copy-start | bytes 112
  4.3 40.0 %copy-start.8 = (s32[32]{0:T(128)S(1)}, s32[32]{0:T(128)}, u32[]{:S(2)}) copy-start(s32[32]{0:T(128)} %param.18) | copy-start | bytes 388
  4.3 40.0 %copy-start.7 = (f32[64,2,64]{2,1,0:T(2,128)S(1)}, f32[64,2,64]{2,1,0:T(2,128)}, u32[]{:S(2)}) copy-start(f32[64,2,64]{2,1,0:T(2,128)} %param.19) | copy-start | bytes 98308
  4.3 11.8 %collective-permute-start = (bf16[3,3,64,128]{3,2,1,0:T(8,128)(2,1)}, bf16[3,3,64,128]{3,2,1,0:T(8,128)(2,1)S(1)}, u32[]{:S(2)}, u32[]{:S(2)}) collective-permute-start(bf16[3,3,64,128]{3,2,1,0:T(8,128)(2,1)} %get-tuple-element.13), channel_id=1, source_target_pairs={{0,8},{8,16},{16,24},{24,32},{32,40},{40,48},{48,56},{56,64},{64,7... | collective-permute-start | bytes 442376 | tf_op jit(solution)/shard_map/ppermute | solution.py:419
  6.9 9.1 %collective-permute-start.1 = (bf16[3,3,64,128]{3,2,1,0:T(8,128)(2,1)}, bf16[3,3,64,128]{3,2,1,0:T(8,128)(2,1)S(1)}, u32[]{:S(2)}, u32[]{:S(2)}) collective-permute-start(bf16[3,3,64,128]{3,2,1,0:T(8,128)(2,1)} %get-tuple-element.14), channel_id=1, source_target_pairs={{8,0},{16,8},{24,16},{32,24},{40,32},{48,40},{56,48},{64,56},{72,6... | collective-permute-start | bytes 442376 | tf_op jit(solution)/shard_map/ppermute | solution.py:420
  7.7 4.4 %collective-permute-start.2 = (bf16[3,2,64,128]{3,2,1,0:T(8,128)(2,1)}, bf16[3,2,64,128]{3,2,1,0:T(8,128)(2,1)S(1)}, u32[]{:S(2)}, u32[]{:S(2)}) collective-permute-start(bf16[3,2,64,128]{3,2,1,0:T(8,128)(2,1)} %get-tuple-element.15), channel_id=1, source_target_pairs={{0,1},{1,2},{2,3},{3,4},{4,5},{5,6},{6,7},{8,9},{9,10},{10,11},{11... | collective-permute-start | bytes 294920 | tf_op jit(solution)/shard_map/ppermute | solution.py:421
  10.2 5.9 %collective-permute-start.3 = (bf16[3,2,64,128]{3,2,1,0:T(8,128)(2,1)}, bf16[3,2,64,128]{3,2,1,0:T(8,128)(2,1)S(1)}, u32[]{:S(2)}, u32[]{:S(2)}) collective-permute-start(bf16[3,2,64,128]{3,2,1,0:T(8,128)(2,1)} %get-tuple-element.15), channel_id=1, source_target_pairs={{1,0},{2,1},{3,2},{4,3},{5,4},{6,5},{7,6},{9,8},{10,9},{11,10},{12... | collective-permute-start | bytes 294920 | tf_op jit(solution)/shard_map/ppermute | solution.py:422
  29.6 1.6 %copy-start = (f32[3,32,64,128]{3,2,1,0:T(8,128)}, f32[3,32,64,128]{3,2,1,0:T(8,128)S(1)}, u32[]{:S(2)}) copy-start(f32[3,32,64,128]{3,2,1,0:T(8,128)S(1)} %get-tuple-element.16.refs_0_) | copy-start | bytes 9437188
  31.3 13.2 %collective-permute-start.6 = (bf16[3,2,64,128]{3,2,1,0:T(8,128)(2,1)S(1)}, bf16[3,2,64,128]{3,2,1,0:T(8,128)(2,1)S(1)}, u32[]{:S(2)}, u32[]{:S(2)}) collective-permute-start(bf16[3,2,64,128]{3,2,1,0:T(8,128)(2,1)S(1)} %get-tuple-element.19), channel_id=1, source_target_pairs={{0,1},{1,2},{2,3},{3,4},{4,5},{5,6},{6,7},{8,9},{9,10},{10,11},{11... | collective-permute-start | bytes 294920 | tf_op jit(solution)/shard_map/ppermute | solution.py:421
  34.5 10.0 %collective-permute-start.7 = (bf16[3,2,64,128]{3,2,1,0:T(8,128)(2,1)S(1)}, bf16[3,2,64,128]{3,2,1,0:T(8,128)(2,1)S(1)}, u32[]{:S(2)}, u32[]{:S(2)}) collective-permute-start(bf16[3,2,64,128]{3,2,1,0:T(8,128)(2,1)S(1)} %get-tuple-element.19), channel_id=1, source_target_pairs={{1,0},{2,1},{3,2},{4,3},{5,4},{6,5},{7,6},{9,8},{10,9},{11,10},{12... | collective-permute-start | bytes 294920 | tf_op jit(solution)/shard_map/ppermute | solution.py:422
  35.8 9.3 %collective-permute-start.4 = (bf16[3,3,64,128]{3,2,1,0:T(8,128)(2,1)S(1)}, bf16[3,3,64,128]{3,2,1,0:T(8,128)(2,1)S(1)}, u32[]{:S(2)}, u32[]{:S(2)}) collective-permute-start(bf16[3,3,64,128]{3,2,1,0:T(8,128)(2,1)S(1)} %get-tuple-element.17), channel_id=1, source_target_pairs={{0,8},{8,16},{16,24},{24,32},{32,40},{40,48},{48,56},{56,64},{64,7... | collective-permute-start | bytes 442376 | tf_op jit(solution)/shard_map/ppermute | solution.py:419
  39.0 6.3 %collective-permute-start.5 = (bf16[3,3,64,128]{3,2,1,0:T(8,128)(2,1)S(1)}, bf16[3,3,64,128]{3,2,1,0:T(8,128)(2,1)S(1)}, u32[]{:S(2)}, u32[]{:S(2)}) collective-permute-start(bf16[3,3,64,128]{3,2,1,0:T(8,128)(2,1)S(1)} %get-tuple-element.18), channel_id=1, source_target_pairs={{8,0},{16,8},{24,16},{32,24},{40,32},{48,40},{56,48},{64,56},{72,6... | collective-permute-start | bytes 442376 | tf_op jit(solution)/shard_map/ppermute | solution.py:420
  45.3 35.7 %copy-start.9 = (s32[16]{0:T(128)S(1)}, s32[16]{0:T(128)}, u32[]{:S(2)}) copy-start(s32[16]{0:T(128)} %param.21) | copy-start | bytes 196
  45.3 74.2 %copy-start.1 = (f32[2,8,32,1024]{3,2,1,0:T(8,128)S(1)}, f32[2,8,32,1024]{3,2,1,0:T(8,128)}, u32[]{:S(2)}) copy-start(f32[2,8,32,1024]{3,2,1,0:T(8,128)} %prior_ref.1) | copy-start | bytes 6291460
  45.3 74.2 %copy-start.3 = (bf16[2,128,128]{2,1,0:T(8,128)(2,1)S(1)}, bf16[2,128,128]{2,1,0:T(8,128)(2,1)}, u32[]{:S(2)}) copy-start(bf16[2,128,128]{2,1,0:T(8,128)(2,1)} %constant.21.clone.rep_ref) | copy-start | bytes 196612
  45.3 74.2 %copy-start.6 = (f32[1,256]{1,0:T(1,128)S(1)}, f32[1,256]{1,0:T(1,128)}, u32[]{:S(2)}) copy-start(f32[1,256]{1,0:T(1,128)} %constant.20.clone.ramp_ref) | copy-start | bytes 3076
  58.4 38.1 %all-to-all-start.1 = ((bf16[256,4,128]{2,1,0:T(4,128)(2,1)}), bf16[256,4,128]{2,1,0:T(4,128)(2,1)S(1)}, u32[]{:S(2)}, u32[]{:S(2)}) async-start(bf16[256,4,128]{2,1,0:T(4,128)(2,1)} %bitcast.4), calls=%async_computation.1 | async-start | bytes 524288 | tf_op jit(solution)/shard_map/all_to_all | solution.py:470
  96.6 22.9 %all-to-all-start = ((bf16[32,32,256]{2,1,0:T(8,128)(2,1)}), bf16[32,32,256]{2,1,0:T(8,128)(2,1)S(1)}, u32[]{:S(2)}, u32[]{:S(2)}) async-start(bf16[32,32,256]{2,1,0:T(8,128)(2,1)} %get-tuple-element.21), calls=%async_computation | async-start | bytes 1048576 | tf_op jit(solution)/shard_map/all_to_all | solution.py:451
  119.5 0.7 copy-start.4

commit v3 on v2

--- a/solution.py
+++ b/solution.py
@@ -83,7 +83,7 @@
     refs = list(refs)
     take = refs.pop
     state_hbm = take(0)
-    span_low, span_high, chord_low, chord_high = (take(0) for _ in range(4))
+    halo_hbm = [take(0) for _ in range(4)]
     vs_hbm, vc_hbm, nu_hbm = (take(0) for _ in range(3))
     mix, table_ref = take(0), take(0)
     if second:
@@ -93,12 +93,13 @@
         amp_out = take(0)
     else:
         low_out, high_out, cells_out = (take(0) for _ in range(3))
-    wide, result, chord, halos, cells, vs, vc, nu, in_sem, out_sem = (take(0) for _ in range(10))
+    wide, result, chord_a, chord_b, halos, cells, vs, vc, nu, in_sem, out_sem = (take(0) for _ in range(11))
     if second:
         before, before_sem, columns, amps = (take(0) for _ in range(4))
+    span_low, span_high, chord_low, chord_high, halo_sem = (take(0) for _ in range(5))
 
     count, stations, normal = wide.shape[0], vs.shape[0], vs.shape[1]
-    chunks, pairs = 4, stations // 2
+    chunks, pairs = 8, stations // 2
     per = stations // chunks
 
     def copies(c):
@@ -119,6 +120,14 @@
             )
         return todo
 
+    halo_copies = [
+        pltpu.make_async_copy(source, target, halo_sem.at[i])
+        for i, (source, target) in enumerate(
+            zip(halo_hbm, (span_low, span_high, chord_low, chord_high))
+        )
+    ]
+    for copy in halo_copies:
+        copy.start()
     for c in range(chunks):
         for copy in copies(c):
             copy.start()
@@ -126,6 +135,10 @@
     nothing = jnp.zeros((count, stations, 8, LANES), F32)
     wide[:, 3 : 3 + stations, 0:8, :] = nothing
     wide[:, 3 : 3 + stations, 8 + normal : 16 + normal, :] = nothing
+    if second:
+        columns[...] = jnp.zeros(columns.shape, F32)
+    for copy in halo_copies:
+        copy.wait()
     wide[:, 0:3, 8 : 8 + normal, :] = span_low[...].astype(F32)
     wide[:, 3 + stations : 6 + stations, 8 : 8 + normal, :] = span_high[...].astype(F32)
     place = lax.rem(lax.broadcasted_iota(jnp.int32, (normal, LANES), 1), 8)
@@ -135,11 +148,9 @@
                 place < 3, chord_low[q, half].astype(F32), chord_high[q, half].astype(F32)
             )
             halos[q, half] = jnp.where(place < 6, near, 0.0)
-    if second:
-        columns[...] = jnp.zeros(columns.shape, F32)
-
-    def matmuls(p):
-        slot, half = lax.rem(p, 2), lax.div(p, 8)
+
+    def matmuls(p, chord):
+        half = lax.div(p, 8)
         parts = []
         for q in range(count):
             for d in range(2):
@@ -149,7 +160,7 @@
                 shift = lax.rem(LANES - 8 * lax.rem(2 * p + d, 16), LANES)
                 beyond = pltpu.roll(halos[q, half], shift, 1).astype(BF16)
                 parts.append(jnp.concatenate([high, low, beyond], axis=1))
-        chord[slot] = jnp.dot(
+        chord[...] = jnp.dot(
             jnp.concatenate(parts), table_ref[...], preferred_element_type=F32
         )
 
@@ -161,9 +172,13 @@
     ROWS = 16
     lane = lax.broadcasted_iota(jnp.int32, (ROWS, LANES), 1)
 
-    def body(p, carry):
-        matmuls(jnp.minimum(p + 1, pairs - 1))
-        slot = lax.rem(p, 2)
+    def body(i, carry):
+        pair(2 * i, chord_a, chord_b)
+        pair(2 * i + 1, chord_b, chord_a)
+        return carry
+
+    def pair(p, chord, later):
+        matmuls(jnp.minimum(p + 1, pairs - 1), later)
         for half in range(2):
             s = 2 * p + half
             for tile in range(normal // ROWS):
@@ -194,8 +209,8 @@
                         both = total if both is None else both + total
                     start = (2 * q + half) * normal + ROWS * tile
                     crow = slice(start, start + ROWS)
-                    chord_first = chord[slot, crow, 0:LANES]
-                    chord_second = chord[slot, crow, LANES : 2 * LANES]
+                    chord_first = chord[crow, 0:LANES]
+                    chord_second = chord[crow, LANES : 2 * LANES]
                     both = both + (centre[q] * float(2 * CENTRE) + chord_second)
                     value = a * first + b * chord_first + g * both
                     for e in range(count):
@@ -215,7 +230,6 @@
                             lax.div(lane, 8) == station, moved, kept
                         )
         out_copy(p).start()
-        return carry
 
     def out_copy(p):
         two = pl.ds(2 * p, 2)
@@ -226,11 +240,11 @@
             copy.wait()
 
     arrive(0)
-    matmuls(0)
+    matmuls(0, chord_a)
     for c in range(chunks):
         if c + 1 < chunks:
             arrive(c + 1)
-        lax.fori_loop(c * pairs // chunks, (c + 1) * pairs // chunks, body, 0)
+        lax.fori_loop(c * pairs // chunks // 2, (c + 1) * pairs // chunks // 2, body, 0)
 
     if second:
         amp = fine_dot(columns[...].T, band_ref[...])
@@ -265,7 +279,7 @@
     vmem = pl.BlockSpec(memory_space=pltpu.VMEM)
     smem = pl.BlockSpec(memory_space=pltpu.SMEM)
     args = [state, *halos, *fields, mixing, table]
-    specs = [hbm] + [vmem] * 4 + [hbm] * 3 + [smem, vmem]
+    specs = [hbm] * 8 + [smem, vmem]
     shapes = [jax.ShapeDtypeStruct(state.shape, F32)]
     if second:
         args += [flow, te_local, band_table]
@@ -276,35 +290,39 @@
         shapes.append(jax.ShapeDtypeStruct((count, stations // 16, normal, LANES), BF16))
     field = pltpu.VMEM((stations, normal, LANES), BF16)
     args = [
-        pltpu.with_memory_space_constraint(x, pltpu.HBM) if spec is hbm else x
+        pltpu.with_memory_space_constraint(x, pltpu.HBM) if spec is hbm and not (second and x is state) else x
         for x, spec in zip(args, specs)
     ]
     scratch = [
         pltpu.VMEM((count, stations + 6, normal + 16, LANES), F32),
         pltpu.VMEM((count, stations, normal, LANES), F32),
-        pltpu.VMEM((2, count * 2 * normal, 2 * LANES), F32),
+        pltpu.VMEM((count * 2 * normal, 2 * LANES), F32),
+        pltpu.VMEM((count * 2 * normal, 2 * LANES), F32),
         pltpu.VMEM((count, stations // 16, normal, LANES), F32),
         pltpu.VMEM((count, stations // 16, normal, LANES), F32),
         field,
         field,
         field,
-        pltpu.SemaphoreType.DMA((4, 4)),
+        pltpu.SemaphoreType.DMA((4, 8)),
         pltpu.SemaphoreType.DMA((pairs,)),
     ]
     if second:
         scratch += [
             pltpu.VMEM((count, stations, normal, LANES), F32),
-            pltpu.SemaphoreType.DMA((4,)),
+            pltpu.SemaphoreType.DMA((8,)),
             pltpu.VMEM((normal, LANES), F32),
             pltpu.VMEM((stations, LANES), F32),
         ]
+    scratch += [pltpu.VMEM((count, 3, normal, LANES), BF16)] * 2
+    scratch += [pltpu.VMEM((count, stations // 16, normal, LANES), BF16)] * 2
+    scratch.append(pltpu.SemaphoreType.DMA((4,)))
     return pl.pallas_call(
         functools.partial(section_kernel, second=second),
         out_shape=tuple(shapes),
         in_specs=specs,
         out_specs=tuple([hbm] + [vmem] * (len(shapes) - 1)),
         scratch_shapes=scratch,
-        compiler_params=pltpu.CompilerParams(vmem_limit_bytes=40 << 20),
+        compiler_params=pltpu.CompilerParams(vmem_limit_bytes=20 << 20),
         cost_estimate=pl.CostEstimate(
             flops=60000000, transcendentals=0, bytes_accessed=12000000
         ),
@@ -422,22 +440,6 @@
             lax.ppermute(edge, "chord", backward),
         )
 
-    edge_shape = jax.ShapeDtypeStruct((count, stations // 16, normal, LANES), BF16)
-    ends_shape = jax.ShapeDtypeStruct((count, 3, normal, LANES), BF16)
-
-    def per_quantity(shape):
-        return pl.BlockSpec((1,) + shape.shape[1:], lambda q: (q, 0, 0, 0))
-
-    edge, low, high = pl.pallas_call(
-        edges_kernel,
-        grid=(count,),
-        out_shape=(edge_shape, ends_shape, ends_shape),
-        in_specs=[per_quantity(flow_state)],
-        out_specs=(per_quantity(edge_shape), per_quantity(ends_shape), per_quantity(ends_shape)),
-        name="edges",
-    )(flow_state)
-    halos = exchange(low, high, edge)
-
     width = bands * 2 * segs
     wanted = jnp.tile(jnp.concatenate([offsets, offsets + slots]), bands)[None]
     packed, send = pl.pallas_call(
@@ -450,8 +452,25 @@
     )(spectra, wanted)
     every = lax.all_to_all(send, "span", 0, 0, tiled=True).reshape(span_n * stations, width)
 
+    edge_shape = jax.ShapeDtypeStruct((count, stations // 16, normal, LANES), BF16)
+    ends_shape = jax.ShapeDtypeStruct((count, 3, normal, LANES), BF16)
+
+    def per_quantity(shape):
+        return pl.BlockSpec((1,) + shape.shape[1:], lambda q: (q, 0, 0, 0))
+
+    edge, low, high = pl.pallas_call(
+        edges_kernel,
+        grid=(count,),
+        out_shape=(edge_shape, ends_shape, ends_shape),
+        in_specs=[per_quantity(flow_state)],
+        out_specs=(per_quantity(edge_shape), per_quantity(ends_shape), per_quantity(ends_shape)),
+        name="edges",
+    )(flow_state)
+    halos = exchange(low, high, edge)
+
     (section_one, low, high, edge) = section(flow_state, halos, fields, mixing, table)
     halos = exchange(low, high, edge)
+    halos, every = lax.optimization_barrier((halos, every))
 
     te_local = te_index - chord_pos * cells
     band_table = band_response.reshape(normal, 2, chord_n, bands).transpose(0, 2, 1, 3)
@@ -497,7 +516,15 @@
         scratch_shapes=[pltpu.VMEM((2 * bands * stations, 2 * width + LANES), BF16)],
         compiler_params=pltpu.CompilerParams(vmem_limit_bytes=32 << 20),
         name="gram",
-    )(prior_gram_blocks, every, packed, ramp, amps, span_pos.reshape(1), reps)
+    )(
+        pltpu.with_memory_space_constraint(prior_gram_blocks, pltpu.HBM),
+        pltpu.with_memory_space_constraint(every, pltpu.HBM),
+        packed,
+        ramp,
+        amps,
+        span_pos.reshape(1),
+        reps,
+    )
     return (flow_next, gram_next)
 
 

time: 124 us -> 112 us (0.903)
  waiting for transfers between devices: 36.8 us -> 17.8 us
  starting transfers between devices: 47.1 us -> 55.9 us
  Pallas kernels: 34.6 us -> 31.5 us
  other arithmetic: 0.09 us -> 1.43 us
    all_to_all x1, waiting for transfers between devices: 18.5 us -> 0.01 us  [shards(): lax.all_to_all(send, 'span', 0, 0, tiled=True)]
    all_to_all x1, starting transfers between devices: 4.38 us -> 12.6 us  [shards(): lax.all_to_all(send, 'span', 0, 0, tiled=True)]
    pallas_call x2, Pallas kernels: 25.9 us -> 21.3 us  [section(): pl.pallas_call(functools.partial(section_kernel, second=second), out_shap...]
    ppermute x2, starting transfers between devices: 5.66 us -> 9.29 us  [exchange(): lax.ppermute(edge, 'chord', forward)]
    ppermute x2, waiting for transfers between devices: 3.94 us -> 0.68 us  [exchange(): lax.ppermute(edge, 'chord', backward)]
    all_to_all x1, waiting for transfers between devices: 12.9 us -> 15.5 us  [shards(): lax.all_to_all(amps.reshape((span_n * chord_n,) + amps.shape[2:]), ('span...]
    ppermute x2, starting transfers between devices: 6 us -> 4.05 us  [exchange(): lax.ppermute(low, 'span', down)]
    pallas_call x1, Pallas kernels: 3.13 us -> 4.75 us  [shards(): pl.pallas_call(gram_kernel, grid=(tiles,), out_shape=jax.ShapeDtypeStruct...]
  transfers between devices with their start and end apart: 10 -> 10, of which waited for: 6 -> 5; matrix products, arithmetic and copies ran while one was open for 1% -> 1% of each run, Pallas kernels for 2% -> 14%
where the time goes in v3:
time: 112 us; the launch traced here: 111 us
  starting transfers between devices  55.9 us (50%)
  Pallas kernels  31.5 us (28%)
  waiting for transfers between devices  17.8 us (16%)
  local copies, waits for them, and re-layouts  3.7 us (3%)
  other arithmetic  1.43 us (1%)
    all_to_all x1, starting transfers between devices, shards(): lax.all_to_all(amps.reshape((span_n * chord_n,) + amps.shape[2:]), ('span...  22.6 us
    pallas_call x2, Pallas kernels, section(): pl.pallas_call(functools.partial(section_kernel, second=second), out_shap...  21.3 us
    all_to_all x1, waiting for transfers between devices, shards(): lax.all_to_all(amps.reshape((span_n * chord_n,) + amps.shape[2:]), ('span...  15.5 us
    all_to_all x1, starting transfers between devices, shards(): lax.all_to_all(send, 'span', 0, 0, tiled=True)  12.6 us
    ppermute x2, starting transfers between devices, exchange(): lax.ppermute(edge, 'chord', forward)  9.29 us
    pallas_call x1, Pallas kernels, shards(): pl.pallas_call(gram_kernel, grid=(tiles,), out_shape=jax.ShapeDtypeStruct...  4.75 us
    ppermute x2, starting transfers between devices, exchange(): lax.ppermute(high, 'span', up)  4.69 us
    ppermute x2, starting transfers between devices, exchange(): lax.ppermute(low, 'span', down)  4.05 us
  transfers between devices with their start and end apart: 10, of which 5 were waited for; matrix products, arithmetic and copies ran while one was open for 1% of the time, Pallas kernels for 14%

profile of v3, /device:TPU:1, one launch (start us, length us, event | category | flops | bytes accessed | tf_op | source)
XLA Modules:
  0.0 111.1 jit_solution(2539993324497350500)
XLA Ops:
  0.6 0.0 copy-start
  0.6 0.0 copy-start.3
  0.7 0.7 broadcast_add_fusion
  1.3 0.7 pad_add_fusion
  2.1 0.6 broadcast_in_dim_tile.3.wanted_ref
  2.7 1.9 %spectra.1 = (bf16[32,256]{1,0:T(8,128)(2,1)}, bf16[32,32,256]{2,1,0:T(8,128)(2,1)}) custom-call(bf16[32,8,128]{2,1,0:T(8,128)(2,1)} %spectra_ref.1, s32[1,256]{1,0:T(1,128)} %broadcast_in_dim_tile.3.wanted_ref), custom_call_target="tpu_custom_call" | custom-call | tf_op jit(solution)/shard_map/spectra/pallas_call | solution.py:445
  4.6 12.6 %all-to-all-start = ((bf16[32,32,256]{2,1,0:T(8,128)(2,1)}), bf16[32,32,256]{2,1,0:T(8,128)(2,1)}, u32[]{:S(2)}, u32[]{:S(2)}) async-start(bf16[32,32,256]{2,1,0:T(8,128)(2,1)} %get-tuple-element.25), calls=%async_computation | async-start | bytes 1048576 | tf_op jit(solution)/shard_map/all_to_all | solution.py:453
  17.3 3.6 %edges.1 = (bf16[3,2,64,128]{3,2,1,0:T(8,128)(2,1)}, bf16[3,3,64,128]{3,2,1,0:T(8,128)(2,1)}, bf16[3,3,64,128]{3,2,1,0:T(8,128)(2,1)}) custom-call(f32[3,32,64,128]{3,2,1,0:T(8,128)} %refs_10_.1), custom_call_target="tpu_custom_call" | custom-call | tf_op jit(solution)/shard_map/edges/pallas_call | solution.py:461
  20.9 0.0 copy-start.8
  20.9 1.6 %collective-permute-start = (bf16[3,3,64,128]{3,2,1,0:T(8,128)(2,1)}, bf16[3,3,64,128]{3,2,1,0:T(8,128)(2,1)S(1)}, u32[]{:S(2)}, u32[]{:S(2)}) collective-permute-start(bf16[3,3,64,128]{3,2,1,0:T(8,128)(2,1)} %get-tuple-element.18), channel_id=1, source_target_pairs={{0,8},{8,16},{16,24},{24,32},{32,40},{40,48},{48,56},{56,64},{64,7... | collective-permute-start | bytes 442376 | tf_op jit(solution)/shard_map/ppermute | solution.py:437
  22.5 0.0 collective-permute-start.1
  22.5 1.3 %collective-permute-start.3 = (bf16[3,2,64,128]{3,2,1,0:T(8,128)(2,1)}, bf16[3,2,64,128]{3,2,1,0:T(8,128)(2,1)S(1)}, u32[]{:S(2)}, u32[]{:S(2)}) collective-permute-start(bf16[3,2,64,128]{3,2,1,0:T(8,128)(2,1)} %get-tuple-element.20), channel_id=1, source_target_pairs={{1,0},{2,1},{3,2},{4,3},{5,4},{6,5},{7,6},{9,8},{10,9},{11,10},{12... | collective-permute-start | bytes 294920 | tf_op jit(solution)/shard_map/ppermute | solution.py:440
  23.8 4.0 %collective-permute-start.2 = (bf16[3,2,64,128]{3,2,1,0:T(8,128)(2,1)}, bf16[3,2,64,128]{3,2,1,0:T(8,128)(2,1)S(1)}, u32[]{:S(2)}, u32[]{:S(2)}) collective-permute-start(bf16[3,2,64,128]{3,2,1,0:T(8,128)(2,1)} %get-tuple-element.20), channel_id=1, source_target_pairs={{0,1},{1,2},{2,3},{3,4},{4,5},{5,6},{6,7},{8,9},{9,10},{10,11},{11... | collective-permute-start | bytes 294920 | tf_op jit(solution)/shard_map/ppermute | solution.py:439
  27.8 0.7 collective-permute-done.3.refs_4_
  28.5 0.0 copy-start.6
  28.5 1.3 %collective-permute-done.2.refs_3_ = bf16[3,2,64,128]{3,2,1,0:T(8,128)(2,1)S(1)} collective-permute-done((bf16[3,2,64,128]{3,2,1,0:T(8,128)(2,1)}, bf16[3,2,64,128]{3,2,1,0:T(8,128)(2,1)S(1)}, u32[]{:S(2)}, u32[]{:S(2)}) %collective-permute-start.2) | collective-permute-done | bytes 98336 | tf_op jit(solution)/shard_map/ppermute | solution.py:439
  29.7 0.0 copy-start.7
  29.7 0.0 collective-permute-done.refs_1_
  29.7 0.0 copy-done.6
  29.7 0.6 copy-done.7
  30.3 0.0 copy-start.5
  30.4 0.0 collective-permute-done.1.refs_2_
  30.4 0.7 copy-done.5
  31.0 0.0 copy-done
  31.0 0.0 copy-done.3
  31.0 11.7 %section_one.1 = (f32[3,32,64,128]{3,2,1,0:T(8,128)S(1)}, bf16[3,3,64,128]{3,2,1,0:T(8,128)(2,1)}, bf16[3,3,64,128]{3,2,1,0:T(8,128)(2,1)}, bf16[3,2,64,128]{3,2,1,0:T(8,128)(2,1)}) custom-call(f32[3,32,64,128]{3,2,1,0:T(8,128)} %refs_10_.1, bf16[3,3,64,128]{3,2,1,0:T(8,128)(2,1)} %copy-done.5, bf16[3,3,64,128]{3,2,1,0:T(8,128)(2,1)} %collective-permute-done.1.refs_2_, ...), custom_call_target="tpu_custom_call" | custom-call | flops 60000000 | bytes 12000000 | tf_op jit(solution)/shard_map/section_one/pallas_call | solution.py:319
  42.8 1.3 %collective-permute-start.7 = (bf16[3,2,64,128]{3,2,1,0:T(8,128)(2,1)}, bf16[3,2,64,128]{3,2,1,0:T(8,128)(2,1)}, u32[]{:S(2)}, u32[]{:S(2)}) collective-permute-start(bf16[3,2,64,128]{3,2,1,0:T(8,128)(2,1)} %get-tuple-element.24), channel_id=1, source_target_pairs={{1,0},{2,1},{3,2},{4,3},{5,4},{6,5},{7,6},{9,8},{10,9},{11,10},{12... | collective-permute-start | bytes 294920 | tf_op jit(solution)/shard_map/ppermute | solution.py:440
  44.1 5.3 %collective-permute-start.6 = (bf16[3,2,64,128]{3,2,1,0:T(8,128)(2,1)}, bf16[3,2,64,128]{3,2,1,0:T(8,128)(2,1)}, u32[]{:S(2)}, u32[]{:S(2)}) collective-permute-start(bf16[3,2,64,128]{3,2,1,0:T(8,128)(2,1)} %get-tuple-element.24), channel_id=1, source_target_pairs={{0,1},{1,2},{2,3},{3,4},{4,5},{5,6},{6,7},{8,9},{9,10},{10,11},{11... | collective-permute-start | bytes 294920 | tf_op jit(solution)/shard_map/ppermute | solution.py:439
  49.3 3.1 %collective-permute-start.4 = (bf16[3,3,64,128]{3,2,1,0:T(8,128)(2,1)}, bf16[3,3,64,128]{3,2,1,0:T(8,128)(2,1)}, u32[]{:S(2)}, u32[]{:S(2)}) collective-permute-start(bf16[3,3,64,128]{3,2,1,0:T(8,128)(2,1)} %get-tuple-element.22), channel_id=1, source_target_pairs={{0,8},{8,16},{16,24},{24,32},{32,40},{40,48},{48,56},{56,64},{64,7... | collective-permute-start | bytes 442376 | tf_op jit(solution)/shard_map/ppermute | solution.py:437
  52.4 4.0 %collective-permute-start.5 = (bf16[3,3,64,128]{3,2,1,0:T(8,128)(2,1)}, bf16[3,3,64,128]{3,2,1,0:T(8,128)(2,1)}, u32[]{:S(2)}, u32[]{:S(2)}) collective-permute-start(bf16[3,3,64,128]{3,2,1,0:T(8,128)(2,1)} %get-tuple-element.23), channel_id=1, source_target_pairs={{8,0},{16,8},{24,16},{32,24},{40,32},{48,40},{56,48},{64,56},{72,6... | collective-permute-start | bytes 442376 | tf_op jit(solution)/shard_map/ppermute | solution.py:438
  56.5 0.0 copy-done.8
  56.5 0.9 copy.16
  57.4 0.1 copy.18.refs_12_
  57.5 0.0 collective-permute-done.7.refs_4_
  57.5 0.0 collective-permute-done.6.refs_3_
  57.5 0.2 collective-permute-done.4.refs_1_
  57.7 0.1 collective-permute-done.5.refs_2_
  57.8 0.0 all-to-all-done
  57.8 0.0 copy-start.1
  57.8 0.0 copy-start.2
  57.8 0.0 copy-start.4
  57.8 9.6 %section_two.1 = (f32[3,32,64,128]{3,2,1,0:T(8,128)}, f32[8,4,128]{2,1,0:T(4,128)S(1)}) custom-call(f32[3,32,64,128]{3,2,1,0:T(8,128)S(1)} %get-tuple-element.21.refs_0_, bf16[3,3,64,128]{3,2,1,0:T(8,128)(2,1)} %collective-permute-done.4.refs_1_, bf16[3,3,64,128]{3,2,1,0:T(8,128)(2,1)} %collective-permute-done.5.refs_2_, ...), custom_call_target="tpu_custom_call" | custom-call | flops 60000000 | bytes 12000000 | tf_op jit(solution)/shard_map/section_two/pallas_call | solution.py:319
  67.4 0.8 broadcast_in_dim.2
  68.2 22.6 %all-to-all-start.1 = ((bf16[256,4,128]{2,1,0:T(4,128)(2,1)}), bf16[256,4,128]{2,1,0:T(4,128)(2,1)S(1)}, u32[]{:S(2)}, u32[]{:S(2)}) async-start(bf16[256,4,128]{2,1,0:T(4,128)(2,1)} %bitcast.4), calls=%async_computation.1 | async-start | bytes 524288 | tf_op jit(solution)/shard_map/all_to_all | solution.py:489
  90.8 15.5 %all-to-all-done.1.amp_ref = bf16[256,4,128]{2,1,0:T(4,128)(2,1)S(1)} async-done(((bf16[256,4,128]{2,1,0:T(4,128)(2,1)}), bf16[256,4,128]{2,1,0:T(4,128)(2,1)S(1)}, u32[]{:S(2)}, u32[]{:S(2)}) %all-to-all-start.1) | async-done | bytes 262176 | tf_op jit(solution)/shard_map/all_to_all | solution.py:489
  106.3 0.0 copy-done.1
  106.3 0.0 copy-done.2
  106.3 0.0 copy-done.4
  106.3 4.8 %gram.1 = f32[2,8,32,1024]{3,2,1,0:T(8,128)} custom-call(f32[2,8,32,1024]{3,2,1,0:T(8,128)} %prior_ref.1, bf16[1024,256]{1,0:T(8,128)(2,1)} %bitcast.every_ref, bf16[32,256]{1,0:T(8,128)(2,1)S(1)} %copy-done.2, f32[1,256]{1,0:T(1,128)S(1)} %copy-done.4, bf16[256,4,128]{2,1,0:T(4,128)(2,1)S(1)} %all-to-all-done.1.amp_ref, s32[1]{0:T(128)} %bitcast.5.where_ref, ...), custom_call_target="tpu_custom_call" | custom-call | tf_op jit(solution)/shard_map/gram/pallas_call | solution.py:502
  (4 shorter events, 0.0 us)
Async XLA Ops:
  0.6 30.4 %copy-start = (bf16[384,256]{1,0:T(8,128)(2,1)S(1)}, bf16[384,256]{1,0:T(8,128)(2,1)}, u32[]{:S(2)}) copy-start(bf16[384,256]{1,0:T(8,128)(2,1)} %constant.19.clone.refs_9_) | copy-start | bytes 589828
  0.6 30.4 %copy-start.3 = (f32[3,3]{1,0:T(4,128)S(1)}, f32[3,3]{1,0:T(4,128)}, u32[]{:S(2)}) copy-start(f32[3,3]{1,0:T(4,128)} %refs_8_.3) | copy-start | bytes 112
  4.6 53.2 %all-to-all-start = ((bf16[32,32,256]{2,1,0:T(8,128)(2,1)}), bf16[32,32,256]{2,1,0:T(8,128)(2,1)}, u32[]{:S(2)}, u32[]{:S(2)}) async-start(bf16[32,32,256]{2,1,0:T(8,128)(2,1)} %get-tuple-element.25), calls=%async_computation | async-start | bytes 1048576 | tf_op jit(solution)/shard_map/all_to_all | solution.py:453
  20.9 35.6 %copy-start.8 = (s32[32]{0:T(128)S(1)}, s32[32]{0:T(128)}, u32[]{:S(2)}) copy-start(s32[32]{0:T(128)} %param.18) | copy-start | bytes 388
  20.9 8.9 %collective-permute-start = (bf16[3,3,64,128]{3,2,1,0:T(8,128)(2,1)}, bf16[3,3,64,128]{3,2,1,0:T(8,128)(2,1)S(1)}, u32[]{:S(2)}, u32[]{:S(2)}) collective-permute-start(bf16[3,3,64,128]{3,2,1,0:T(8,128)(2,1)} %get-tuple-element.18), channel_id=1, source_target_pairs={{0,8},{8,16},{16,24},{24,32},{32,40},{40,48},{48,56},{56,64},{64,7... | collective-permute-start | bytes 442376 | tf_op jit(solution)/shard_map/ppermute | solution.py:437
  22.5 7.9 %collective-permute-start.1 = (bf16[3,3,64,128]{3,2,1,0:T(8,128)(2,1)}, bf16[3,3,64,128]{3,2,1,0:T(8,128)(2,1)}, u32[]{:S(2)}, u32[]{:S(2)}) collective-permute-start(bf16[3,3,64,128]{3,2,1,0:T(8,128)(2,1)} %get-tuple-element.19), channel_id=1, source_target_pairs={{8,0},{16,8},{24,16},{32,24},{40,32},{48,40},{56,48},{64,56},{72,6... | collective-permute-start | bytes 442376 | tf_op jit(solution)/shard_map/ppermute | solution.py:438
  22.5 6.0 %collective-permute-start.3 = (bf16[3,2,64,128]{3,2,1,0:T(8,128)(2,1)}, bf16[3,2,64,128]{3,2,1,0:T(8,128)(2,1)S(1)}, u32[]{:S(2)}, u32[]{:S(2)}) collective-permute-start(bf16[3,2,64,128]{3,2,1,0:T(8,128)(2,1)} %get-tuple-element.20), channel_id=1, source_target_pairs={{1,0},{2,1},{3,2},{4,3},{5,4},{6,5},{7,6},{9,8},{10,9},{11,10},{12... | collective-permute-start | bytes 294920 | tf_op jit(solution)/shard_map/ppermute | solution.py:440
  23.8 5.9 %collective-permute-start.2 = (bf16[3,2,64,128]{3,2,1,0:T(8,128)(2,1)}, bf16[3,2,64,128]{3,2,1,0:T(8,128)(2,1)S(1)}, u32[]{:S(2)}, u32[]{:S(2)}) collective-permute-start(bf16[3,2,64,128]{3,2,1,0:T(8,128)(2,1)} %get-tuple-element.20), channel_id=1, source_target_pairs={{0,1},{1,2},{2,3},{3,4},{4,5},{5,6},{6,7},{8,9},{9,10},{10,11},{11... | collective-permute-start | bytes 294920 | tf_op jit(solution)/shard_map/ppermute | solution.py:439
  28.5 1.3 %copy-start.6 = (bf16[3,2,64,128]{3,2,1,0:T(8,128)(2,1)}, bf16[3,2,64,128]{3,2,1,0:T(8,128)(2,1)S(1)}, u32[]{:S(2)}) copy-start(bf16[3,2,64,128]{3,2,1,0:T(8,128)(2,1)S(1)} %collective-permute-done.3.refs_4_) | copy-start | bytes 294916
  29.7 0.6 copy-start.7
  30.3 0.7 copy-start.5
  42.8 14.7 %collective-permute-start.7 = (bf16[3,2,64,128]{3,2,1,0:T(8,128)(2,1)}, bf16[3,2,64,128]{3,2,1,0:T(8,128)(2,1)}, u32[]{:S(2)}, u32[]{:S(2)}) collective-permute-start(bf16[3,2,64,128]{3,2,1,0:T(8,128)(2,1)} %get-tuple-element.24), channel_id=1, source_target_pairs={{1,0},{2,1},{3,2},{4,3},{5,4},{6,5},{7,6},{9,8},{10,9},{11,10},{12... | collective-permute-start | bytes 294920 | tf_op jit(solution)/shard_map/ppermute | solution.py:440
  44.1 13.4 %collective-permute-start.6 = (bf16[3,2,64,128]{3,2,1,0:T(8,128)(2,1)}, bf16[3,2,64,128]{3,2,1,0:T(8,128)(2,1)}, u32[]{:S(2)}, u32[]{:S(2)}) collective-permute-start(bf16[3,2,64,128]{3,2,1,0:T(8,128)(2,1)} %get-tuple-element.24), channel_id=1, source_target_pairs={{0,1},{1,2},{2,3},{3,4},{4,5},{5,6},{6,7},{8,9},{9,10},{10,11},{11... | collective-permute-start | bytes 294920 | tf_op jit(solution)/shard_map/ppermute | solution.py:439
  49.3 8.3 %collective-permute-start.4 = (bf16[3,3,64,128]{3,2,1,0:T(8,128)(2,1)}, bf16[3,3,64,128]{3,2,1,0:T(8,128)(2,1)}, u32[]{:S(2)}, u32[]{:S(2)}) collective-permute-start(bf16[3,3,64,128]{3,2,1,0:T(8,128)(2,1)} %get-tuple-element.22), channel_id=1, source_target_pairs={{0,8},{8,16},{16,24},{24,32},{32,40},{40,48},{48,56},{56,64},{64,7... | collective-permute-start | bytes 442376 | tf_op jit(solution)/shard_map/ppermute | solution.py:437
  52.4 5.4 %collective-permute-start.5 = (bf16[3,3,64,128]{3,2,1,0:T(8,128)(2,1)}, bf16[3,3,64,128]{3,2,1,0:T(8,128)(2,1)}, u32[]{:S(2)}, u32[]{:S(2)}) collective-permute-start(bf16[3,3,64,128]{3,2,1,0:T(8,128)(2,1)} %get-tuple-element.23), channel_id=1, source_target_pairs={{8,0},{16,8},{24,16},{32,24},{40,32},{48,40},{56,48},{64,56},{72,6... | collective-permute-start | bytes 442376 | tf_op jit(solution)/shard_map/ppermute | solution.py:438
  57.8 48.5 %copy-start.1 = (bf16[2,128,128]{2,1,0:T(8,128)(2,1)S(1)}, bf16[2,128,128]{2,1,0:T(8,128)(2,1)}, u32[]{:S(2)}) copy-start(bf16[2,128,128]{2,1,0:T(8,128)(2,1)} %constant.21.clone.rep_ref) | copy-start | bytes 196612
  57.8 48.5 %copy-start.2 = (bf16[32,256]{1,0:T(8,128)(2,1)S(1)}, bf16[32,256]{1,0:T(8,128)(2,1)}, u32[]{:S(2)}) copy-start(bf16[32,256]{1,0:T(8,128)(2,1)} %get-tuple-element.32.own_ref) | copy-start | bytes 49156
  57.8 48.5 %copy-start.4 = (f32[1,256]{1,0:T(1,128)S(1)}, f32[1,256]{1,0:T(1,128)}, u32[]{:S(2)}) copy-start(f32[1,256]{1,0:T(1,128)} %constant.20.clone.ramp_ref) | copy-start | bytes 3076
  68.2 38.2 %all-to-all-start.1 = ((bf16[256,4,128]{2,1,0:T(4,128)(2,1)}), bf16[256,4,128]{2,1,0:T(4,128)(2,1)S(1)}, u32[]{:S(2)}, u32[]{:S(2)}) async-start(bf16[256,4,128]{2,1,0:T(4,128)(2,1)} %bitcast.4), calls=%async_computation.1 | async-start | bytes 524288 | tf_op jit(solution)/shard_map/all_to_all | solution.py:489

commit v4 on v3

--- a/solution.py
+++ b/solution.py
@@ -78,27 +78,34 @@
     high_ref[0] = flow_ref[0, stations - 3 : stations].astype(BF16)
 
 
-def section_kernel(*refs, second):
-    take = list(refs).pop
+def section_kernel(*refs, second, profile, carried, quantities):
     refs = list(refs)
     take = refs.pop
-    state_hbm = take(0)
+    state_ref = take(0)
     halo_hbm = [take(0) for _ in range(4)]
     vs_hbm, vc_hbm, nu_hbm = (take(0) for _ in range(3))
     mix, table_ref = take(0), take(0)
     if second:
-        flow_hbm, te_ref, band_ref = (take(0) for _ in range(3))
+        flow_hbm = take(0)
+    if profile:
+        te_ref, band_ref = take(0), take(0)
+    if carried:
+        take(0)
     out_hbm = take(0)
-    if second:
+    if profile:
         amp_out = take(0)
-    else:
+    if not second:
         low_out, high_out, cells_out = (take(0) for _ in range(3))
     wide, result, chord_a, chord_b, halos, cells, vs, vc, nu, in_sem, out_sem = (take(0) for _ in range(11))
     if second:
-        before, before_sem, columns, amps = (take(0) for _ in range(4))
+        before, before_sem = take(0), take(0)
+    if profile:
+        columns, amps = take(0), take(0)
     span_low, span_high, chord_low, chord_high, halo_sem = (take(0) for _ in range(5))
 
-    count, stations, normal = wide.shape[0], vs.shape[0], vs.shape[1]
+    count, stations, normal = len(quantities), vs.shape[0], vs.shape[1]
+    everything = range(state_ref.shape[0])
+    some = pl.ds(quantities[0], count)
     chunks, pairs = 8, stations // 2
     per = stations // chunks
 
@@ -106,7 +113,7 @@
         rows = pl.ds(per * c, per)
         todo = [
             pltpu.make_async_copy(
-                state_hbm.at[:, rows],
+                state_ref.at[some, rows],
                 wide.at[:, pl.ds(3 + per * c, per), pl.ds(8, normal), :],
                 in_sem.at[0, c],
             ),
@@ -116,7 +123,7 @@
         ]
         if second:
             todo.append(
-                pltpu.make_async_copy(flow_hbm.at[:, rows], before.at[:, rows], before_sem.at[c])
+                pltpu.make_async_copy(flow_hbm.at[some, rows], before.at[:, rows], before_sem.at[c])
             )
         return todo
 
@@ -135,19 +142,19 @@
     nothing = jnp.zeros((count, stations, 8, LANES), F32)
     wide[:, 3 : 3 + stations, 0:8, :] = nothing
     wide[:, 3 : 3 + stations, 8 + normal : 16 + normal, :] = nothing
-    if second:
+    if profile:
         columns[...] = jnp.zeros(columns.shape, F32)
     for copy in halo_copies:
         copy.wait()
-    wide[:, 0:3, 8 : 8 + normal, :] = span_low[...].astype(F32)
-    wide[:, 3 + stations : 6 + stations, 8 : 8 + normal, :] = span_high[...].astype(F32)
+    wide[:, 0:3, 8 : 8 + normal, :] = span_low[some].astype(F32)
+    wide[:, 3 + stations : 6 + stations, 8 : 8 + normal, :] = span_high[some].astype(F32)
     place = lax.rem(lax.broadcasted_iota(jnp.int32, (normal, LANES), 1), 8)
-    for q in range(count):
+    for local, q in enumerate(quantities):
         for half in range(stations // 16):
             near = jnp.where(
                 place < 3, chord_low[q, half].astype(F32), chord_high[q, half].astype(F32)
             )
-            halos[q, half] = jnp.where(place < 6, near, 0.0)
+            halos[local, half] = jnp.where(place < 6, near, 0.0)
 
     def matmuls(p, chord):
         half = lax.div(p, 8)
@@ -166,8 +173,8 @@
 
     scale = 0.5 if second else 1.0
     couple = [
-        [scale * ((1.0 if q == e else 0.0) + TIME_STEP * mix[q, e]) for e in range(count)]
-        for q in range(count)
+        [scale * ((1.0 if q == e else 0.0) + TIME_STEP * mix[q, e]) for e in everything]
+        for q in quantities
     ]
     ROWS = 16
     lane = lax.broadcasted_iota(jnp.int32, (ROWS, LANES), 1)
@@ -187,14 +194,16 @@
                 b = vc[s, rows, :].astype(F32) * (-scale * TIME_STEP / 60)
                 g = nu[s, rows, :].astype(F32) * (scale * TIME_STEP / 180)
                 centre = [
-                    wide[e, 3 + s, 8 + ROWS * tile : 8 + ROWS * tile + ROWS, :]
-                    for e in range(count)
+                    wide[e - quantities[0], 3 + s, 8 + ROWS * tile : 8 + ROWS * tile + ROWS, :]
+                    if e in quantities
+                    else state_ref[e, s, rows, :]
+                    for e in everything
                 ]
-                for q in range(count):
+                for local, q in enumerate(quantities):
 
                     def at(ds, dn):
                         low = 8 + ROWS * tile + dn
-                        return wide[q, 3 + s + ds, low : low + ROWS, :]
+                        return wide[local, 3 + s + ds, low : low + ROWS, :]
 
                     first = None
                     both = None
@@ -207,18 +216,18 @@
                         total = total * float(SECOND[reach - 1])
                         first = diff if first is None else first + diff
                         both = total if both is None else both + total
-                    start = (2 * q + half) * normal + ROWS * tile
+                    start = (2 * local + half) * normal + ROWS * tile
                     crow = slice(start, start + ROWS)
                     chord_first = chord[crow, 0:LANES]
                     chord_second = chord[crow, LANES : 2 * LANES]
                     both = both + (centre[q] * float(2 * CENTRE) + chord_second)
                     value = a * first + b * chord_first + g * both
-                    for e in range(count):
-                        value = value + couple[q][e] * centre[e]
+                    for e in everything:
+                        value = value + couple[local][e] * centre[e]
                     if second:
-                        value = value + 0.5 * before[q, s, rows, :]
-                    result[q, s, rows, :] = value
-                    if second and q == 0:
+                        value = value + 0.5 * before[local, s, rows, :]
+                    result[local, s, rows, :] = value
+                    if profile and q == 0:
                         hit = jnp.where(lane == te_ref[s], value, 0.0)
                         column = jnp.sum(hit, axis=1, keepdims=True)
                         columns[rows, :] += jnp.where(lane == s, column, 0.0)
@@ -233,7 +242,7 @@
 
     def out_copy(p):
         two = pl.ds(2 * p, 2)
-        return pltpu.make_async_copy(result.at[:, two], out_hbm.at[:, two], out_sem.at[p])
+        return pltpu.make_async_copy(result.at[:, two], out_hbm.at[some, two], out_sem.at[p])
 
     def arrive(c):
         for copy in copies(c):
@@ -246,20 +255,20 @@
             arrive(c + 1)
         lax.fori_loop(c * pairs // chunks // 2, (c + 1) * pairs // chunks // 2, body, 0)
 
-    if second:
+    if profile:
         amp = fine_dot(columns[...].T, band_ref[...])
         amps[...] = amp[:stations].astype(BF16).astype(F32)
         lane4 = lax.div(lax.broadcasted_iota(jnp.int32, (4, LANES), 1), 16)
         pieces = [jnp.zeros((4, LANES), F32) for _ in range(8)]
         for u in range(8):
-            some = amps[pl.ds(u, 4, stride=8), :]
+            taken = amps[pl.ds(u, 4, stride=8), :]
             for j in range(8):
                 shift = (16 * (u - j)) % LANES
-                moved = pltpu.roll(some, shift, 1) if shift else some
+                moved = pltpu.roll(taken, shift, 1) if shift else taken
                 pieces[j] = jnp.where(lane4 == u, moved, pieces[j])
         for j in range(8):
             amp_out[j] = pieces[j]
-    else:
+    if not second:
         cells_out[...] = cells[...].astype(BF16)
         low_out[...] = result[:, 0:3].astype(BF16)
         high_out[...] = result[:, stations - 3 : stations].astype(BF16)
@@ -271,35 +280,58 @@
     lax.fori_loop(0, pairs, drain, 0)
 
 
-def section(state, halos, fields, mixing, table, flow=None, te_local=None, band_table=None):
-    count, stations, normal, _ = state.shape
-    second = flow is not None
+def section(
+    state,
+    halos,
+    fields,
+    mixing,
+    table,
+    quantities=(0, 1, 2),
+    flow=None,
+    te_local=None,
+    band_table=None,
+    onto=None,
+):
+    total, stations, normal, _ = state.shape
+    count = len(quantities)
+    second, profile, carried = flow is not None, te_local is not None, onto is not None
     pairs = stations // 2
     hbm = pl.BlockSpec(memory_space=pltpu.HBM)
     vmem = pl.BlockSpec(memory_space=pltpu.VMEM)
     smem = pl.BlockSpec(memory_space=pltpu.SMEM)
     args = [state, *halos, *fields, mixing, table]
-    specs = [hbm] * 8 + [smem, vmem]
+    specs = [vmem if second else hbm] + [hbm] * 7 + [smem, vmem]
     shapes = [jax.ShapeDtypeStruct(state.shape, F32)]
+    aliases = {}
     if second:
-        args += [flow, te_local, band_table]
-        specs += [hbm, smem, vmem]
+        args.append(flow)
+        specs.append(hbm)
+    if profile:
+        args += [te_local, band_table]
+        specs += [smem, vmem]
         shapes.append(jax.ShapeDtypeStruct((8, 4, LANES), F32))
-    else:
+    if carried:
+        aliases = {len(args): 0}
+        args.append(onto)
+        specs.append(hbm)
+    if not second:
         shapes += [jax.ShapeDtypeStruct((count, 3, normal, LANES), BF16)] * 2
         shapes.append(jax.ShapeDtypeStruct((count, stations // 16, normal, LANES), BF16))
-    field = pltpu.VMEM((stations, normal, LANES), BF16)
     args = [
-        pltpu.with_memory_space_constraint(x, pltpu.HBM) if spec is hbm and not (second and x is state) else x
+        pltpu.with_memory_space_constraint(x, pltpu.HBM) if spec is hbm else x
         for x, spec in zip(args, specs)
     ]
+    field = pltpu.VMEM((stations, normal, LANES), BF16)
+    block = pltpu.VMEM((count, stations, normal, LANES), F32)
+    differences = pltpu.VMEM((count * 2 * normal, 2 * LANES), F32)
+    edge = pltpu.VMEM((count, stations // 16, normal, LANES), F32)
     scratch = [
         pltpu.VMEM((count, stations + 6, normal + 16, LANES), F32),
-        pltpu.VMEM((count, stations, normal, LANES), F32),
-        pltpu.VMEM((count * 2 * normal, 2 * LANES), F32),
-        pltpu.VMEM((count * 2 * normal, 2 * LANES), F32),
-        pltpu.VMEM((count, stations // 16, normal, LANES), F32),
-        pltpu.VMEM((count, stations // 16, normal, LANES), F32),
+        block,
+        differences,
+        differences,
+        edge,
+        edge,
         field,
         field,
         field,
@@ -307,35 +339,45 @@
         pltpu.SemaphoreType.DMA((pairs,)),
     ]
     if second:
-        scratch += [
-            pltpu.VMEM((count, stations, normal, LANES), F32),
-            pltpu.SemaphoreType.DMA((8,)),
-            pltpu.VMEM((normal, LANES), F32),
-            pltpu.VMEM((stations, LANES), F32),
-        ]
-    scratch += [pltpu.VMEM((count, 3, normal, LANES), BF16)] * 2
-    scratch += [pltpu.VMEM((count, stations // 16, normal, LANES), BF16)] * 2
+        scratch += [block, pltpu.SemaphoreType.DMA((8,))]
+    if profile:
+        scratch += [pltpu.VMEM((normal, LANES), F32), pltpu.VMEM((stations, LANES), F32)]
+    scratch += [pltpu.VMEM((total, 3, normal, LANES), BF16)] * 2
+    scratch += [pltpu.VMEM((total, stations // 16, normal, LANES), BF16)] * 2
     scratch.append(pltpu.SemaphoreType.DMA((4,)))
     return pl.pallas_call(
-        functools.partial(section_kernel, second=second),
+        functools.partial(
+            section_kernel,
+            second=second,
+            profile=profile,
+            carried=carried,
+            quantities=quantities,
+        ),
         out_shape=tuple(shapes),
         in_specs=specs,
         out_specs=tuple([hbm] + [vmem] * (len(shapes) - 1)),
         scratch_shapes=scratch,
+        input_output_aliases=aliases,
         compiler_params=pltpu.CompilerParams(vmem_limit_bytes=20 << 20),
         cost_estimate=pl.CostEstimate(
-            flops=60000000, transcendentals=0, bytes_accessed=12000000
+            flops=20000000 * count, transcendentals=0, bytes_accessed=8000000 * count
         ),
-        name="section_two" if second else "section_one",
+        name=("section_two_" if second else "section_one_") + "".join(map(str, quantities)),
     )(*args)
 
 
 def spectra_kernel(spectra_ref, wanted_ref, own_ref, send_ref):
     stations, bands, slots = spectra_ref.shape
-    width = wanted_ref.shape[1]
+    width = own_ref.shape[1]
+    segs = wanted_ref.shape[0]
+    lanes = lax.broadcasted_iota(jnp.int32, (1, width), 1)
+    wanted = jnp.zeros((1, width), jnp.int32)
+    for k in range(segs):
+        wanted = jnp.where(lax.rem(lanes, segs) == k, wanted_ref[k], wanted)
+    wanted = wanted + (slots // 2) * lax.rem(lax.div(lanes, segs), 2)
     rows = spectra_ref[...].astype(F32).reshape(stations * bands, slots).astype(BF16)
     slot = lax.broadcasted_iota(jnp.int32, (slots, width), 0)
-    choose = jnp.where(slot == wanted_ref[...], 1.0, 0.0).astype(BF16)
+    choose = jnp.where(slot == wanted, 1.0, 0.0).astype(BF16)
     got = jnp.dot(rows, choose, preferred_element_type=F32)
     row_band = lax.rem(lax.broadcasted_iota(jnp.int32, got.shape, 0), bands)
     lane_band = lax.div(lax.broadcasted_iota(jnp.int32, got.shape, 1), width // bands)
@@ -346,11 +388,37 @@
         send_ref[d] = packed
 
 
-def gram_kernel(prior_ref, every_ref, own_ref, ramp_ref, amp_ref, where_ref, rep_ref, out_ref, left):
-    step = pl.program_id(0)
+def stored_kernel(prior_ref, every_ref, own_ref, ramp_ref, out_ref, left):
     bands, stations, tile = prior_ref.shape[1:]
     width = own_ref.shape[1]
-    sources = amp_ref.shape[0] // (tile // stations) // pl.num_programs(0)
+
+    @pl.when(pl.program_id(0) == 0)
+    def _():
+        own = own_ref[...].astype(F32)
+        lane = lax.broadcasted_iota(jnp.int32, own.shape, 1)
+        real = lax.rem(lane, 32) < 16
+        turned = jnp.where(real, pltpu.roll(own, width - 16, 1), -pltpu.roll(own, 16, 1))
+        for c, part in enumerate((own, turned)):
+            part = part * ramp_ref[...]
+            high = part.astype(BF16).astype(F32)
+            low = part - high
+            for b in range(bands):
+                at = (c * bands + b) * stations
+                keep = lax.div(lane, 32) == b
+                rows = slice(at, at + stations)
+                left[rows, 0:width] = jnp.where(keep, high, 0.0).astype(BF16)
+                left[rows, width : 2 * width] = jnp.where(keep, low, 0.0).astype(BF16)
+
+    stored = every_ref[...]
+    got = nt_dot(left[...], jnp.concatenate([stored, stored], axis=1))
+    out_ref[...] = DECAY * prior_ref[...] + got.reshape(2, bands, stations, tile)
+
+
+def amplitude_kernel(known_ref, amp_ref, where_ref, rep_ref, out_ref, left):
+    step = pl.program_id(0)
+    bands, stations, tile = known_ref.shape[1:]
+    blocks = tile // stations
+    sources = amp_ref.shape[0] // blocks // pl.num_programs(0)
 
     def spread(source):
         whole = amp_ref[pl.ds(source * sources, sources)].astype(F32)
@@ -367,35 +435,17 @@
 
     @pl.when(step == 0)
     def _():
-        own = own_ref[...].astype(F32)
-        ramp = ramp_ref[...]
-        lane = lax.broadcasted_iota(jnp.int32, own.shape, 1)
-        real = lax.rem(lane, 32) < 16
-        turned = jnp.where(
-            real, pltpu.roll(own, width - 16, 1), -pltpu.roll(own, 16, 1)
-        )
         mine = spread(where_ref[0])
-        place = lax.broadcasted_iota(jnp.int32, (stations, LANES), 1)
-        for c, part in enumerate((own, turned)):
-            part = part * ramp
-            high = part.astype(BF16).astype(F32)
-            low = part - high
+        place = lax.rem(lax.broadcasted_iota(jnp.int32, (stations, LANES), 1), 8)
+        for c in range(2):
             amp = jnp.dot(mine, rep_ref[c], preferred_element_type=F32)
             for b in range(bands):
                 at = (c * bands + b) * stations
-                keep = lax.div(lane, 32) == b
-                rows = slice(at, at + stations)
-                left[rows, 0:width] = jnp.where(keep, high, 0.0).astype(BF16)
-                left[rows, width : 2 * width] = jnp.where(keep, low, 0.0).astype(BF16)
-                left[rows, 2 * width : 2 * width + LANES] = jnp.where(
-                    lax.rem(place, 8) == b, amp, 0.0
-                ).astype(BF16)
-
-    blocks = tile // stations
+                left[at : at + stations, :] = jnp.where(place == b, amp, 0.0).astype(BF16)
+
     right = jnp.concatenate([spread(step * blocks + i) for i in range(blocks)])
-    stored = every_ref[...]
-    got = nt_dot(left[...], jnp.concatenate([stored, stored, right], axis=1))
-    out_ref[...] = DECAY * prior_ref[...] + got.reshape(2, bands, stations, tile)
+    got = nt_dot(left[...], right)
+    out_ref[...] = known_ref[...] + got.reshape(2, bands, stations, tile)
 
 
 def amplitude_tables():
@@ -440,18 +490,6 @@
             lax.ppermute(edge, "chord", backward),
         )
 
-    width = bands * 2 * segs
-    wanted = jnp.tile(jnp.concatenate([offsets, offsets + slots]), bands)[None]
-    packed, send = pl.pallas_call(
-        spectra_kernel,
-        out_shape=(
-            jax.ShapeDtypeStruct((stations, width), BF16),
-            jax.ShapeDtypeStruct((span_n, stations, width), BF16),
-        ),
-        name="spectra",
-    )(spectra, wanted)
-    every = lax.all_to_all(send, "span", 0, 0, tiled=True).reshape(span_n * stations, width)
-
     edge_shape = jax.ShapeDtypeStruct((count, stations // 16, normal, LANES), BF16)
     ends_shape = jax.ShapeDtypeStruct((count, 3, normal, LANES), BF16)
 
@@ -468,9 +506,24 @@
     )(flow_state)
     halos = exchange(low, high, edge)
 
+    width = bands * 2 * segs
+    _, stored = lax.optimization_barrier((edge, spectra))
+    packed, send = pl.pallas_call(
+        spectra_kernel,
+        out_shape=(
+            jax.ShapeDtypeStruct((stations, width), BF16),
+            jax.ShapeDtypeStruct((span_n, stations, width), BF16),
+        ),
+        in_specs=[
+            pl.BlockSpec(memory_space=pltpu.VMEM),
+            pl.BlockSpec(memory_space=pltpu.SMEM),
+        ],
+        name="spectra",
+    )(stored, offsets)
+    every = lax.all_to_all(send, "span", 0, 0, tiled=True).reshape(span_n * stations, width)
+
     (section_one, low, high, edge) = section(flow_state, halos, fields, mixing, table)
     halos = exchange(low, high, edge)
-    halos, every = lax.optimization_barrier((halos, every))
 
     te_local = te_index - chord_pos * cells
     band_table = band_response.reshape(normal, 2, chord_n, bands).transpose(0, 2, 1, 3)
@@ -481,6 +534,7 @@
         fields,
         mixing,
         table,
+        (0,),
         flow=flow_state,
         te_local=te_local,
         band_table=band_table,
@@ -489,38 +543,61 @@
     amps = lax.all_to_all(
         amps.reshape((span_n * chord_n,) + amps.shape[2:]), ("span", "chord"), 0, 0, tiled=True
     )
+    (flow_next,) = section(
+        section_one, halos, fields, mixing, table, (1, 2), flow=flow_state, onto=flow_next
+    )
 
     ramp = np.tile((np.arange(segs, dtype=np.float32) + 1) / segs, 2 * bands)[None]
     tiles = 4
     tile = span_n * stations // tiles
+    gram_shape = jax.ShapeDtypeStruct(prior_gram_blocks.shape, F32)
     gram_block = pl.BlockSpec((2, bands, stations, tile), lambda t: (0, 0, 0, t))
+    params = pltpu.CompilerParams(vmem_limit_bytes=24 << 20)
 
     def whole(x):
         return pl.BlockSpec(x.shape, lambda t: (0,) * x.ndim)
 
-    reps = amplitude_tables()
-    gram_next = pl.pallas_call(
-        gram_kernel,
+    known = pl.pallas_call(
+        stored_kernel,
         grid=(tiles,),
-        out_shape=jax.ShapeDtypeStruct(prior_gram_blocks.shape, F32),
+        out_shape=gram_shape,
         in_specs=[
             gram_block,
             pl.BlockSpec((tile, width), lambda t: (t, 0)),
             whole(packed),
             whole(ramp),
+        ],
+        out_specs=gram_block,
+        scratch_shapes=[pltpu.VMEM((2 * bands * stations, 2 * width), BF16)],
+        compiler_params=params,
+        cost_estimate=pl.CostEstimate(
+            flops=30000000, transcendentals=0, bytes_accessed=12000000
+        ),
+        name="gram_stored",
+    )(
+        pltpu.with_memory_space_constraint(prior_gram_blocks, pltpu.HBM),
+        pltpu.with_memory_space_constraint(every, pltpu.HBM),
+        packed,
+        ramp,
+    )
+    known, flow_next = lax.optimization_barrier((known, flow_next))
+    reps = amplitude_tables()
+    gram_next = pl.pallas_call(
+        amplitude_kernel,
+        grid=(tiles,),
+        out_shape=gram_shape,
+        in_specs=[
+            gram_block,
             whole(amps),
             pl.BlockSpec(memory_space=pltpu.SMEM),
             whole(reps),
         ],
         out_specs=gram_block,
-        scratch_shapes=[pltpu.VMEM((2 * bands * stations, 2 * width + LANES), BF16)],
-        compiler_params=pltpu.CompilerParams(vmem_limit_bytes=32 << 20),
-        name="gram",
+        scratch_shapes=[pltpu.VMEM((2 * bands * stations, LANES), BF16)],
+        compiler_params=params,
+        name="gram_amplitudes",
     )(
-        pltpu.with_memory_space_constraint(prior_gram_blocks, pltpu.HBM),
-        pltpu.with_memory_space_constraint(every, pltpu.HBM),
-        packed,
-        ramp,
+        known,
         amps,
         span_pos.reshape(1),
         reps,

time: 112 us -> 108 us (0.964)
  waiting for transfers between devices: 17.8 us -> 8.24 us
  Pallas kernels: 31.5 us -> 38.1 us
  local copies, waits for them, and re-layouts: 3.7 us -> 6.03 us
  starting transfers between devices: 55.9 us -> 53.9 us
  other arithmetic: 1.43 us -> 0.01 us
    all_to_all x1, waiting for transfers between devices: 15.5 us -> 3.55 us  [shards(): lax.all_to_all(amps.reshape((span_n * chord_n,) + amps.shape[2:]), ('span...]
    pallas_call x3 -> x5, Pallas kernels: 26 us -> 32.6 us  [the longest x3 25.6 us: section(): pl.pallas_call(functools.partial(section_kernel, second=second, profile=p...]
    ppermute x2, waiting for transfers between devices: 0.68 us -> 4.04 us  [exchange(): lax.ppermute(edge, 'chord', backward)]
    ppermute x2, starting transfers between devices: 9.29 us -> 7.04 us  [exchange(): lax.ppermute(edge, 'chord', forward)]
    ppermute x2, starting transfers between devices: 4.05 us -> 6.07 us  [exchange(): lax.ppermute(low, 'span', down)]
    all_to_all x1, starting transfers between devices: 22.6 us -> 20.7 us  [shards(): lax.all_to_all(amps.reshape((span_n * chord_n,) + amps.shape[2:]), ('span...]
    transpose x1, local copies, waits for them, and re-layouts: 0.01 us -> 1.48 us  [shards(): band_response.reshape(normal, 2, chord_n, bands).transpose(0, 2, 1, 3)]
  transfers between devices with their start and end apart: 10 -> 10, of which waited for: 5 -> 3; matrix products, arithmetic and copies ran while one was open for 1% -> 4% of each run, Pallas kernels for 14% -> 27%
where the time goes in v4:
time: 108 us; the launch traced here: 107 us
  starting transfers between devices  53.9 us (50%)
  Pallas kernels  38.1 us (35%)
  waiting for transfers between devices  8.24 us (8%)
  local copies, waits for them, and re-layouts  6.03 us (6%)
    pallas_call x3, Pallas kernels, section(): pl.pallas_call(functools.partial(section_kernel, second=second, profile=p...  25.6 us
    all_to_all x1, starting transfers between devices, shards(): lax.all_to_all(amps.reshape((span_n * chord_n,) + amps.shape[2:]), ('span...  20.7 us
    all_to_all x1, starting transfers between devices, shards(): lax.all_to_all(send, 'span', 0, 0, tiled=True)  12.8 us
    ppermute x2, starting transfers between devices, exchange(): lax.ppermute(edge, 'chord', forward)  7.04 us
    ppermute x2, starting transfers between devices, exchange(): lax.ppermute(low, 'span', down)  6.07 us
    ppermute x2, starting transfers between devices, exchange(): lax.ppermute(high, 'span', up)  4.84 us
    ppermute x2, waiting for transfers between devices, exchange(): lax.ppermute(edge, 'chord', backward)  4.04 us
    pallas_call x1, Pallas kernels, shards(): pl.pallas_call(edges_kernel, grid=(count,), out_shape=(edge_shape, ends_s...  3.62 us
  transfers between devices with their start and end apart: 10, of which 3 were waited for; matrix products, arithmetic and copies ran while one was open for 4% of the time, Pallas kernels for 27%

profile of v4, /device:TPU:1, one launch (start us, length us, event | category | flops | bytes accessed | tf_op | source)
XLA Modules:
  0.0 107.2 jit_solution(3947603251885007654)
XLA Ops:
  0.6 0.0 copy-start
  0.6 0.0 copy-start.2
  0.7 3.6 %edges.1 = (bf16[3,2,64,128]{3,2,1,0:T(8,128)(2,1)}, bf16[3,3,64,128]{3,2,1,0:T(8,128)(2,1)}, bf16[3,3,64,128]{3,2,1,0:T(8,128)(2,1)}) custom-call(f32[3,32,64,128]{3,2,1,0:T(8,128)} %refs_10_.3), custom_call_target="tpu_custom_call" | custom-call | tf_op jit(solution)/shard_map/edges/pallas_call | solution.py:499
  4.3 1.9 %spectra.1 = (bf16[32,256]{1,0:T(8,128)(2,1)}, bf16[32,32,256]{2,1,0:T(8,128)(2,1)}) custom-call(bf16[32,8,128]{2,1,0:T(8,128)(2,1)} %spectra_ref, s32[16]{0:T(128)} %wanted_ref.1), custom_call_target="tpu_custom_call" | custom-call | tf_op jit(solution)/shard_map/spectra/pallas_call | solution.py:511
  6.2 0.0 copy-start.8
  6.2 12.8 %all-to-all-start = ((bf16[32,32,256]{2,1,0:T(8,128)(2,1)}), bf16[32,32,256]{2,1,0:T(8,128)(2,1)}, u32[]{:S(2)}, u32[]{:S(2)}) async-start(bf16[32,32,256]{2,1,0:T(8,128)(2,1)} %get-tuple-element.18), calls=%async_computation | async-start | bytes 1048576 | tf_op jit(solution)/shard_map/all_to_all | solution.py:523
  19.0 1.7 %collective-permute-start = (bf16[3,3,64,128]{3,2,1,0:T(8,128)(2,1)}, bf16[3,3,64,128]{3,2,1,0:T(8,128)(2,1)S(1)}, u32[]{:S(2)}, u32[]{:S(2)}) collective-permute-start(bf16[3,3,64,128]{3,2,1,0:T(8,128)(2,1)} %get-tuple-element.20), channel_id=1, source_target_pairs={{0,8},{8,16},{16,24},{24,32},{32,40},{40,48},{48,56},{56,64},{64,7... | collective-permute-start | bytes 442376 | tf_op jit(solution)/shard_map/ppermute | solution.py:487
  20.7 0.0 collective-permute-start.1
  20.7 3.2 %collective-permute-start.2 = (bf16[3,2,64,128]{3,2,1,0:T(8,128)(2,1)}, bf16[3,2,64,128]{3,2,1,0:T(8,128)(2,1)S(1)}, u32[]{:S(2)}, u32[]{:S(2)}) collective-permute-start(bf16[3,2,64,128]{3,2,1,0:T(8,128)(2,1)} %get-tuple-element.16), channel_id=1, source_target_pairs={{0,1},{1,2},{2,3},{3,4},{4,5},{5,6},{6,7},{8,9},{9,10},{10,11},{11... | collective-permute-start | bytes 294920 | tf_op jit(solution)/shard_map/ppermute | solution.py:489
  23.9 1.3 %collective-permute-start.3 = (bf16[3,2,64,128]{3,2,1,0:T(8,128)(2,1)}, bf16[3,2,64,128]{3,2,1,0:T(8,128)(2,1)S(1)}, u32[]{:S(2)}, u32[]{:S(2)}) collective-permute-start(bf16[3,2,64,128]{3,2,1,0:T(8,128)(2,1)} %get-tuple-element.16), channel_id=1, source_target_pairs={{1,0},{2,1},{3,2},{4,3},{5,4},{6,5},{7,6},{9,8},{10,9},{11,10},{12... | collective-permute-start | bytes 294920 | tf_op jit(solution)/shard_map/ppermute | solution.py:490
  25.2 0.6 collective-permute-done.2.refs_3_
  25.8 0.0 copy-start.6
  25.8 4.0 %collective-permute-done.3.refs_4_ = bf16[3,2,64,128]{3,2,1,0:T(8,128)(2,1)S(1)} collective-permute-done((bf16[3,2,64,128]{3,2,1,0:T(8,128)(2,1)}, bf16[3,2,64,128]{3,2,1,0:T(8,128)(2,1)S(1)}, u32[]{:S(2)}, u32[]{:S(2)}) %collective-permute-start.3) | collective-permute-done | bytes 98336 | tf_op jit(solution)/shard_map/ppermute | solution.py:490
  29.9 0.0 copy-start.7
  29.9 0.0 collective-permute-done.refs_1_
  29.9 0.0 copy-done.6
  29.9 0.6 copy-done.7
  30.5 0.0 copy-start.5
  30.5 0.7 copy-done.5
  31.2 0.0 collective-permute-done.1.refs_2_
  31.2 0.0 copy-done
  31.2 0.0 copy-done.2
  31.2 11.7 %section_one_012.1 = (f32[3,32,64,128]{3,2,1,0:T(8,128)S(1)}, bf16[3,3,64,128]{3,2,1,0:T(8,128)(2,1)S(1)}, bf16[3,3,64,128]{3,2,1,0:T(8,128)(2,1)}, bf16[3,2,64,128]{3,2,1,0:T(8,128)(2,1)}) custom-call(f32[3,32,64,128]{3,2,1,0:T(8,128)} %refs_10_.3, bf16[3,3,64,128]{3,2,1,0:T(8,128)(2,1)} %copy-done.5, ...), custom_call_target="tpu_custom_call" | custom-call | flops 60000000 | bytes 24000000 | tf_op jit(solution)/shard_map/section_one_012/pallas_call | solution.py:348
  42.9 3.8 %collective-permute-start.6 = (bf16[3,2,64,128]{3,2,1,0:T(8,128)(2,1)}, bf16[3,2,64,128]{3,2,1,0:T(8,128)(2,1)}, u32[]{:S(2)}, u32[]{:S(2)}) collective-permute-start(bf16[3,2,64,128]{3,2,1,0:T(8,128)(2,1)} %get-tuple-element.25), channel_id=1, source_target_pairs={{0,1},{1,2},{2,3},{3,4},{4,5},{5,6},{6,7},{8,9},{9,10},{10,11},{11... | collective-permute-start | bytes 294920 | tf_op jit(solution)/shard_map/ppermute | solution.py:489
  46.7 1.3 %collective-permute-start.7 = (bf16[3,2,64,128]{3,2,1,0:T(8,128)(2,1)}, bf16[3,2,64,128]{3,2,1,0:T(8,128)(2,1)}, u32[]{:S(2)}, u32[]{:S(2)}) collective-permute-start(bf16[3,2,64,128]{3,2,1,0:T(8,128)(2,1)} %get-tuple-element.25), channel_id=1, source_target_pairs={{1,0},{2,1},{3,2},{4,3},{5,4},{6,5},{7,6},{9,8},{10,9},{11,10},{12... | collective-permute-start | bytes 294920 | tf_op jit(solution)/shard_map/ppermute | solution.py:490
  48.0 3.1 %collective-permute-start.4 = (bf16[3,3,64,128]{3,2,1,0:T(8,128)(2,1)}, bf16[3,3,64,128]{3,2,1,0:T(8,128)(2,1)}, u32[]{:S(2)}, u32[]{:S(2)}) collective-permute-start(bf16[3,3,64,128]{3,2,1,0:T(8,128)(2,1)} %get-tuple-element.23), channel_id=1, source_target_pairs={{0,8},{8,16},{16,24},{24,32},{32,40},{40,48},{48,56},{56,64},{64,7... | collective-permute-start | bytes 442376 | tf_op jit(solution)/shard_map/ppermute | solution.py:487
  51.2 6.1 %collective-permute-start.5 = (bf16[3,3,64,128]{3,2,1,0:T(8,128)(2,1)S(1)}, bf16[3,3,64,128]{3,2,1,0:T(8,128)(2,1)}, u32[]{:S(2)}, u32[]{:S(2)}) collective-permute-start(bf16[3,3,64,128]{3,2,1,0:T(8,128)(2,1)S(1)} %get-tuple-element.24), channel_id=1, source_target_pairs={{8,0},{16,8},{24,16},{32,24},{40,32},{48,40},{56,48},{64,56},{72,6... | collective-permute-start | bytes 442376 | tf_op jit(solution)/shard_map/ppermute | solution.py:488
  57.2 0.0 copy-done.8
  57.2 1.6 %copy.17 = f32[64,2,64]{0,2,1:T(8,128)} copy(f32[64,2,64]{2,1,0:T(2,128)} %param.19) | data formatting | bytes 65536 | tf_op args[6]
  58.8 1.5 %copy.18 = f32[64,8,2,8]{0,3,2,1:T(8,128)} copy(f32[64,8,2,8]{0,3,1,2:T(8,128)} %bitcast.9) | data formatting | bytes 65536 | tf_op jit(solution)/shard_map/transpose | solution.py:529
  60.3 0.9 copy.19.refs_12_
  61.2 0.0 collective-permute-done.6.refs_3_
  61.2 0.0 collective-permute-done.7.refs_4_
  61.2 0.0 collective-permute-done.4.refs_1_
  61.2 0.0 collective-permute-done.5.refs_2_
  61.2 6.3 %section_two_0.1 = (f32[3,32,64,128]{3,2,1,0:T(8,128)}, f32[8,4,128]{2,1,0:T(4,128)S(1)}) custom-call(f32[3,32,64,128]{3,2,1,0:T(8,128)S(1)} %get-tuple-element.22.refs_0_, bf16[3,3,64,128]{3,2,1,0:T(8,128)(2,1)} %collective-permute-done.4.refs_1_, bf16[3,3,64,128]{3,2,1,0:T(8,128)(2,1)} %collective-permute-done.5.refs_2_, ...), custom_call_target="tpu_custom_call" | custom-call | flops 20000000 | bytes 8000000 | tf_op jit(solution)/shard_map/section_two_0/pallas_call | solution.py:348
  67.6 0.0 all-to-all-done
  67.6 0.8 broadcast_in_dim.2
  68.4 20.7 %all-to-all-start.1 = ((bf16[256,4,128]{2,1,0:T(4,128)(2,1)}), bf16[256,4,128]{2,1,0:T(4,128)(2,1)}, u32[]{:S(2)}, u32[]{:S(2)}) async-start(bf16[256,4,128]{2,1,0:T(4,128)(2,1)} %bitcast.7), calls=%async_computation.1 | async-start | bytes 524288 | tf_op jit(solution)/shard_map/all_to_all | solution.py:543
  89.0 0.0 copy-start.3
  89.0 0.0 copy-start.4
  89.1 7.6 %section_two_12.1 = f32[3,32,64,128]{3,2,1,0:T(8,128)} custom-call(f32[3,32,64,128]{3,2,1,0:T(8,128)S(1)} %get-tuple-element.22.refs_0_, bf16[3,3,64,128]{3,2,1,0:T(8,128)(2,1)} %collective-permute-done.4.refs_1_, bf16[3,3,64,128]{3,2,1,0:T(8,128)(2,1)} %collective-permute-done.5.refs_2_, ...), custom_call_target="tpu_custom_call", output_to_operand_aliasing={{}: (11, {})} | custom-call | flops 40000000 | bytes 16000000 | tf_op jit(solution)/shard_map/section_two_12/pallas_call | solution.py:348
  96.6 0.0 copy-start.1
  96.7 0.0 copy-done.3
  96.7 0.0 copy-done.4
  96.7 3.4 %gram_stored.1.known_ref = f32[2,8,32,1024]{3,2,1,0:T(8,128)S(1)} custom-call(f32[2,8,32,1024]{3,2,1,0:T(8,128)} %prior_ref.1, bf16[1024,256]{1,0:T(8,128)(2,1)} %bitcast.every_ref, bf16[32,256]{1,0:T(8,128)(2,1)S(1)} %copy-done.3, f32[1,256]{1,0:T(1,128)S(1)} %copy-done.4), custom_call_target="tpu_custom_call" | custom-call | flops 30000000 | bytes 12000000 | tf_op jit(solution)/shard_map/gram_stored/pallas_call | solution.py:560
  100.1 3.5 %all-to-all-done.1.amp_ref = bf16[256,4,128]{2,1,0:T(4,128)(2,1)} async-done(((bf16[256,4,128]{2,1,0:T(4,128)(2,1)}), bf16[256,4,128]{2,1,0:T(4,128)(2,1)}, u32[]{:S(2)}, u32[]{:S(2)}) %all-to-all-start.1) | async-done | bytes 262176 | tf_op jit(solution)/shard_map/all_to_all | solution.py:543
  103.7 0.0 copy-done.1
  103.7 3.5 %gram_amplitudes.1 = f32[2,8,32,1024]{3,2,1,0:T(8,128)} custom-call(f32[2,8,32,1024]{3,2,1,0:T(8,128)S(1)} %gram_stored.1.known_ref, bf16[256,4,128]{2,1,0:T(4,128)(2,1)} %all-to-all-done.1.amp_ref, s32[1]{0:T(128)} %bitcast.5.where_ref, bf16[2,128,128]{2,1,0:T(8,128)(2,1)S(1)} %copy-done.1), custom_call_target="tpu_custom_call" | custom-call | tf_op jit(solution)/shard_map/gram_amplitudes/pallas_call | solution.py:585
  (2 shorter events, 0.0 us)
Async XLA Ops:
  0.6 30.6 %copy-start = (bf16[384,256]{1,0:T(8,128)(2,1)S(1)}, bf16[384,256]{1,0:T(8,128)(2,1)}, u32[]{:S(2)}) copy-start(bf16[384,256]{1,0:T(8,128)(2,1)} %constant.17.clone.refs_9_) | copy-start | bytes 589828
  0.6 30.6 %copy-start.2 = (f32[3,3]{1,0:T(4,128)S(1)}, f32[3,3]{1,0:T(4,128)}, u32[]{:S(2)}) copy-start(f32[3,3]{1,0:T(4,128)} %refs_8_.5) | copy-start | bytes 112
  6.2 51.0 %copy-start.8 = (s32[32]{0:T(128)S(1)}, s32[32]{0:T(128)}, u32[]{:S(2)}) copy-start(s32[32]{0:T(128)} %param.18) | copy-start | bytes 388
  6.2 61.4 %all-to-all-start = ((bf16[32,32,256]{2,1,0:T(8,128)(2,1)}), bf16[32,32,256]{2,1,0:T(8,128)(2,1)}, u32[]{:S(2)}, u32[]{:S(2)}) async-start(bf16[32,32,256]{2,1,0:T(8,128)(2,1)} %get-tuple-element.18), calls=%async_computation | async-start | bytes 1048576 | tf_op jit(solution)/shard_map/all_to_all | solution.py:523
  19.0 10.9 %collective-permute-start = (bf16[3,3,64,128]{3,2,1,0:T(8,128)(2,1)}, bf16[3,3,64,128]{3,2,1,0:T(8,128)(2,1)S(1)}, u32[]{:S(2)}, u32[]{:S(2)}) collective-permute-start(bf16[3,3,64,128]{3,2,1,0:T(8,128)(2,1)} %get-tuple-element.20), channel_id=1, source_target_pairs={{0,8},{8,16},{16,24},{24,32},{32,40},{40,48},{48,56},{56,64},{64,7... | collective-permute-start | bytes 442376 | tf_op jit(solution)/shard_map/ppermute | solution.py:487
  20.7 10.5 %collective-permute-start.1 = (bf16[3,3,64,128]{3,2,1,0:T(8,128)(2,1)}, bf16[3,3,64,128]{3,2,1,0:T(8,128)(2,1)}, u32[]{:S(2)}, u32[]{:S(2)}) collective-permute-start(bf16[3,3,64,128]{3,2,1,0:T(8,128)(2,1)} %get-tuple-element.21), channel_id=1, source_target_pairs={{8,0},{16,8},{24,16},{32,24},{40,32},{48,40},{56,48},{64,56},{72,6... | collective-permute-start | bytes 442376 | tf_op jit(solution)/shard_map/ppermute | solution.py:488
  20.7 5.1 %collective-permute-start.2 = (bf16[3,2,64,128]{3,2,1,0:T(8,128)(2,1)}, bf16[3,2,64,128]{3,2,1,0:T(8,128)(2,1)S(1)}, u32[]{:S(2)}, u32[]{:S(2)}) collective-permute-start(bf16[3,2,64,128]{3,2,1,0:T(8,128)(2,1)} %get-tuple-element.16), channel_id=1, source_target_pairs={{0,1},{1,2},{2,3},{3,4},{4,5},{5,6},{6,7},{8,9},{9,10},{10,11},{11... | collective-permute-start | bytes 294920 | tf_op jit(solution)/shard_map/ppermute | solution.py:489
  23.9 6.0 %collective-permute-start.3 = (bf16[3,2,64,128]{3,2,1,0:T(8,128)(2,1)}, bf16[3,2,64,128]{3,2,1,0:T(8,128)(2,1)S(1)}, u32[]{:S(2)}, u32[]{:S(2)}) collective-permute-start(bf16[3,2,64,128]{3,2,1,0:T(8,128)(2,1)} %get-tuple-element.16), channel_id=1, source_target_pairs={{1,0},{2,1},{3,2},{4,3},{5,4},{6,5},{7,6},{9,8},{10,9},{11,10},{12... | collective-permute-start | bytes 294920 | tf_op jit(solution)/shard_map/ppermute | solution.py:490
  25.8 4.0 %copy-start.6 = (bf16[3,2,64,128]{3,2,1,0:T(8,128)(2,1)}, bf16[3,2,64,128]{3,2,1,0:T(8,128)(2,1)S(1)}, u32[]{:S(2)}) copy-start(bf16[3,2,64,128]{3,2,1,0:T(8,128)(2,1)S(1)} %collective-permute-done.2.refs_3_) | copy-start | bytes 294916
  29.9 0.6 copy-start.7
  30.5 0.7 copy-start.5
  42.9 18.3 %collective-permute-start.6 = (bf16[3,2,64,128]{3,2,1,0:T(8,128)(2,1)}, bf16[3,2,64,128]{3,2,1,0:T(8,128)(2,1)}, u32[]{:S(2)}, u32[]{:S(2)}) collective-permute-start(bf16[3,2,64,128]{3,2,1,0:T(8,128)(2,1)} %get-tuple-element.25), channel_id=1, source_target_pairs={{0,1},{1,2},{2,3},{3,4},{4,5},{5,6},{6,7},{8,9},{9,10},{10,11},{11... | collective-permute-start | bytes 294920 | tf_op jit(solution)/shard_map/ppermute | solution.py:489
  46.7 14.4 %collective-permute-start.7 = (bf16[3,2,64,128]{3,2,1,0:T(8,128)(2,1)}, bf16[3,2,64,128]{3,2,1,0:T(8,128)(2,1)}, u32[]{:S(2)}, u32[]{:S(2)}) collective-permute-start(bf16[3,2,64,128]{3,2,1,0:T(8,128)(2,1)} %get-tuple-element.25), channel_id=1, source_target_pairs={{1,0},{2,1},{3,2},{4,3},{5,4},{6,5},{7,6},{9,8},{10,9},{11,10},{12... | collective-permute-start | bytes 294920 | tf_op jit(solution)/shard_map/ppermute | solution.py:490
  48.0 13.2 %collective-permute-start.4 = (bf16[3,3,64,128]{3,2,1,0:T(8,128)(2,1)}, bf16[3,3,64,128]{3,2,1,0:T(8,128)(2,1)}, u32[]{:S(2)}, u32[]{:S(2)}) collective-permute-start(bf16[3,3,64,128]{3,2,1,0:T(8,128)(2,1)} %get-tuple-element.23), channel_id=1, source_target_pairs={{0,8},{8,16},{16,24},{24,32},{32,40},{40,48},{48,56},{56,64},{64,7... | collective-permute-start | bytes 442376 | tf_op jit(solution)/shard_map/ppermute | solution.py:487
  51.2 10.0 %collective-permute-start.5 = (bf16[3,3,64,128]{3,2,1,0:T(8,128)(2,1)S(1)}, bf16[3,3,64,128]{3,2,1,0:T(8,128)(2,1)}, u32[]{:S(2)}, u32[]{:S(2)}) collective-permute-start(bf16[3,3,64,128]{3,2,1,0:T(8,128)(2,1)S(1)} %get-tuple-element.24), channel_id=1, source_target_pairs={{8,0},{16,8},{24,16},{32,24},{40,32},{48,40},{56,48},{64,56},{72,6... | collective-permute-start | bytes 442376 | tf_op jit(solution)/shard_map/ppermute | solution.py:488
  68.4 35.3 %all-to-all-start.1 = ((bf16[256,4,128]{2,1,0:T(4,128)(2,1)}), bf16[256,4,128]{2,1,0:T(4,128)(2,1)}, u32[]{:S(2)}, u32[]{:S(2)}) async-start(bf16[256,4,128]{2,1,0:T(4,128)(2,1)} %bitcast.7), calls=%async_computation.1 | async-start | bytes 524288 | tf_op jit(solution)/shard_map/all_to_all | solution.py:543
  89.0 7.6 %copy-start.3 = (bf16[32,256]{1,0:T(8,128)(2,1)S(1)}, bf16[32,256]{1,0:T(8,128)(2,1)}, u32[]{:S(2)}) copy-start(bf16[32,256]{1,0:T(8,128)(2,1)} %get-tuple-element.19.own_ref) | copy-start | bytes 49156
  89.0 7.6 %copy-start.4 = (f32[1,256]{1,0:T(1,128)S(1)}, f32[1,256]{1,0:T(1,128)}, u32[]{:S(2)}) copy-start(f32[1,256]{1,0:T(1,128)} %constant.18.clone.ramp_ref) | copy-start | bytes 3076
  96.6 7.0 %copy-start.1 = (bf16[2,128,128]{2,1,0:T(8,128)(2,1)S(1)}, bf16[2,128,128]{2,1,0:T(8,128)(2,1)}, u32[]{:S(2)}) copy-start(bf16[2,128,128]{2,1,0:T(8,128)(2,1)} %constant.19.clone.rep_ref) | copy-start | bytes 196612

commit v5 on v4

--- a/solution.py
+++ b/solution.py
@@ -525,28 +525,6 @@
     (section_one, low, high, edge) = section(flow_state, halos, fields, mixing, table)
     halos = exchange(low, high, edge)
 
-    te_local = te_index - chord_pos * cells
-    band_table = band_response.reshape(normal, 2, chord_n, bands).transpose(0, 2, 1, 3)
-    band_table = band_table.reshape(normal, chord_n * 2 * bands)
-    flow_next, amps = section(
-        section_one,
-        halos,
-        fields,
-        mixing,
-        table,
-        (0,),
-        flow=flow_state,
-        te_local=te_local,
-        band_table=band_table,
-    )
-    amps = jnp.broadcast_to(amps.astype(BF16)[None], (span_n,) + amps.shape)
-    amps = lax.all_to_all(
-        amps.reshape((span_n * chord_n,) + amps.shape[2:]), ("span", "chord"), 0, 0, tiled=True
-    )
-    (flow_next,) = section(
-        section_one, halos, fields, mixing, table, (1, 2), flow=flow_state, onto=flow_next
-    )
-
     ramp = np.tile((np.arange(segs, dtype=np.float32) + 1) / segs, 2 * bands)[None]
     tiles = 4
     tile = span_n * stations // tiles
@@ -580,6 +558,30 @@
         packed,
         ramp,
     )
+    halos, known = lax.optimization_barrier((halos, known))
+
+    te_local = te_index - chord_pos * cells
+    band_table = band_response.reshape(normal, 2, chord_n, bands).transpose(0, 2, 1, 3)
+    band_table = band_table.reshape(normal, chord_n * 2 * bands)
+    flow_next, amps = section(
+        section_one,
+        halos,
+        fields,
+        mixing,
+        table,
+        (0,),
+        flow=flow_state,
+        te_local=te_local,
+        band_table=band_table,
+    )
+    amps = jnp.broadcast_to(amps.astype(BF16)[None], (span_n,) + amps.shape)
+    amps = lax.all_to_all(
+        amps.reshape((span_n * chord_n,) + amps.shape[2:]), ("span", "chord"), 0, 0, tiled=True
+    )
+    (flow_next,) = section(
+        section_one, halos, fields, mixing, table, (1, 2), flow=flow_state, onto=flow_next
+    )
+
     known, flow_next = lax.optimization_barrier((known, flow_next))
     reps = amplitude_tables()
     gram_next = pl.pallas_call(

time: 108 us -> 110 us (1.019)
  starting transfers between devices: 53.9 us -> 55.4 us
    all_to_all x1, waiting for transfers between devices: 3.55 us -> 6.99 us  [shards(): lax.all_to_all(amps.reshape((span_n * chord_n,) + amps.shape[2:]), ('span...]
    ppermute x2, waiting for transfers between devices: 4.04 us -> 0.67 us  [exchange(): lax.ppermute(edge, 'chord', backward)]
    ppermute x2, starting transfers between devices: 7.04 us -> 9.29 us  [exchange(): lax.ppermute(edge, 'chord', forward)]
    all_to_all x1, starting transfers between devices: 20.7 us -> 18.5 us  [shards(): lax.all_to_all(amps.reshape((span_n * chord_n,) + amps.shape[2:]), ('span...]
    ppermute x2, starting transfers between devices: 6.07 us -> 7.52 us  [exchange(): lax.ppermute(low, 'span', down)]
    unnamed x19 -> x23, local copies, waits for them, and re-layouts: 2.88 us -> 3.81 us
  transfers between devices with their start and end apart: 10 -> 10, of which waited for: 3 -> 3; matrix products, arithmetic and copies ran while one was open for 4% -> 2% of each run, Pallas kernels for 27% -> 21%
where the time goes in v5:
time: 110 us
  starting transfers between devices  55.4 us (50%)
  Pallas kernels  38.3 us (35%)
  waiting for transfers between devices  8.95 us (8%)
  local copies, waits for them, and re-layouts  6.11 us (6%)
    pallas_call x3, Pallas kernels, section(): pl.pallas_call(functools.partial(section_kernel, second=second, profile=p...  25.8 us
    all_to_all x1, starting transfers between devices, shards(): lax.all_to_all(amps.reshape((span_n * chord_n,) + amps.shape[2:]), ('span...  18.5 us
    all_to_all x1, starting transfers between devices, shards(): lax.all_to_all(send, 'span', 0, 0, tiled=True)  12.8 us
    ppermute x2, starting transfers between devices, exchange(): lax.ppermute(edge, 'chord', forward)  9.29 us
    ppermute x2, starting transfers between devices, exchange(): lax.ppermute(low, 'span', down)  7.52 us
    all_to_all x1, waiting for transfers between devices, shards(): lax.all_to_all(amps.reshape((span_n * chord_n,) + amps.shape[2:]), ('span...  6.99 us
    ppermute x2, starting transfers between devices, exchange(): lax.ppermute(high, 'span', up)  4.76 us
    unnamed x23, local copies, waits for them, and re-layouts  3.81 us
  transfers between devices with their start and end apart: 10, of which 3 were waited for; matrix products, arithmetic and copies ran while one was open for 2% of the time, Pallas kernels for 21%

profile of v5, /device:TPU:1, one launch (start us, length us, event | category | flops | bytes accessed | tf_op | source)
XLA Modules:
  0.0 109.6 jit_solution(5421349948962051412)
XLA Ops:
  0.6 0.0 copy-start.2
  0.6 0.0 copy-start.4
  0.7 3.6 %edges.1 = (bf16[3,2,64,128]{3,2,1,0:T(8,128)(2,1)}, bf16[3,3,64,128]{3,2,1,0:T(8,128)(2,1)}, bf16[3,3,64,128]{3,2,1,0:T(8,128)(2,1)}) custom-call(f32[3,32,64,128]{3,2,1,0:T(8,128)} %refs_10_.3), custom_call_target="tpu_custom_call" | custom-call | tf_op jit(solution)/shard_map/edges/pallas_call | solution.py:499
  4.3 1.9 %spectra.1 = (bf16[32,256]{1,0:T(8,128)(2,1)}, bf16[32,32,256]{2,1,0:T(8,128)(2,1)}) custom-call(bf16[32,8,128]{2,1,0:T(8,128)(2,1)} %spectra_ref, s32[16]{0:T(128)} %wanted_ref.1), custom_call_target="tpu_custom_call" | custom-call | tf_op jit(solution)/shard_map/spectra/pallas_call | solution.py:511
  6.2 0.0 copy-start.10
  6.2 12.8 %all-to-all-start = ((bf16[32,32,256]{2,1,0:T(8,128)(2,1)}), bf16[32,32,256]{2,1,0:T(8,128)(2,1)}, u32[]{:S(2)}, u32[]{:S(2)}) async-start(bf16[32,32,256]{2,1,0:T(8,128)(2,1)} %get-tuple-element.28), calls=%async_computation | async-start | bytes 1048576 | tf_op jit(solution)/shard_map/all_to_all | solution.py:523
  19.0 0.0 copy-start.5
  19.0 0.0 copy-start.6
  19.0 1.7 %collective-permute-start = (bf16[3,3,64,128]{3,2,1,0:T(8,128)(2,1)}, bf16[3,3,64,128]{3,2,1,0:T(8,128)(2,1)S(1)}, u32[]{:S(2)}, u32[]{:S(2)}) collective-permute-start(bf16[3,3,64,128]{3,2,1,0:T(8,128)(2,1)} %get-tuple-element.21), channel_id=1, source_target_pairs={{0,8},{8,16},{16,24},{24,32},{32,40},{40,48},{48,56},{56,64},{64,7... | collective-permute-start | bytes 442376 | tf_op jit(solution)/shard_map/ppermute | solution.py:487
  20.7 0.0 collective-permute-start.1
  20.7 1.3 %collective-permute-start.3 = (bf16[3,2,64,128]{3,2,1,0:T(8,128)(2,1)}, bf16[3,2,64,128]{3,2,1,0:T(8,128)(2,1)S(1)}, u32[]{:S(2)}, u32[]{:S(2)}) collective-permute-start(bf16[3,2,64,128]{3,2,1,0:T(8,128)(2,1)} %get-tuple-element.23), channel_id=1, source_target_pairs={{1,0},{2,1},{3,2},{4,3},{5,4},{6,5},{7,6},{9,8},{10,9},{11,10},{12... | collective-permute-start | bytes 294920 | tf_op jit(solution)/shard_map/ppermute | solution.py:490
  22.0 4.0 %collective-permute-start.2 = (bf16[3,2,64,128]{3,2,1,0:T(8,128)(2,1)}, bf16[3,2,64,128]{3,2,1,0:T(8,128)(2,1)S(1)}, u32[]{:S(2)}, u32[]{:S(2)}) collective-permute-start(bf16[3,2,64,128]{3,2,1,0:T(8,128)(2,1)} %get-tuple-element.23), channel_id=1, source_target_pairs={{0,1},{1,2},{2,3},{3,4},{4,5},{5,6},{6,7},{8,9},{9,10},{10,11},{11... | collective-permute-start | bytes 294920 | tf_op jit(solution)/shard_map/ppermute | solution.py:489
  26.0 0.7 collective-permute-done.3.refs_4_
  26.7 0.0 copy-start.8
  26.7 1.3 %collective-permute-done.2.refs_3_ = bf16[3,2,64,128]{3,2,1,0:T(8,128)(2,1)S(1)} collective-permute-done((bf16[3,2,64,128]{3,2,1,0:T(8,128)(2,1)}, bf16[3,2,64,128]{3,2,1,0:T(8,128)(2,1)S(1)}, u32[]{:S(2)}, u32[]{:S(2)}) %collective-permute-start.2) | collective-permute-done | bytes 98336 | tf_op jit(solution)/shard_map/ppermute | solution.py:489
  28.0 0.0 copy-start.9
  28.0 0.0 collective-permute-done.refs_1_
  28.0 0.0 copy-done.8
  28.0 0.6 copy-done.9
  28.6 0.0 copy-start.7
  28.6 0.6 copy-done.7
  29.2 0.0 collective-permute-done.1.refs_2_
  29.2 0.0 copy-done.2
  29.2 0.0 copy-done.4
  29.2 11.7 %section_one_012.1 = (f32[3,32,64,128]{3,2,1,0:T(8,128)S(1)}, bf16[3,3,64,128]{3,2,1,0:T(8,128)(2,1)}, bf16[3,3,64,128]{3,2,1,0:T(8,128)(2,1)}, bf16[3,2,64,128]{3,2,1,0:T(8,128)(2,1)S(1)}) custom-call(f32[3,32,64,128]{3,2,1,0:T(8,128)} %refs_10_.3, bf16[3,3,64,128]{3,2,1,0:T(8,128)(2,1)} %copy-done.7, ...), custom_call_target="tpu_custom_call" | custom-call | flops 60000000 | bytes 24000000 | tf_op jit(solution)/shard_map/section_one_012/pallas_call | solution.py:348
  41.0 1.3 %collective-permute-start.7 = (bf16[3,2,64,128]{3,2,1,0:T(8,128)(2,1)S(1)}, bf16[3,2,64,128]{3,2,1,0:T(8,128)(2,1)}, u32[]{:S(2)}, u32[]{:S(2)}) collective-permute-start(bf16[3,2,64,128]{3,2,1,0:T(8,128)(2,1)S(1)} %get-tuple-element.26), channel_id=1, source_target_pairs={{1,0},{2,1},{3,2},{4,3},{5,4},{6,5},{7,6},{9,8},{10,9},{11,10},{12... | collective-permute-start | bytes 294920 | tf_op jit(solution)/shard_map/ppermute | solution.py:490
  42.3 5.3 %collective-permute-start.6 = (bf16[3,2,64,128]{3,2,1,0:T(8,128)(2,1)S(1)}, bf16[3,2,64,128]{3,2,1,0:T(8,128)(2,1)}, u32[]{:S(2)}, u32[]{:S(2)}) collective-permute-start(bf16[3,2,64,128]{3,2,1,0:T(8,128)(2,1)S(1)} %get-tuple-element.26), channel_id=1, source_target_pairs={{0,1},{1,2},{2,3},{3,4},{4,5},{5,6},{6,7},{8,9},{9,10},{10,11},{11... | collective-permute-start | bytes 294920 | tf_op jit(solution)/shard_map/ppermute | solution.py:489
  47.6 3.1 %collective-permute-start.4 = (bf16[3,3,64,128]{3,2,1,0:T(8,128)(2,1)}, bf16[3,3,64,128]{3,2,1,0:T(8,128)(2,1)}, u32[]{:S(2)}, u32[]{:S(2)}) collective-permute-start(bf16[3,3,64,128]{3,2,1,0:T(8,128)(2,1)} %get-tuple-element.24), channel_id=1, source_target_pairs={{0,8},{8,16},{16,24},{24,32},{32,40},{40,48},{48,56},{56,64},{64,7... | collective-permute-start | bytes 442376 | tf_op jit(solution)/shard_map/ppermute | solution.py:487
  50.6 7.5 %collective-permute-start.5 = (bf16[3,3,64,128]{3,2,1,0:T(8,128)(2,1)}, bf16[3,3,64,128]{3,2,1,0:T(8,128)(2,1)}, u32[]{:S(2)}, u32[]{:S(2)}) collective-permute-start(bf16[3,3,64,128]{3,2,1,0:T(8,128)(2,1)} %get-tuple-element.25), channel_id=1, source_target_pairs={{8,0},{16,8},{24,16},{32,24},{40,32},{48,40},{56,48},{64,56},{72,6... | collective-permute-start | bytes 442376 | tf_op jit(solution)/shard_map/ppermute | solution.py:488
  58.1 0.0 copy-done.10
  58.1 0.9 copy.17
  59.1 0.6 copy.18
  59.7 0.9 copy.19.refs_12_
  60.6 0.0 all-to-all-done
  60.6 0.0 copy-done.5
  60.6 0.0 copy-done.6
  60.6 3.4 %gram_stored.1.known_ref = f32[2,8,32,1024]{3,2,1,0:T(8,128)S(1)} custom-call(f32[2,8,32,1024]{3,2,1,0:T(8,128)} %prior_ref.1, bf16[1024,256]{1,0:T(8,128)(2,1)} %bitcast.every_ref, bf16[32,256]{1,0:T(8,128)(2,1)S(1)} %copy-done.5, f32[1,256]{1,0:T(1,128)S(1)} %copy-done.6), custom_call_target="tpu_custom_call" | custom-call | flops 30000000 | bytes 12000000 | tf_op jit(solution)/shard_map/gram_stored/pallas_call | solution.py:538
  64.1 0.0 copy-start
  64.1 0.0 collective-permute-done.7.refs_4_
  64.1 0.0 collective-permute-done.6.refs_3_
  64.1 0.0 collective-permute-done.4.refs_1_
  64.1 0.0 collective-permute-done.5.refs_2_
  64.1 6.5 %section_two_0.1 = (f32[3,32,64,128]{3,2,1,0:T(8,128)}, f32[8,4,128]{2,1,0:T(4,128)S(1)}) custom-call(f32[3,32,64,128]{3,2,1,0:T(8,128)S(1)} %get-tuple-element.31.refs_0_, bf16[3,3,64,128]{3,2,1,0:T(8,128)(2,1)} %collective-permute-done.4.refs_1_, bf16[3,3,64,128]{3,2,1,0:T(8,128)(2,1)} %collective-permute-done.5.refs_2_, ...), custom_call_target="tpu_custom_call" | custom-call | flops 20000000 | bytes 8000000 | tf_op jit(solution)/shard_map/section_two_0/pallas_call | solution.py:348
  70.6 0.0 copy-done
  70.6 0.8 broadcast_in_dim.2
  71.4 18.5 %all-to-all-start.1 = ((bf16[256,4,128]{2,1,0:T(4,128)(2,1)}), bf16[256,4,128]{2,1,0:T(4,128)(2,1)}, u32[]{:S(2)}, u32[]{:S(2)}) async-start(bf16[256,4,128]{2,1,0:T(4,128)(2,1)} %bitcast.7), calls=%async_computation.1 | async-start | bytes 524288 | tf_op jit(solution)/shard_map/all_to_all | solution.py:578
  89.9 0.0 copy-start.3
  89.9 7.6 %section_two_12.1 = f32[3,32,64,128]{3,2,1,0:T(8,128)} custom-call(f32[3,32,64,128]{3,2,1,0:T(8,128)S(1)} %get-tuple-element.31.refs_0_, bf16[3,3,64,128]{3,2,1,0:T(8,128)(2,1)} %collective-permute-done.4.refs_1_, bf16[3,3,64,128]{3,2,1,0:T(8,128)(2,1)} %collective-permute-done.5.refs_2_, ...), custom_call_target="tpu_custom_call", output_to_operand_aliasing={{}: (11, {})} | custom-call | flops 40000000 | bytes 16000000 | tf_op jit(solution)/shard_map/section_two_12/pallas_call | solution.py:348
  97.5 7.0 %all-to-all-done.1.amp_ref = bf16[256,4,128]{2,1,0:T(4,128)(2,1)} async-done(((bf16[256,4,128]{2,1,0:T(4,128)(2,1)}), bf16[256,4,128]{2,1,0:T(4,128)(2,1)}, u32[]{:S(2)}, u32[]{:S(2)}) %all-to-all-start.1) | async-done | bytes 262176 | tf_op jit(solution)/shard_map/all_to_all | solution.py:578
  104.5 0.0 copy-done.3
  104.5 0.0 copy-start.1
  104.5 1.6 %copy-done.1 = f32[2,8,32,1024]{3,2,1,0:T(8,128)S(1)} copy-done((f32[2,8,32,1024]{3,2,1,0:T(8,128)S(1)}, f32[2,8,32,1024]{3,2,1,0:T(8,128)}, u32[]{:S(2)}) %copy-start.1) | copy-done | bytes 2097176
  106.1 3.5 %gram_amplitudes.1 = f32[2,8,32,1024]{3,2,1,0:T(8,128)} custom-call(f32[2,8,32,1024]{3,2,1,0:T(8,128)S(1)} %copy-done.1, bf16[256,4,128]{2,1,0:T(4,128)(2,1)} %all-to-all-done.1.amp_ref, s32[1]{0:T(128)} %bitcast.5.where_ref, bf16[2,128,128]{2,1,0:T(8,128)(2,1)S(1)} %copy-done.3), custom_call_target="tpu_custom_call" | custom-call | tf_op jit(solution)/shard_map/gram_amplitudes/pallas_call | solution.py:587
  (2 shorter events, 0.0 us)
Async XLA Ops:
  0.6 28.6 %copy-start.2 = (bf16[384,256]{1,0:T(8,128)(2,1)S(1)}, bf16[384,256]{1,0:T(8,128)(2,1)}, u32[]{:S(2)}) copy-start(bf16[384,256]{1,0:T(8,128)(2,1)} %constant.17.clone.refs_9_) | copy-start | bytes 589828
  0.6 28.6 %copy-start.4 = (f32[3,3]{1,0:T(4,128)S(1)}, f32[3,3]{1,0:T(4,128)}, u32[]{:S(2)}) copy-start(f32[3,3]{1,0:T(4,128)} %refs_8_.5) | copy-start | bytes 112
  6.2 51.9 %copy-start.10 = (s32[32]{0:T(128)S(1)}, s32[32]{0:T(128)}, u32[]{:S(2)}) copy-start(s32[32]{0:T(128)} %param.18) | copy-start | bytes 388
  6.2 54.4 %all-to-all-start = ((bf16[32,32,256]{2,1,0:T(8,128)(2,1)}), bf16[32,32,256]{2,1,0:T(8,128)(2,1)}, u32[]{:S(2)}, u32[]{:S(2)}) async-start(bf16[32,32,256]{2,1,0:T(8,128)(2,1)} %get-tuple-element.28), calls=%async_computation | async-start | bytes 1048576 | tf_op jit(solution)/shard_map/all_to_all | solution.py:523
  19.0 41.6 %copy-start.5 = (bf16[32,256]{1,0:T(8,128)(2,1)S(1)}, bf16[32,256]{1,0:T(8,128)(2,1)}, u32[]{:S(2)}) copy-start(bf16[32,256]{1,0:T(8,128)(2,1)} %get-tuple-element.29.own_ref) | copy-start | bytes 49156
  19.0 41.6 %copy-start.6 = (f32[1,256]{1,0:T(1,128)S(1)}, f32[1,256]{1,0:T(1,128)}, u32[]{:S(2)}) copy-start(f32[1,256]{1,0:T(1,128)} %constant.18.clone.ramp_ref) | copy-start | bytes 3076
  19.0 8.9 %collective-permute-start = (bf16[3,3,64,128]{3,2,1,0:T(8,128)(2,1)}, bf16[3,3,64,128]{3,2,1,0:T(8,128)(2,1)S(1)}, u32[]{:S(2)}, u32[]{:S(2)}) collective-permute-start(bf16[3,3,64,128]{3,2,1,0:T(8,128)(2,1)} %get-tuple-element.21), channel_id=1, source_target_pairs={{0,8},{8,16},{16,24},{24,32},{32,40},{40,48},{48,56},{56,64},{64,7... | collective-permute-start | bytes 442376 | tf_op jit(solution)/shard_map/ppermute | solution.py:487
  20.7 8.5 %collective-permute-start.1 = (bf16[3,3,64,128]{3,2,1,0:T(8,128)(2,1)}, bf16[3,3,64,128]{3,2,1,0:T(8,128)(2,1)}, u32[]{:S(2)}, u32[]{:S(2)}) collective-permute-start(bf16[3,3,64,128]{3,2,1,0:T(8,128)(2,1)} %get-tuple-element.22), channel_id=1, source_target_pairs={{8,0},{16,8},{24,16},{32,24},{40,32},{48,40},{56,48},{64,56},{72,6... | collective-permute-start | bytes 442376 | tf_op jit(solution)/shard_map/ppermute | solution.py:488
  20.7 6.0 %collective-permute-start.3 = (bf16[3,2,64,128]{3,2,1,0:T(8,128)(2,1)}, bf16[3,2,64,128]{3,2,1,0:T(8,128)(2,1)S(1)}, u32[]{:S(2)}, u32[]{:S(2)}) collective-permute-start(bf16[3,2,64,128]{3,2,1,0:T(8,128)(2,1)} %get-tuple-element.23), channel_id=1, source_target_pairs={{1,0},{2,1},{3,2},{4,3},{5,4},{6,5},{7,6},{9,8},{10,9},{11,10},{12... | collective-permute-start | bytes 294920 | tf_op jit(solution)/shard_map/ppermute | solution.py:490
  22.0 5.9 %collective-permute-start.2 = (bf16[3,2,64,128]{3,2,1,0:T(8,128)(2,1)}, bf16[3,2,64,128]{3,2,1,0:T(8,128)(2,1)S(1)}, u32[]{:S(2)}, u32[]{:S(2)}) collective-permute-start(bf16[3,2,64,128]{3,2,1,0:T(8,128)(2,1)} %get-tuple-element.23), channel_id=1, source_target_pairs={{0,1},{1,2},{2,3},{3,4},{4,5},{5,6},{6,7},{8,9},{9,10},{10,11},{11... | collective-permute-start | bytes 294920 | tf_op jit(solution)/shard_map/ppermute | solution.py:489
  26.7 1.3 %copy-start.8 = (bf16[3,2,64,128]{3,2,1,0:T(8,128)(2,1)}, bf16[3,2,64,128]{3,2,1,0:T(8,128)(2,1)S(1)}, u32[]{:S(2)}) copy-start(bf16[3,2,64,128]{3,2,1,0:T(8,128)(2,1)S(1)} %collective-permute-done.3.refs_4_) | copy-start | bytes 294916
  28.0 0.6 copy-start.9
  28.6 0.6 copy-start.7
  41.0 23.1 %collective-permute-start.7 = (bf16[3,2,64,128]{3,2,1,0:T(8,128)(2,1)S(1)}, bf16[3,2,64,128]{3,2,1,0:T(8,128)(2,1)}, u32[]{:S(2)}, u32[]{:S(2)}) collective-permute-start(bf16[3,2,64,128]{3,2,1,0:T(8,128)(2,1)S(1)} %get-tuple-element.26), channel_id=1, source_target_pairs={{1,0},{2,1},{3,2},{4,3},{5,4},{6,5},{7,6},{9,8},{10,9},{11,10},{12... | collective-permute-start | bytes 294920 | tf_op jit(solution)/shard_map/ppermute | solution.py:490
  42.3 21.8 %collective-permute-start.6 = (bf16[3,2,64,128]{3,2,1,0:T(8,128)(2,1)S(1)}, bf16[3,2,64,128]{3,2,1,0:T(8,128)(2,1)}, u32[]{:S(2)}, u32[]{:S(2)}) collective-permute-start(bf16[3,2,64,128]{3,2,1,0:T(8,128)(2,1)S(1)} %get-tuple-element.26), channel_id=1, source_target_pairs={{0,1},{1,2},{2,3},{3,4},{4,5},{5,6},{6,7},{8,9},{9,10},{10,11},{11... | collective-permute-start | bytes 294920 | tf_op jit(solution)/shard_map/ppermute | solution.py:489
  47.6 16.5 %collective-permute-start.4 = (bf16[3,3,64,128]{3,2,1,0:T(8,128)(2,1)}, bf16[3,3,64,128]{3,2,1,0:T(8,128)(2,1)}, u32[]{:S(2)}, u32[]{:S(2)}) collective-permute-start(bf16[3,3,64,128]{3,2,1,0:T(8,128)(2,1)} %get-tuple-element.24), channel_id=1, source_target_pairs={{0,8},{8,16},{16,24},{24,32},{32,40},{40,48},{48,56},{56,64},{64,7... | collective-permute-start | bytes 442376 | tf_op jit(solution)/shard_map/ppermute | solution.py:487
  50.6 13.5 %collective-permute-start.5 = (bf16[3,3,64,128]{3,2,1,0:T(8,128)(2,1)}, bf16[3,3,64,128]{3,2,1,0:T(8,128)(2,1)}, u32[]{:S(2)}, u32[]{:S(2)}) collective-permute-start(bf16[3,3,64,128]{3,2,1,0:T(8,128)(2,1)} %get-tuple-element.25), channel_id=1, source_target_pairs={{8,0},{16,8},{24,16},{32,24},{40,32},{48,40},{56,48},{64,56},{72,6... | collective-permute-start | bytes 442376 | tf_op jit(solution)/shard_map/ppermute | solution.py:488
  64.1 6.5 %copy-start = (f32[2,8,32,1024]{3,2,1,0:T(8,128)}, f32[2,8,32,1024]{3,2,1,0:T(8,128)S(1)}, u32[]{:S(2)}) copy-start(f32[2,8,32,1024]{3,2,1,0:T(8,128)S(1)} %gram_stored.1.known_ref) | copy-start | bytes 6291460
  71.4 33.1 %all-to-all-start.1 = ((bf16[256,4,128]{2,1,0:T(4,128)(2,1)}), bf16[256,4,128]{2,1,0:T(4,128)(2,1)}, u32[]{:S(2)}, u32[]{:S(2)}) async-start(bf16[256,4,128]{2,1,0:T(4,128)(2,1)} %bitcast.7), calls=%async_computation.1 | async-start | bytes 524288 | tf_op jit(solution)/shard_map/all_to_all | solution.py:578
  89.9 14.6 %copy-start.3 = (bf16[2,128,128]{2,1,0:T(8,128)(2,1)S(1)}, bf16[2,128,128]{2,1,0:T(8,128)(2,1)}, u32[]{:S(2)}) copy-start(bf16[2,128,128]{2,1,0:T(8,128)(2,1)} %constant.19.clone.rep_ref) | copy-start | bytes 196612
  104.5 1.6 %copy-start.1 = (f32[2,8,32,1024]{3,2,1,0:T(8,128)S(1)}, f32[2,8,32,1024]{3,2,1,0:T(8,128)}, u32[]{:S(2)}) copy-start(f32[2,8,32,1024]{3,2,1,0:T(8,128)} %copy-done) | copy-start | bytes 6291460

commit v6 on v5

--- a/solution.py
+++ b/solution.py
@@ -520,6 +520,7 @@
         ],
         name="spectra",
     )(stored, offsets)
+    halos, send = lax.optimization_barrier((halos, send))
     every = lax.all_to_all(send, "span", 0, 0, tiled=True).reshape(span_n * stations, width)
 
     (section_one, low, high, edge) = section(flow_state, halos, fields, mixing, table)
@@ -599,7 +600,7 @@
         compiler_params=params,
         name="gram_amplitudes",
     )(
-        known,
+        pltpu.with_memory_space_constraint(known, pltpu.HBM),
         amps,
         span_pos.reshape(1),
         reps,

time: 110 us -> 101 us (0.918)
  starting transfers between devices: 55.4 us -> 50.3 us
  local copies, waits for them, and re-layouts: 6.11 us -> 3.29 us
  waiting for transfers between devices: 8.95 us -> 7.03 us
    ppermute x2, starting transfers between devices: 7.52 us -> 0.72 us  [exchange(): lax.ppermute(low, 'span', down)]
    unnamed x23, local copies, waits for them, and re-layouts: 3.81 us -> 0.97 us
    all_to_all x1, starting transfers between devices: 12.8 us -> 14.1 us  [shards(): lax.all_to_all(send, 'span', 0, 0, tiled=True)]
    ppermute x2, waiting for transfers between devices: 1.26 us -> 0.01 us  [exchange(): lax.ppermute(edge, 'chord', forward)]
  transfers between devices with their start and end apart: 10 -> 10, of which waited for: 3 -> 1; matrix products, arithmetic and copies ran while one was open for 2% -> 2% of each run, Pallas kernels for 21% -> 25%
where the time goes in v6:
time: 101 us
  starting transfers between devices  50.3 us (50%)
  Pallas kernels  39.2 us (39%)
  waiting for transfers between devices  7.03 us (7%)
  local copies, waits for them, and re-layouts  3.29 us (3%)
    pallas_call x3, Pallas kernels, section(): pl.pallas_call(functools.partial(section_kernel, second=second, profile=p...  25.8 us
    all_to_all x1, starting transfers between devices, shards(): lax.all_to_all(amps.reshape((span_n * chord_n,) + amps.shape[2:]), ('span...  19.2 us
    all_to_all x1, starting transfers between devices, shards(): lax.all_to_all(send, 'span', 0, 0, tiled=True)  14.1 us
    ppermute x2, starting transfers between devices, exchange(): lax.ppermute(edge, 'chord', forward)  9.19 us
    all_to_all x1, waiting for transfers between devices, shards(): lax.all_to_all(amps.reshape((span_n * chord_n,) + amps.shape[2:]), ('span...  6.99 us
    ppermute x2, starting transfers between devices, exchange(): lax.ppermute(high, 'span', up)  4.51 us
    pallas_call x1, Pallas kernels, shards(): pl.pallas_call(amplitude_kernel, grid=(tiles,), out_shape=gram_shape, in_...  4.4 us
    pallas_call x1, Pallas kernels, shards(): pl.pallas_call(edges_kernel, grid=(count,), out_shape=(edge_shape, ends_s...  3.61 us
  transfers between devices with their start and end apart: 10, of which 1 were waited for; matrix products, arithmetic and copies ran while one was open for 2% of the time, Pallas kernels for 25%

profile of v6, /device:TPU:1, one launch (start us, length us, event | category | flops | bytes accessed | tf_op | source)
XLA Modules:
  0.0 100.8 jit_solution(14576196864295164153)
XLA Ops:
  0.6 0.0 copy-start.1
  0.6 0.0 copy-start.3
  0.7 3.6 %edges.1 = (bf16[3,2,64,128]{3,2,1,0:T(8,128)(2,1)}, bf16[3,3,64,128]{3,2,1,0:T(8,128)(2,1)}, bf16[3,3,64,128]{3,2,1,0:T(8,128)(2,1)}) custom-call(f32[3,32,64,128]{3,2,1,0:T(8,128)} %refs_10_.3), custom_call_target="tpu_custom_call" | custom-call | tf_op jit(solution)/shard_map/edges/pallas_call | solution.py:499
  4.3 2.6 %collective-permute-start = (bf16[3,3,64,128]{3,2,1,0:T(8,128)(2,1)}, bf16[3,3,64,128]{3,2,1,0:T(8,128)(2,1)S(1)}, u32[]{:S(2)}, u32[]{:S(2)}) collective-permute-start(bf16[3,3,64,128]{3,2,1,0:T(8,128)(2,1)} %get-tuple-element.26), channel_id=1, source_target_pairs={{0,8},{8,16},{16,24},{24,32},{32,40},{40,48},{48,56},{56,64},{64,7... | collective-permute-start | bytes 442376 | tf_op jit(solution)/shard_map/ppermute | solution.py:487
  6.9 0.7 collective-permute-start.1
  7.6 1.3 %collective-permute-start.3 = (bf16[3,2,64,128]{3,2,1,0:T(8,128)(2,1)}, bf16[3,2,64,128]{3,2,1,0:T(8,128)(2,1)S(1)}, u32[]{:S(2)}, u32[]{:S(2)}) collective-permute-start(bf16[3,2,64,128]{3,2,1,0:T(8,128)(2,1)} %get-tuple-element.28), channel_id=1, source_target_pairs={{1,0},{2,1},{3,2},{4,3},{5,4},{6,5},{7,6},{9,8},{10,9},{11,10},{12... | collective-permute-start | bytes 294920 | tf_op jit(solution)/shard_map/ppermute | solution.py:490
  8.9 4.0 %collective-permute-start.2 = (bf16[3,2,64,128]{3,2,1,0:T(8,128)(2,1)}, bf16[3,2,64,128]{3,2,1,0:T(8,128)(2,1)S(1)}, u32[]{:S(2)}, u32[]{:S(2)}) collective-permute-start(bf16[3,2,64,128]{3,2,1,0:T(8,128)(2,1)} %get-tuple-element.28), channel_id=1, source_target_pairs={{0,1},{1,2},{2,3},{3,4},{4,5},{5,6},{6,7},{8,9},{9,10},{10,11},{11... | collective-permute-start | bytes 294920 | tf_op jit(solution)/shard_map/ppermute | solution.py:489
  12.9 1.9 %spectra.1 = (bf16[32,256]{1,0:T(8,128)(2,1)}, bf16[32,32,256]{2,1,0:T(8,128)(2,1)}) custom-call(bf16[32,8,128]{2,1,0:T(8,128)(2,1)} %spectra_ref, s32[16]{0:T(128)} %wanted_ref.1), custom_call_target="tpu_custom_call" | custom-call | tf_op jit(solution)/shard_map/spectra/pallas_call | solution.py:511
  14.8 0.0 collective-permute-done.3.refs_4_
  14.8 0.0 copy-start.8
  14.8 0.0 collective-permute-done.2.refs_3_
  14.8 0.0 copy-start.9
  14.8 0.0 collective-permute-done.refs_1_
  14.8 0.0 copy-start.6
  14.9 0.0 collective-permute-done.1.refs_2_
  14.9 0.0 copy-start.7
  14.9 0.0 copy-start.10
  14.9 14.1 %all-to-all-start = ((bf16[32,32,256]{2,1,0:T(8,128)(2,1)}), bf16[32,32,256]{2,1,0:T(8,128)(2,1)}, u32[]{:S(2)}, u32[]{:S(2)}) async-start(bf16[32,32,256]{2,1,0:T(8,128)(2,1)} %get-tuple-element.38), calls=%async_computation | async-start | bytes 1048576 | tf_op jit(solution)/shard_map/all_to_all | solution.py:524
  28.9 0.0 copy-start.4
  29.0 0.0 copy-start.5
  29.0 0.0 copy-done.8
  29.0 0.0 copy-done.9
  29.0 0.0 copy-done.6
  29.0 0.0 copy-done.7
  29.0 0.0 copy-done.1
  29.0 0.0 copy-done.3
  29.0 11.7 %section_one_012.1 = (f32[3,32,64,128]{3,2,1,0:T(8,128)S(1)}, bf16[3,3,64,128]{3,2,1,0:T(8,128)(2,1)}, bf16[3,3,64,128]{3,2,1,0:T(8,128)(2,1)}, bf16[3,2,64,128]{3,2,1,0:T(8,128)(2,1)S(1)}) custom-call(f32[3,32,64,128]{3,2,1,0:T(8,128)} %refs_10_.3, bf16[3,3,64,128]{3,2,1,0:T(8,128)(2,1)} %copy-done.6, bf16[3,3,64,128]{3,2,1,0:T(8,128)(2,1)} %copy-done.7, ...), custom_call_target="tpu_custom_call" | custom-call | flops 60000000 | bytes 24000000 | tf_op jit(solution)/shard_map/section_one_012/pallas_call | solution.py:348
  40.8 1.3 %collective-permute-start.7 = (bf16[3,2,64,128]{3,2,1,0:T(8,128)(2,1)S(1)}, bf16[3,2,64,128]{3,2,1,0:T(8,128)(2,1)}, u32[]{:S(2)}, u32[]{:S(2)}) collective-permute-start(bf16[3,2,64,128]{3,2,1,0:T(8,128)(2,1)S(1)} %get-tuple-element.37), channel_id=1, source_target_pairs={{1,0},{2,1},{3,2},{4,3},{5,4},{6,5},{7,6},{9,8},{10,9},{11,10},{12... | collective-permute-start | bytes 294920 | tf_op jit(solution)/shard_map/ppermute | solution.py:490
  42.1 5.2 %collective-permute-start.6 = (bf16[3,2,64,128]{3,2,1,0:T(8,128)(2,1)S(1)}, bf16[3,2,64,128]{3,2,1,0:T(8,128)(2,1)}, u32[]{:S(2)}, u32[]{:S(2)}) collective-permute-start(bf16[3,2,64,128]{3,2,1,0:T(8,128)(2,1)S(1)} %get-tuple-element.37), channel_id=1, source_target_pairs={{0,1},{1,2},{2,3},{3,4},{4,5},{5,6},{6,7},{8,9},{9,10},{10,11},{11... | collective-permute-start | bytes 294920 | tf_op jit(solution)/shard_map/ppermute | solution.py:489
  47.3 1.9 %collective-permute-start.4 = (bf16[3,3,64,128]{3,2,1,0:T(8,128)(2,1)}, bf16[3,3,64,128]{3,2,1,0:T(8,128)(2,1)}, u32[]{:S(2)}, u32[]{:S(2)}) collective-permute-start(bf16[3,3,64,128]{3,2,1,0:T(8,128)(2,1)} %get-tuple-element.35), channel_id=1, source_target_pairs={{0,8},{8,16},{16,24},{24,32},{32,40},{40,48},{48,56},{56,64},{64,7... | collective-permute-start | bytes 442376 | tf_op jit(solution)/shard_map/ppermute | solution.py:487
  49.2 0.0 collective-permute-start.5
  49.2 0.0 copy-done.10
  49.2 0.9 copy.17
  50.1 0.6 copy.18
  50.8 0.9 copy.19.refs_12_
  51.7 0.0 all-to-all-done
  51.7 0.0 copy-done.4
  51.7 0.0 copy-done.5
  51.7 3.4 %gram_stored.1.known_ref = f32[2,8,32,1024]{3,2,1,0:T(8,128)S(1)} custom-call(f32[2,8,32,1024]{3,2,1,0:T(8,128)} %prior_ref.1, bf16[1024,256]{1,0:T(8,128)(2,1)} %bitcast.every_ref, bf16[32,256]{1,0:T(8,128)(2,1)S(1)} %copy-done.4, f32[1,256]{1,0:T(1,128)S(1)} %copy-done.5), custom_call_target="tpu_custom_call" | custom-call | flops 30000000 | bytes 12000000 | tf_op jit(solution)/shard_map/gram_stored/pallas_call | solution.py:539
  55.1 0.0 copy-start
  55.2 0.0 collective-permute-done.7.refs_4_
  55.2 0.0 collective-permute-done.6.refs_3_
  55.2 0.0 collective-permute-done.4.refs_1_
  55.2 0.0 collective-permute-done.5.refs_2_
  55.2 6.5 %section_two_0.1 = (f32[3,32,64,128]{3,2,1,0:T(8,128)}, f32[8,4,128]{2,1,0:T(4,128)S(1)}) custom-call(f32[3,32,64,128]{3,2,1,0:T(8,128)S(1)} %get-tuple-element.41.refs_0_, bf16[3,3,64,128]{3,2,1,0:T(8,128)(2,1)} %collective-permute-done.4.refs_1_, bf16[3,3,64,128]{3,2,1,0:T(8,128)(2,1)} %collective-permute-done.5.refs_2_, ...), custom_call_target="tpu_custom_call" | custom-call | flops 20000000 | bytes 8000000 | tf_op jit(solution)/shard_map/section_two_0/pallas_call | solution.py:348
  61.7 0.0 copy-done
  61.7 0.8 broadcast_in_dim.2
  62.5 19.2 %all-to-all-start.1 = ((bf16[256,4,128]{2,1,0:T(4,128)(2,1)}), bf16[256,4,128]{2,1,0:T(4,128)(2,1)}, u32[]{:S(2)}, u32[]{:S(2)}) async-start(bf16[256,4,128]{2,1,0:T(4,128)(2,1)} %bitcast.7), calls=%async_computation.1 | async-start | bytes 524288 | tf_op jit(solution)/shard_map/all_to_all | solution.py:579
  81.7 0.0 copy-start.2
  81.7 7.6 %section_two_12.1 = f32[3,32,64,128]{3,2,1,0:T(8,128)} custom-call(f32[3,32,64,128]{3,2,1,0:T(8,128)S(1)} %get-tuple-element.41.refs_0_, bf16[3,3,64,128]{3,2,1,0:T(8,128)(2,1)} %collective-permute-done.4.refs_1_, bf16[3,3,64,128]{3,2,1,0:T(8,128)(2,1)} %collective-permute-done.5.refs_2_, ...), custom_call_target="tpu_custom_call", output_to_operand_aliasing={{}: (11, {})} | custom-call | flops 40000000 | bytes 16000000 | tf_op jit(solution)/shard_map/section_two_12/pallas_call | solution.py:348
  89.4 7.0 %all-to-all-done.1.amp_ref = bf16[256,4,128]{2,1,0:T(4,128)(2,1)} async-done(((bf16[256,4,128]{2,1,0:T(4,128)(2,1)}), bf16[256,4,128]{2,1,0:T(4,128)(2,1)}, u32[]{:S(2)}, u32[]{:S(2)}) %all-to-all-start.1) | async-done | bytes 262176 | tf_op jit(solution)/shard_map/all_to_all | solution.py:579
  96.4 0.0 copy-done.2
  96.4 4.4 %gram_amplitudes.1 = f32[2,8,32,1024]{3,2,1,0:T(8,128)} custom-call(f32[2,8,32,1024]{3,2,1,0:T(8,128)} %copy-done, bf16[256,4,128]{2,1,0:T(4,128)(2,1)} %all-to-all-done.1.amp_ref, s32[1]{0:T(128)} %bitcast.5.where_ref, bf16[2,128,128]{2,1,0:T(8,128)(2,1)S(1)} %copy-done.2), custom_call_target="tpu_custom_call" | custom-call | tf_op jit(solution)/shard_map/gram_amplitudes/pallas_call | solution.py:588
  (2 shorter events, 0.0 us)
Async XLA Ops:
  0.6 28.4 %copy-start.1 = (bf16[384,256]{1,0:T(8,128)(2,1)S(1)}, bf16[384,256]{1,0:T(8,128)(2,1)}, u32[]{:S(2)}) copy-start(bf16[384,256]{1,0:T(8,128)(2,1)} %constant.17.clone.refs_9_) | copy-start | bytes 589828
  0.6 28.4 %copy-start.3 = (f32[3,3]{1,0:T(4,128)S(1)}, f32[3,3]{1,0:T(4,128)}, u32[]{:S(2)}) copy-start(f32[3,3]{1,0:T(4,128)} %refs_8_.5) | copy-start | bytes 112
  4.3 10.6 %collective-permute-start = (bf16[3,3,64,128]{3,2,1,0:T(8,128)(2,1)}, bf16[3,3,64,128]{3,2,1,0:T(8,128)(2,1)S(1)}, u32[]{:S(2)}, u32[]{:S(2)}) collective-permute-start(bf16[3,3,64,128]{3,2,1,0:T(8,128)(2,1)} %get-tuple-element.26), channel_id=1, source_target_pairs={{0,8},{8,16},{16,24},{24,32},{32,40},{40,48},{48,56},{56,64},{64,7... | collective-permute-start | bytes 442376 | tf_op jit(solution)/shard_map/ppermute | solution.py:487
  6.9 8.0 %collective-permute-start.1 = (bf16[3,3,64,128]{3,2,1,0:T(8,128)(2,1)}, bf16[3,3,64,128]{3,2,1,0:T(8,128)(2,1)S(1)}, u32[]{:S(2)}, u32[]{:S(2)}) collective-permute-start(bf16[3,3,64,128]{3,2,1,0:T(8,128)(2,1)} %get-tuple-element.27), channel_id=1, source_target_pairs={{8,0},{16,8},{24,16},{32,24},{40,32},{48,40},{56,48},{64,56},{72,6... | collective-permute-start | bytes 442376 | tf_op jit(solution)/shard_map/ppermute | solution.py:488
  7.6 7.2 %collective-permute-start.3 = (bf16[3,2,64,128]{3,2,1,0:T(8,128)(2,1)}, bf16[3,2,64,128]{3,2,1,0:T(8,128)(2,1)S(1)}, u32[]{:S(2)}, u32[]{:S(2)}) collective-permute-start(bf16[3,2,64,128]{3,2,1,0:T(8,128)(2,1)} %get-tuple-element.28), channel_id=1, source_target_pairs={{1,0},{2,1},{3,2},{4,3},{5,4},{6,5},{7,6},{9,8},{10,9},{11,10},{12... | collective-permute-start | bytes 294920 | tf_op jit(solution)/shard_map/ppermute | solution.py:490
  8.9 6.0 %collective-permute-start.2 = (bf16[3,2,64,128]{3,2,1,0:T(8,128)(2,1)}, bf16[3,2,64,128]{3,2,1,0:T(8,128)(2,1)S(1)}, u32[]{:S(2)}, u32[]{:S(2)}) collective-permute-start(bf16[3,2,64,128]{3,2,1,0:T(8,128)(2,1)} %get-tuple-element.28), channel_id=1, source_target_pairs={{0,1},{1,2},{2,3},{3,4},{4,5},{5,6},{6,7},{8,9},{9,10},{10,11},{11... | collective-permute-start | bytes 294920 | tf_op jit(solution)/shard_map/ppermute | solution.py:489
  14.8 14.2 %copy-start.8 = (bf16[3,2,64,128]{3,2,1,0:T(8,128)(2,1)}, bf16[3,2,64,128]{3,2,1,0:T(8,128)(2,1)S(1)}, u32[]{:S(2)}) copy-start(bf16[3,2,64,128]{3,2,1,0:T(8,128)(2,1)S(1)} %collective-permute-done.3.refs_4_) | copy-start | bytes 294916
  14.8 14.2 %copy-start.9 = (bf16[3,2,64,128]{3,2,1,0:T(8,128)(2,1)}, bf16[3,2,64,128]{3,2,1,0:T(8,128)(2,1)S(1)}, u32[]{:S(2)}) copy-start(bf16[3,2,64,128]{3,2,1,0:T(8,128)(2,1)S(1)} %collective-permute-done.2.refs_3_) | copy-start | bytes 294916
  14.8 14.2 %copy-start.6 = (bf16[3,3,64,128]{3,2,1,0:T(8,128)(2,1)}, bf16[3,3,64,128]{3,2,1,0:T(8,128)(2,1)S(1)}, u32[]{:S(2)}) copy-start(bf16[3,3,64,128]{3,2,1,0:T(8,128)(2,1)S(1)} %collective-permute-done.refs_1_) | copy-start | bytes 442372
  14.9 14.1 %copy-start.7 = (bf16[3,3,64,128]{3,2,1,0:T(8,128)(2,1)}, bf16[3,3,64,128]{3,2,1,0:T(8,128)(2,1)S(1)}, u32[]{:S(2)}) copy-start(bf16[3,3,64,128]{3,2,1,0:T(8,128)(2,1)S(1)} %collective-permute-done.1.refs_2_) | copy-start | bytes 442372
  14.9 34.3 %copy-start.10 = (s32[32]{0:T(128)S(1)}, s32[32]{0:T(128)}, u32[]{:S(2)}) copy-start(s32[32]{0:T(128)} %param.18) | copy-start | bytes 388
  14.9 36.8 %all-to-all-start = ((bf16[32,32,256]{2,1,0:T(8,128)(2,1)}), bf16[32,32,256]{2,1,0:T(8,128)(2,1)}, u32[]{:S(2)}, u32[]{:S(2)}) async-start(bf16[32,32,256]{2,1,0:T(8,128)(2,1)} %get-tuple-element.38), calls=%async_computation | async-start | bytes 1048576 | tf_op jit(solution)/shard_map/all_to_all | solution.py:524
  28.9 22.7 %copy-start.4 = (bf16[32,256]{1,0:T(8,128)(2,1)S(1)}, bf16[32,256]{1,0:T(8,128)(2,1)}, u32[]{:S(2)}) copy-start(bf16[32,256]{1,0:T(8,128)(2,1)} %get-tuple-element.39.own_ref) | copy-start | bytes 49156
  29.0 22.7 %copy-start.5 = (f32[1,256]{1,0:T(1,128)S(1)}, f32[1,256]{1,0:T(1,128)}, u32[]{:S(2)}) copy-start(f32[1,256]{1,0:T(1,128)} %constant.18.clone.ramp_ref) | copy-start | bytes 3076
  40.8 14.4 %collective-permute-start.7 = (bf16[3,2,64,128]{3,2,1,0:T(8,128)(2,1)S(1)}, bf16[3,2,64,128]{3,2,1,0:T(8,128)(2,1)}, u32[]{:S(2)}, u32[]{:S(2)}) collective-permute-start(bf16[3,2,64,128]{3,2,1,0:T(8,128)(2,1)S(1)} %get-tuple-element.37), channel_id=1, source_target_pairs={{1,0},{2,1},{3,2},{4,3},{5,4},{6,5},{7,6},{9,8},{10,9},{11,10},{12... | collective-permute-start | bytes 294920 | tf_op jit(solution)/shard_map/ppermute | solution.py:490
  42.1 13.1 %collective-permute-start.6 = (bf16[3,2,64,128]{3,2,1,0:T(8,128)(2,1)S(1)}, bf16[3,2,64,128]{3,2,1,0:T(8,128)(2,1)}, u32[]{:S(2)}, u32[]{:S(2)}) collective-permute-start(bf16[3,2,64,128]{3,2,1,0:T(8,128)(2,1)S(1)} %get-tuple-element.37), channel_id=1, source_target_pairs={{0,1},{1,2},{2,3},{3,4},{4,5},{5,6},{6,7},{8,9},{9,10},{10,11},{11... | collective-permute-start | bytes 294920 | tf_op jit(solution)/shard_map/ppermute | solution.py:489
  47.3 7.9 %collective-permute-start.4 = (bf16[3,3,64,128]{3,2,1,0:T(8,128)(2,1)}, bf16[3,3,64,128]{3,2,1,0:T(8,128)(2,1)}, u32[]{:S(2)}, u32[]{:S(2)}) collective-permute-start(bf16[3,3,64,128]{3,2,1,0:T(8,128)(2,1)} %get-tuple-element.35), channel_id=1, source_target_pairs={{0,8},{8,16},{16,24},{24,32},{32,40},{40,48},{48,56},{56,64},{64,7... | collective-permute-start | bytes 442376 | tf_op jit(solution)/shard_map/ppermute | solution.py:487
  49.2 6.0 %collective-permute-start.5 = (bf16[3,3,64,128]{3,2,1,0:T(8,128)(2,1)}, bf16[3,3,64,128]{3,2,1,0:T(8,128)(2,1)}, u32[]{:S(2)}, u32[]{:S(2)}) collective-permute-start(bf16[3,3,64,128]{3,2,1,0:T(8,128)(2,1)} %get-tuple-element.36), channel_id=1, source_target_pairs={{8,0},{16,8},{24,16},{32,24},{40,32},{48,40},{56,48},{64,56},{72,6... | collective-permute-start | bytes 442376 | tf_op jit(solution)/shard_map/ppermute | solution.py:488
  55.1 6.5 %copy-start = (f32[2,8,32,1024]{3,2,1,0:T(8,128)}, f32[2,8,32,1024]{3,2,1,0:T(8,128)S(1)}, u32[]{:S(2)}) copy-start(f32[2,8,32,1024]{3,2,1,0:T(8,128)S(1)} %gram_stored.1.known_ref) | copy-start | bytes 6291460
  62.5 33.9 %all-to-all-start.1 = ((bf16[256,4,128]{2,1,0:T(4,128)(2,1)}), bf16[256,4,128]{2,1,0:T(4,128)(2,1)}, u32[]{:S(2)}, u32[]{:S(2)}) async-start(bf16[256,4,128]{2,1,0:T(4,128)(2,1)} %bitcast.7), calls=%async_computation.1 | async-start | bytes 524288 | tf_op jit(solution)/shard_map/all_to_all | solution.py:579
  81.7 14.6 %copy-start.2 = (bf16[2,128,128]{2,1,0:T(8,128)(2,1)S(1)}, bf16[2,128,128]{2,1,0:T(8,128)(2,1)}, u32[]{:S(2)}) copy-start(bf16[2,128,128]{2,1,0:T(8,128)(2,1)} %constant.19.clone.rep_ref) | copy-start | bytes 196612

commit v7 on v6

--- a/solution.py
+++ b/solution.py
@@ -63,7 +63,12 @@
     return lax.div(lax.broadcasted_iota(jnp.int32, shape, len(shape) - 1), 8)
 
 
-def edges_kernel(flow_ref, cells_ref, low_ref, high_ref):
+def ends_kernel(first_ref, last_ref, low_ref, high_ref):
+    low_ref[0] = first_ref[0, 0:3].astype(BF16)
+    high_ref[0] = last_ref[0, 1:4].astype(BF16)
+
+
+def edges_kernel(flow_ref, cells_ref):
     stations, normal = flow_ref.shape[1:3]
     lane = edge_lanes((16, LANES))
     for half in range(stations // 16):
@@ -74,8 +79,6 @@
                 moved = pltpu.roll(flow_ref[0, 16 * half + s, rows, :], (3 + 8 * s) % LANES, 1)
                 packed = jnp.where(lane == s, moved, packed)
             cells_ref[0, half, rows, :] = packed.astype(BF16)
-    low_ref[0] = flow_ref[0, 0:3].astype(BF16)
-    high_ref[0] = flow_ref[0, stations - 3 : stations].astype(BF16)
 
 
 def section_kernel(*refs, second, profile, carried, quantities):
@@ -496,14 +499,30 @@
     def per_quantity(shape):
         return pl.BlockSpec((1,) + shape.shape[1:], lambda q: (q, 0, 0, 0))
 
-    edge, low, high = pl.pallas_call(
+    four = (1, 4, normal, cells)
+    low, high = pl.pallas_call(
+        ends_kernel,
+        grid=(count,),
+        out_shape=(ends_shape, ends_shape),
+        in_specs=[
+            pl.BlockSpec(four, lambda q: (q, 0, 0, 0)),
+            pl.BlockSpec(four, lambda q: (q, stations // 4 - 1, 0, 0)),
+        ],
+        out_specs=(per_quantity(ends_shape), per_quantity(ends_shape)),
+        name="ends",
+    )(flow_state, flow_state)
+    flow_edges, _ = lax.optimization_barrier((flow_state, low))
+    edge = pl.pallas_call(
         edges_kernel,
         grid=(count,),
-        out_shape=(edge_shape, ends_shape, ends_shape),
+        out_shape=edge_shape,
         in_specs=[per_quantity(flow_state)],
-        out_specs=(per_quantity(edge_shape), per_quantity(ends_shape), per_quantity(ends_shape)),
+        out_specs=per_quantity(edge_shape),
         name="edges",
-    )(flow_state)
+        cost_estimate=pl.CostEstimate(
+            flops=10000000, transcendentals=0, bytes_accessed=12000000
+        ),
+    )(flow_edges)
     halos = exchange(low, high, edge)
 
     width = bands * 2 * segs
@@ -524,8 +543,6 @@
     every = lax.all_to_all(send, "span", 0, 0, tiled=True).reshape(span_n * stations, width)
 
     (section_one, low, high, edge) = section(flow_state, halos, fields, mixing, table)
-    halos = exchange(low, high, edge)
-
     ramp = np.tile((np.arange(segs, dtype=np.float32) + 1) / segs, 2 * bands)[None]
     tiles = 4
     tile = span_n * stations // tiles
@@ -539,7 +556,7 @@
     known = pl.pallas_call(
         stored_kernel,
         grid=(tiles,),
-        out_shape=gram_shape,
+        out_shape=pltpu.HBM(prior_gram_blocks.shape, F32),
         in_specs=[
             gram_block,
             pl.BlockSpec((tile, width), lambda t: (t, 0)),
@@ -559,7 +576,9 @@
         packed,
         ramp,
     )
-    halos, known = lax.optimization_barrier((halos, known))
+    edge, known = lax.optimization_barrier((edge, known))
+    halos = exchange(low, high, edge)
+
 
     te_local = te_index - chord_pos * cells
     band_table = band_response.reshape(normal, 2, chord_n, bands).transpose(0, 2, 1, 3)

time: 101 us -> 106 us (1.050)
  Pallas kernels: 39.2 us -> 42.9 us
  waiting for transfers between devices: 7.03 us -> 10.2 us
  starting transfers between devices: 50.3 us -> 48.8 us
    pallas_call x2 -> x3, Pallas kernels: 7.05 us -> 10.8 us  [the longest x1 4.61 us: shards(): pl.pallas_call(stored_kernel, grid=(tiles,), out_shape=pltpu.HBM(prior_gr...]
    all_to_all x1, waiting for transfers between devices: 0.01 us -> 3.12 us  [shards(): lax.all_to_all(send, 'span', 0, 0, tiled=True)]
    all_to_all x1, starting transfers between devices: 19.2 us -> 17.8 us  [shards(): lax.all_to_all(amps.reshape((span_n * chord_n,) + amps.shape[2:]), ('span...]
  transfers between devices with their start and end apart: 10 -> 10, of which waited for: 1 -> 2; matrix products, arithmetic and copies ran while one was open for 2% -> 2% of each run, Pallas kernels for 25% -> 28%
where the time goes in v7:
time: 106 us; the launch traced here: 105 us
  starting transfers between devices  48.8 us (46%)
  Pallas kernels  42.9 us (40%)
  waiting for transfers between devices  10.2 us (10%)
  local copies, waits for them, and re-layouts  2.46 us (2%)
    pallas_call x3, Pallas kernels, section(): pl.pallas_call(functools.partial(section_kernel, second=second, profile=p...  25.7 us
    all_to_all x1, starting transfers between devices, shards(): lax.all_to_all(amps.reshape((span_n * chord_n,) + amps.shape[2:]), ('span...  17.8 us
    all_to_all x1, starting transfers between devices, shards(): lax.all_to_all(send, 'span', 0, 0, tiled=True)  14 us
    ppermute x2, starting transfers between devices, exchange(): lax.ppermute(edge, 'chord', forward)  9.33 us
    all_to_all x1, waiting for transfers between devices, shards(): lax.all_to_all(amps.reshape((span_n * chord_n,) + amps.shape[2:]), ('span...  7.01 us
    pallas_call x1, Pallas kernels, shards(): pl.pallas_call(stored_kernel, grid=(tiles,), out_shape=pltpu.HBM(prior_gr...  4.61 us
    pallas_call x1, Pallas kernels, shards(): pl.pallas_call(amplitude_kernel, grid=(tiles,), out_shape=gram_shape, in_...  4.41 us
    ppermute x2, starting transfers between devices, exchange(): lax.ppermute(high, 'span', up)  4.38 us
  transfers between devices with their start and end apart: 10, of which 2 were waited for; matrix products, arithmetic and copies ran while one was open for 2% of the time, Pallas kernels for 28%

profile of v7, /device:TPU:1, one launch (start us, length us, event | category | flops | bytes accessed | tf_op | source)
XLA Modules:
  0.0 105.2 jit_solution(6436394156805497210)
XLA Ops:
  0.6 2.7 %ends.1 = (bf16[3,3,64,128]{3,2,1,0:T(8,128)(2,1)}, bf16[3,3,64,128]{3,2,1,0:T(8,128)(2,1)}) custom-call(f32[3,32,64,128]{3,2,1,0:T(8,128)} %refs_10_.3, f32[3,32,64,128]{3,2,1,0:T(8,128)} %refs_10_.3), custom_call_target="tpu_custom_call" | custom-call | tf_op jit(solution)/shard_map/ends/pallas_call | solution.py:503
  3.3 0.0 copy-start
  3.3 0.0 copy-start.2
  3.3 2.7 %collective-permute-start = (bf16[3,3,64,128]{3,2,1,0:T(8,128)(2,1)}, bf16[3,3,64,128]{3,2,1,0:T(8,128)(2,1)S(1)}, u32[]{:S(2)}, u32[]{:S(2)}) collective-permute-start(bf16[3,3,64,128]{3,2,1,0:T(8,128)(2,1)} %get-tuple-element.23), channel_id=1, source_target_pairs={{0,8},{8,16},{16,24},{24,32},{32,40},{40,48},{48,56},{56,64},{64,7... | collective-permute-start | bytes 442376 | tf_op jit(solution)/shard_map/ppermute | solution.py:490
  6.0 0.7 collective-permute-start.1
  6.8 3.5 %edges.1 = bf16[3,2,64,128]{3,2,1,0:T(8,128)(2,1)} custom-call(f32[3,32,64,128]{3,2,1,0:T(8,128)} %refs_10_.3), custom_call_target="tpu_custom_call" | custom-call | flops 10000000 | bytes 12000000 | tf_op jit(solution)/shard_map/edges/pallas_call | solution.py:515
  10.3 1.3 %collective-permute-start.3 = (bf16[3,2,64,128]{3,2,1,0:T(8,128)(2,1)}, bf16[3,2,64,128]{3,2,1,0:T(8,128)(2,1)S(1)}, u32[]{:S(2)}, u32[]{:S(2)}) collective-permute-start(bf16[3,2,64,128]{3,2,1,0:T(8,128)(2,1)} %edges.1), channel_id=1, source_target_pairs={{1,0},{2,1},{3,2},{4,3},{5,4},{6,5},{7,6},{9,8},{10,9},{11,10},{12... | collective-permute-start | bytes 294920 | tf_op jit(solution)/shard_map/ppermute | solution.py:493
  11.6 4.0 %collective-permute-start.2 = (bf16[3,2,64,128]{3,2,1,0:T(8,128)(2,1)}, bf16[3,2,64,128]{3,2,1,0:T(8,128)(2,1)S(1)}, u32[]{:S(2)}, u32[]{:S(2)}) collective-permute-start(bf16[3,2,64,128]{3,2,1,0:T(8,128)(2,1)} %edges.1), channel_id=1, source_target_pairs={{0,1},{1,2},{2,3},{3,4},{4,5},{5,6},{6,7},{8,9},{9,10},{10,11},{11... | collective-permute-start | bytes 294920 | tf_op jit(solution)/shard_map/ppermute | solution.py:492
  15.6 1.9 %spectra.1 = (bf16[32,256]{1,0:T(8,128)(2,1)}, bf16[32,32,256]{2,1,0:T(8,128)(2,1)}) custom-call(bf16[32,8,128]{2,1,0:T(8,128)(2,1)} %spectra_ref, s32[16]{0:T(128)} %wanted_ref.1), custom_call_target="tpu_custom_call" | custom-call | tf_op jit(solution)/shard_map/spectra/pallas_call | solution.py:530
  17.5 0.0 collective-permute-done.3.refs_4_
  17.5 0.0 copy-start.7
  17.5 0.0 collective-permute-done.2.refs_3_
  17.5 0.0 copy-start.8
  17.5 0.0 collective-permute-done.refs_1_
  17.5 0.0 copy-start.5
  17.5 0.0 collective-permute-done.1.refs_2_
  17.6 0.0 copy-start.6
  17.6 0.0 copy-start.3
  17.6 0.0 copy-start.4
  17.6 14.0 %all-to-all-start = ((bf16[32,32,256]{2,1,0:T(8,128)(2,1)}), bf16[32,32,256]{2,1,0:T(8,128)(2,1)}, u32[]{:S(2)}, u32[]{:S(2)}) async-start(bf16[32,32,256]{2,1,0:T(8,128)(2,1)} %get-tuple-element.33), calls=%async_computation | async-start | bytes 1048576 | tf_op jit(solution)/shard_map/all_to_all | solution.py:543
  31.6 0.0 copy-done.7
  31.7 0.0 copy-done.8
  31.7 0.0 copy-done.5
  31.7 0.0 copy-done.6
  31.7 0.0 copy-done
  31.7 0.0 copy-done.2
  31.7 11.8 %section_one_012.1 = (f32[3,32,64,128]{3,2,1,0:T(8,128)S(1)}, bf16[3,3,64,128]{3,2,1,0:T(8,128)(2,1)}, bf16[3,3,64,128]{3,2,1,0:T(8,128)(2,1)}, bf16[3,2,64,128]{3,2,1,0:T(8,128)(2,1)S(1)}) custom-call(f32[3,32,64,128]{3,2,1,0:T(8,128)} %refs_10_.3, bf16[3,3,64,128]{3,2,1,0:T(8,128)(2,1)} %copy-done.5, bf16[3,3,64,128]{3,2,1,0:T(8,128)(2,1)} %copy-done.6, ...), custom_call_target="tpu_custom_call" | custom-call | flops 60000000 | bytes 24000000 | tf_op jit(solution)/shard_map/section_one_012/pallas_call | solution.py:351
  43.5 0.0 copy-start.10
  43.5 0.0 copy-start.9
  43.5 1.7 %collective-permute-start.4 = (bf16[3,3,64,128]{3,2,1,0:T(8,128)(2,1)}, bf16[3,3,64,128]{3,2,1,0:T(8,128)(2,1)}, u32[]{:S(2)}, u32[]{:S(2)}) collective-permute-start(bf16[3,3,64,128]{3,2,1,0:T(8,128)(2,1)} %get-tuple-element.37), channel_id=1, source_target_pairs={{0,8},{8,16},{16,24},{24,32},{32,40},{40,48},{48,56},{56,64},{64,7... | collective-permute-start | bytes 442376 | tf_op jit(solution)/shard_map/ppermute | solution.py:490
  45.2 0.0 collective-permute-start.5
  45.2 3.1 %all-to-all-done = bf16[32,32,256]{2,1,0:T(8,128)(2,1)} async-done(((bf16[32,32,256]{2,1,0:T(8,128)(2,1)}), bf16[32,32,256]{2,1,0:T(8,128)(2,1)}, u32[]{:S(2)}, u32[]{:S(2)}) %all-to-all-start) | async-done | bytes 524320 | tf_op jit(solution)/shard_map/all_to_all | solution.py:543
  48.3 0.0 copy-done.3
  48.3 0.0 copy-done.4
  48.3 4.6 %gram_stored.1.known_ref = f32[2,8,32,1024]{3,2,1,0:T(8,128)} custom-call(f32[2,8,32,1024]{3,2,1,0:T(8,128)} %prior_ref.1, bf16[1024,256]{1,0:T(8,128)(2,1)} %bitcast.every_ref, bf16[32,256]{1,0:T(8,128)(2,1)S(1)} %copy-done.3, f32[1,256]{1,0:T(1,128)S(1)} %copy-done.4), custom_call_target="tpu_custom_call" | custom-call | flops 30000000 | bytes 12000000 | tf_op jit(solution)/shard_map/gram_stored/pallas_call | solution.py:556
  52.9 1.3 %collective-permute-start.7 = (bf16[3,2,64,128]{3,2,1,0:T(8,128)(2,1)S(1)}, bf16[3,2,64,128]{3,2,1,0:T(8,128)(2,1)}, u32[]{:S(2)}, u32[]{:S(2)}) collective-permute-start(bf16[3,2,64,128]{3,2,1,0:T(8,128)(2,1)S(1)} %get-tuple-element.39), channel_id=1, source_target_pairs={{1,0},{2,1},{3,2},{4,3},{5,4},{6,5},{7,6},{9,8},{10,9},{11,10},{12... | collective-permute-start | bytes 294920 | tf_op jit(solution)/shard_map/ppermute | solution.py:493
  54.2 5.3 %collective-permute-start.6 = (bf16[3,2,64,128]{3,2,1,0:T(8,128)(2,1)S(1)}, bf16[3,2,64,128]{3,2,1,0:T(8,128)(2,1)}, u32[]{:S(2)}, u32[]{:S(2)}) collective-permute-start(bf16[3,2,64,128]{3,2,1,0:T(8,128)(2,1)S(1)} %get-tuple-element.39), channel_id=1, source_target_pairs={{0,1},{1,2},{2,3},{3,4},{4,5},{5,6},{6,7},{8,9},{9,10},{10,11},{11... | collective-permute-start | bytes 294920 | tf_op jit(solution)/shard_map/ppermute | solution.py:492
  59.6 0.0 copy-done.10
  59.6 0.0 copy-done.9
  59.6 0.7 copy.17
  60.3 0.8 copy.18
  61.1 0.1 copy.19.refs_12_
  61.2 0.0 collective-permute-done.4.refs_1_
  61.2 0.0 collective-permute-done.5.refs_2_
  61.2 0.0 collective-permute-done.7.refs_4_
  61.2 0.0 collective-permute-done.6.refs_3_
  61.3 6.3 %section_two_0.1 = (f32[3,32,64,128]{3,2,1,0:T(8,128)}, f32[8,4,128]{2,1,0:T(4,128)S(1)}) custom-call(f32[3,32,64,128]{3,2,1,0:T(8,128)S(1)} %get-tuple-element.36.refs_0_, bf16[3,3,64,128]{3,2,1,0:T(8,128)(2,1)} %collective-permute-done.4.refs_1_, bf16[3,3,64,128]{3,2,1,0:T(8,128)(2,1)} %collective-permute-done.5.refs_2_, ...), custom_call_target="tpu_custom_call" | custom-call | flops 20000000 | bytes 8000000 | tf_op jit(solution)/shard_map/section_two_0/pallas_call | solution.py:351
  67.6 0.8 broadcast_in_dim.2
  68.4 17.8 %all-to-all-start.1 = ((bf16[256,4,128]{2,1,0:T(4,128)(2,1)}), bf16[256,4,128]{2,1,0:T(4,128)(2,1)}, u32[]{:S(2)}, u32[]{:S(2)}) async-start(bf16[256,4,128]{2,1,0:T(4,128)(2,1)} %bitcast.7), calls=%async_computation.1 | async-start | bytes 524288 | tf_op jit(solution)/shard_map/all_to_all | solution.py:598
  86.2 0.0 copy-start.1
  86.2 7.6 %section_two_12.1 = f32[3,32,64,128]{3,2,1,0:T(8,128)} custom-call(f32[3,32,64,128]{3,2,1,0:T(8,128)S(1)} %get-tuple-element.36.refs_0_, bf16[3,3,64,128]{3,2,1,0:T(8,128)(2,1)} %collective-permute-done.4.refs_1_, bf16[3,3,64,128]{3,2,1,0:T(8,128)(2,1)} %collective-permute-done.5.refs_2_, ...), custom_call_target="tpu_custom_call", output_to_operand_aliasing={{}: (11, {})} | custom-call | flops 40000000 | bytes 16000000 | tf_op jit(solution)/shard_map/section_two_12/pallas_call | solution.py:351
  93.8 7.0 %all-to-all-done.1.amp_ref = bf16[256,4,128]{2,1,0:T(4,128)(2,1)} async-done(((bf16[256,4,128]{2,1,0:T(4,128)(2,1)}), bf16[256,4,128]{2,1,0:T(4,128)(2,1)}, u32[]{:S(2)}, u32[]{:S(2)}) %all-to-all-start.1) | async-done | bytes 262176 | tf_op jit(solution)/shard_map/all_to_all | solution.py:598
  100.8 0.0 copy-done.1
  100.8 4.4 %gram_amplitudes.1 = f32[2,8,32,1024]{3,2,1,0:T(8,128)} custom-call(f32[2,8,32,1024]{3,2,1,0:T(8,128)} %gram_stored.1.known_ref, bf16[256,4,128]{2,1,0:T(4,128)(2,1)} %all-to-all-done.1.amp_ref, s32[1]{0:T(128)} %bitcast.5.where_ref, bf16[2,128,128]{2,1,0:T(8,128)(2,1)S(1)} %copy-done.1), custom_call_target="tpu_custom_call" | custom-call | tf_op jit(solution)/shard_map/gram_amplitudes/pallas_call | solution.py:607
  (2 shorter events, 0.0 us)
Async XLA Ops:
  3.3 28.3 %copy-start = (bf16[384,256]{1,0:T(8,128)(2,1)S(1)}, bf16[384,256]{1,0:T(8,128)(2,1)}, u32[]{:S(2)}) copy-start(bf16[384,256]{1,0:T(8,128)(2,1)} %constant.17.clone.refs_9_) | copy-start | bytes 589828
  3.3 28.3 %copy-start.2 = (f32[3,3]{1,0:T(4,128)S(1)}, f32[3,3]{1,0:T(4,128)}, u32[]{:S(2)}) copy-start(f32[3,3]{1,0:T(4,128)} %refs_8_.5) | copy-start | bytes 112
  3.3 14.2 %collective-permute-start = (bf16[3,3,64,128]{3,2,1,0:T(8,128)(2,1)}, bf16[3,3,64,128]{3,2,1,0:T(8,128)(2,1)S(1)}, u32[]{:S(2)}, u32[]{:S(2)}) collective-permute-start(bf16[3,3,64,128]{3,2,1,0:T(8,128)(2,1)} %get-tuple-element.23), channel_id=1, source_target_pairs={{0,8},{8,16},{16,24},{24,32},{32,40},{40,48},{48,56},{56,64},{64,7... | collective-permute-start | bytes 442376 | tf_op jit(solution)/shard_map/ppermute | solution.py:490
  6.0 11.5 %collective-permute-start.1 = (bf16[3,3,64,128]{3,2,1,0:T(8,128)(2,1)}, bf16[3,3,64,128]{3,2,1,0:T(8,128)(2,1)S(1)}, u32[]{:S(2)}, u32[]{:S(2)}) collective-permute-start(bf16[3,3,64,128]{3,2,1,0:T(8,128)(2,1)} %get-tuple-element.24), channel_id=1, source_target_pairs={{8,0},{16,8},{24,16},{32,24},{40,32},{48,40},{56,48},{64,56},{72,6... | collective-permute-start | bytes 442376 | tf_op jit(solution)/shard_map/ppermute | solution.py:491
  10.3 7.2 %collective-permute-start.3 = (bf16[3,2,64,128]{3,2,1,0:T(8,128)(2,1)}, bf16[3,2,64,128]{3,2,1,0:T(8,128)(2,1)S(1)}, u32[]{:S(2)}, u32[]{:S(2)}) collective-permute-start(bf16[3,2,64,128]{3,2,1,0:T(8,128)(2,1)} %edges.1), channel_id=1, source_target_pairs={{1,0},{2,1},{3,2},{4,3},{5,4},{6,5},{7,6},{9,8},{10,9},{11,10},{12... | collective-permute-start | bytes 294920 | tf_op jit(solution)/shard_map/ppermute | solution.py:493
  11.6 6.0 %collective-permute-start.2 = (bf16[3,2,64,128]{3,2,1,0:T(8,128)(2,1)}, bf16[3,2,64,128]{3,2,1,0:T(8,128)(2,1)S(1)}, u32[]{:S(2)}, u32[]{:S(2)}) collective-permute-start(bf16[3,2,64,128]{3,2,1,0:T(8,128)(2,1)} %edges.1), channel_id=1, source_target_pairs={{0,1},{1,2},{2,3},{3,4},{4,5},{5,6},{6,7},{8,9},{9,10},{10,11},{11... | collective-permute-start | bytes 294920 | tf_op jit(solution)/shard_map/ppermute | solution.py:492
  17.5 14.1 %copy-start.7 = (bf16[3,2,64,128]{3,2,1,0:T(8,128)(2,1)}, bf16[3,2,64,128]{3,2,1,0:T(8,128)(2,1)S(1)}, u32[]{:S(2)}) copy-start(bf16[3,2,64,128]{3,2,1,0:T(8,128)(2,1)S(1)} %collective-permute-done.3.refs_4_) | copy-start | bytes 294916
  17.5 14.1 %copy-start.8 = (bf16[3,2,64,128]{3,2,1,0:T(8,128)(2,1)}, bf16[3,2,64,128]{3,2,1,0:T(8,128)(2,1)S(1)}, u32[]{:S(2)}) copy-start(bf16[3,2,64,128]{3,2,1,0:T(8,128)(2,1)S(1)} %collective-permute-done.2.refs_3_) | copy-start | bytes 294916
  17.5 14.1 %copy-start.5 = (bf16[3,3,64,128]{3,2,1,0:T(8,128)(2,1)}, bf16[3,3,64,128]{3,2,1,0:T(8,128)(2,1)S(1)}, u32[]{:S(2)}) copy-start(bf16[3,3,64,128]{3,2,1,0:T(8,128)(2,1)S(1)} %collective-permute-done.refs_1_) | copy-start | bytes 442372
  17.6 14.1 %copy-start.6 = (bf16[3,3,64,128]{3,2,1,0:T(8,128)(2,1)}, bf16[3,3,64,128]{3,2,1,0:T(8,128)(2,1)S(1)}, u32[]{:S(2)}) copy-start(bf16[3,3,64,128]{3,2,1,0:T(8,128)(2,1)S(1)} %collective-permute-done.1.refs_2_) | copy-start | bytes 442372
  17.6 30.8 %copy-start.3 = (bf16[32,256]{1,0:T(8,128)(2,1)S(1)}, bf16[32,256]{1,0:T(8,128)(2,1)}, u32[]{:S(2)}) copy-start(bf16[32,256]{1,0:T(8,128)(2,1)} %get-tuple-element.34.own_ref) | copy-start | bytes 49156
  17.6 30.8 %copy-start.4 = (f32[1,256]{1,0:T(1,128)S(1)}, f32[1,256]{1,0:T(1,128)}, u32[]{:S(2)}) copy-start(f32[1,256]{1,0:T(1,128)} %constant.18.clone.ramp_ref) | copy-start | bytes 3076
  17.6 30.7 %all-to-all-start = ((bf16[32,32,256]{2,1,0:T(8,128)(2,1)}), bf16[32,32,256]{2,1,0:T(8,128)(2,1)}, u32[]{:S(2)}, u32[]{:S(2)}) async-start(bf16[32,32,256]{2,1,0:T(8,128)(2,1)} %get-tuple-element.33), calls=%async_computation | async-start | bytes 1048576 | tf_op jit(solution)/shard_map/all_to_all | solution.py:543
  43.5 16.1 %copy-start.10 = (s32[32]{0:T(128)S(1)}, s32[32]{0:T(128)}, u32[]{:S(2)}) copy-start(s32[32]{0:T(128)} %param.18) | copy-start | bytes 388
  43.5 16.1 %copy-start.9 = (f32[64,2,64]{2,1,0:T(2,128)S(1)}, f32[64,2,64]{2,1,0:T(2,128)}, u32[]{:S(2)}) copy-start(f32[64,2,64]{2,1,0:T(2,128)} %param.19) | copy-start | bytes 98308
  43.5 17.7 %collective-permute-start.4 = (bf16[3,3,64,128]{3,2,1,0:T(8,128)(2,1)}, bf16[3,3,64,128]{3,2,1,0:T(8,128)(2,1)}, u32[]{:S(2)}, u32[]{:S(2)}) collective-permute-start(bf16[3,3,64,128]{3,2,1,0:T(8,128)(2,1)} %get-tuple-element.37), channel_id=1, source_target_pairs={{0,8},{8,16},{16,24},{24,32},{32,40},{40,48},{48,56},{56,64},{64,7... | collective-permute-start | bytes 442376 | tf_op jit(solution)/shard_map/ppermute | solution.py:490
  45.2 16.0 %collective-permute-start.5 = (bf16[3,3,64,128]{3,2,1,0:T(8,128)(2,1)}, bf16[3,3,64,128]{3,2,1,0:T(8,128)(2,1)}, u32[]{:S(2)}, u32[]{:S(2)}) collective-permute-start(bf16[3,3,64,128]{3,2,1,0:T(8,128)(2,1)} %get-tuple-element.38), channel_id=1, source_target_pairs={{8,0},{16,8},{24,16},{32,24},{40,32},{48,40},{56,48},{64,56},{72,6... | collective-permute-start | bytes 442376 | tf_op jit(solution)/shard_map/ppermute | solution.py:491
  52.9 8.3 %collective-permute-start.7 = (bf16[3,2,64,128]{3,2,1,0:T(8,128)(2,1)S(1)}, bf16[3,2,64,128]{3,2,1,0:T(8,128)(2,1)}, u32[]{:S(2)}, u32[]{:S(2)}) collective-permute-start(bf16[3,2,64,128]{3,2,1,0:T(8,128)(2,1)S(1)} %get-tuple-element.39), channel_id=1, source_target_pairs={{1,0},{2,1},{3,2},{4,3},{5,4},{6,5},{7,6},{9,8},{10,9},{11,10},{12... | collective-permute-start | bytes 294920 | tf_op jit(solution)/shard_map/ppermute | solution.py:493
  54.2 7.0 %collective-permute-start.6 = (bf16[3,2,64,128]{3,2,1,0:T(8,128)(2,1)S(1)}, bf16[3,2,64,128]{3,2,1,0:T(8,128)(2,1)}, u32[]{:S(2)}, u32[]{:S(2)}) collective-permute-start(bf16[3,2,64,128]{3,2,1,0:T(8,128)(2,1)S(1)} %get-tuple-element.39), channel_id=1, source_target_pairs={{0,1},{1,2},{2,3},{3,4},{4,5},{5,6},{6,7},{8,9},{9,10},{10,11},{11... | collective-permute-start | bytes 294920 | tf_op jit(solution)/shard_map/ppermute | solution.py:492
  68.4 32.4 %all-to-all-start.1 = ((bf16[256,4,128]{2,1,0:T(4,128)(2,1)}), bf16[256,4,128]{2,1,0:T(4,128)(2,1)}, u32[]{:S(2)}, u32[]{:S(2)}) async-start(bf16[256,4,128]{2,1,0:T(4,128)(2,1)} %bitcast.7), calls=%async_computation.1 | async-start | bytes 524288 | tf_op jit(solution)/shard_map/all_to_all | solution.py:598
  86.2 14.6 %copy-start.1 = (bf16[2,128,128]{2,1,0:T(8,128)(2,1)S(1)}, bf16[2,128,128]{2,1,0:T(8,128)(2,1)}, u32[]{:S(2)}) copy-start(bf16[2,128,128]{2,1,0:T(8,128)(2,1)} %constant.19.clone.rep_ref) | copy-start | bytes 196612

commit v8 on v6

--- a/solution.py
+++ b/solution.py
@@ -266,8 +266,9 @@
                 shift = (16 * (u - j)) % LANES
                 moved = pltpu.roll(taken, shift, 1) if shift else taken
                 pieces[j] = jnp.where(lane4 == u, moved, pieces[j])
-        for j in range(8):
-            amp_out[j] = pieces[j]
+        sent = jnp.stack(pieces).astype(BF16)
+        for d in range(amp_out.shape[0]):
+            amp_out[d] = sent
     if not second:
         cells_out[...] = cells[...].astype(BF16)
         low_out[...] = result[:, 0:3].astype(BF16)
@@ -291,6 +292,7 @@
     te_local=None,
     band_table=None,
     onto=None,
+    receivers=1,
 ):
     total, stations, normal, _ = state.shape
     count = len(quantities)
@@ -309,7 +311,7 @@
     if profile:
         args += [te_local, band_table]
         specs += [smem, vmem]
-        shapes.append(jax.ShapeDtypeStruct((8, 4, LANES), F32))
+        shapes.append(jax.ShapeDtypeStruct((receivers, 8, 4, LANES), BF16))
     if carried:
         aliases = {len(args): 0}
         args.append(onto)
@@ -574,8 +576,8 @@
         flow=flow_state,
         te_local=te_local,
         band_table=band_table,
+        receivers=span_n,
     )
-    amps = jnp.broadcast_to(amps.astype(BF16)[None], (span_n,) + amps.shape)
     amps = lax.all_to_all(
         amps.reshape((span_n * chord_n,) + amps.shape[2:]), ("span", "chord"), 0, 0, tiled=True
     )

time: 101 us -> 101 us (level)
  no operation moved by 1% of the time
where the time goes in v8:
time: 101 us
  starting transfers between devices  50.3 us (50%)
  Pallas kernels  39.2 us (39%)
  waiting for transfers between devices  7.03 us (7%)
  local copies, waits for them, and re-layouts  3.22 us (3%)
    pallas_call x3, Pallas kernels, section(): pl.pallas_call(functools.partial(section_kernel, second=second, profile=p...  25.8 us
    all_to_all x1, starting transfers between devices, shards(): lax.all_to_all(amps.reshape((span_n * chord_n,) + amps.shape[2:]), ('span...  19.2 us
    all_to_all x1, starting transfers between devices, shards(): lax.all_to_all(send, 'span', 0, 0, tiled=True)  14.1 us
    ppermute x2, starting transfers between devices, exchange(): lax.ppermute(edge, 'chord', forward)  9.18 us
    all_to_all x1, waiting for transfers between devices, shards(): lax.all_to_all(amps.reshape((span_n * chord_n,) + amps.shape[2:]), ('span...  6.99 us
    ppermute x2, starting transfers between devices, exchange(): lax.ppermute(high, 'span', up)  4.51 us
    pallas_call x1, Pallas kernels, shards(): pl.pallas_call(amplitude_kernel, grid=(tiles,), out_shape=gram_shape, in_...  4.4 us
    pallas_call x1, Pallas kernels, shards(): pl.pallas_call(edges_kernel, grid=(count,), out_shape=(edge_shape, ends_s...  3.61 us
  transfers between devices with their start and end apart: 10, of which 1 were waited for; matrix products, arithmetic and copies ran while one was open for 2% of the time, Pallas kernels for 25%

profile of v8, /device:TPU:1, one launch (start us, length us, event | category | flops | bytes accessed | tf_op | source)
XLA Modules:
  0.0 100.6 jit_solution(8208116171610721039)
XLA Ops:
  0.6 0.0 copy-start.1
  0.6 0.0 copy-start.4
  0.7 3.6 %edges.1 = (bf16[3,2,64,128]{3,2,1,0:T(8,128)(2,1)}, bf16[3,3,64,128]{3,2,1,0:T(8,128)(2,1)}, bf16[3,3,64,128]{3,2,1,0:T(8,128)(2,1)}) custom-call(f32[3,32,64,128]{3,2,1,0:T(8,128)} %refs_10_.3), custom_call_target="tpu_custom_call" | custom-call | tf_op jit(solution)/shard_map/edges/pallas_call | solution.py:501
  4.3 2.6 %collective-permute-start = (bf16[3,3,64,128]{3,2,1,0:T(8,128)(2,1)}, bf16[3,3,64,128]{3,2,1,0:T(8,128)(2,1)S(1)}, u32[]{:S(2)}, u32[]{:S(2)}) collective-permute-start(bf16[3,3,64,128]{3,2,1,0:T(8,128)(2,1)} %get-tuple-element.26), channel_id=1, source_target_pairs={{0,8},{8,16},{16,24},{24,32},{32,40},{40,48},{48,56},{56,64},{64,7... | collective-permute-start | bytes 442376 | tf_op jit(solution)/shard_map/ppermute | solution.py:489
  6.9 0.7 collective-permute-start.1
  7.6 1.3 %collective-permute-start.3 = (bf16[3,2,64,128]{3,2,1,0:T(8,128)(2,1)}, bf16[3,2,64,128]{3,2,1,0:T(8,128)(2,1)S(1)}, u32[]{:S(2)}, u32[]{:S(2)}) collective-permute-start(bf16[3,2,64,128]{3,2,1,0:T(8,128)(2,1)} %get-tuple-element.28), channel_id=1, source_target_pairs={{1,0},{2,1},{3,2},{4,3},{5,4},{6,5},{7,6},{9,8},{10,9},{11,10},{12... | collective-permute-start | bytes 294920 | tf_op jit(solution)/shard_map/ppermute | solution.py:492
  8.9 4.0 %collective-permute-start.2 = (bf16[3,2,64,128]{3,2,1,0:T(8,128)(2,1)}, bf16[3,2,64,128]{3,2,1,0:T(8,128)(2,1)S(1)}, u32[]{:S(2)}, u32[]{:S(2)}) collective-permute-start(bf16[3,2,64,128]{3,2,1,0:T(8,128)(2,1)} %get-tuple-element.28), channel_id=1, source_target_pairs={{0,1},{1,2},{2,3},{3,4},{4,5},{5,6},{6,7},{8,9},{9,10},{10,11},{11... | collective-permute-start | bytes 294920 | tf_op jit(solution)/shard_map/ppermute | solution.py:491
  12.9 1.9 %spectra.1 = (bf16[32,256]{1,0:T(8,128)(2,1)}, bf16[32,32,256]{2,1,0:T(8,128)(2,1)}) custom-call(bf16[32,8,128]{2,1,0:T(8,128)(2,1)} %spectra_ref, s32[16]{0:T(128)} %wanted_ref.1), custom_call_target="tpu_custom_call" | custom-call | tf_op jit(solution)/shard_map/spectra/pallas_call | solution.py:513
  14.8 0.0 collective-permute-done.3.refs_4_
  14.8 0.0 copy-start.9
  14.8 0.0 collective-permute-done.2.refs_3_
  14.8 0.0 copy-start.10
  14.8 0.0 collective-permute-done.refs_1_
  14.8 0.0 copy-start.7
  14.9 0.0 collective-permute-done.1.refs_2_
  14.9 0.0 copy-start.8
  14.9 0.0 copy-start.11
  14.9 14.1 %all-to-all-start = ((bf16[32,32,256]{2,1,0:T(8,128)(2,1)}), bf16[32,32,256]{2,1,0:T(8,128)(2,1)}, u32[]{:S(2)}, u32[]{:S(2)}) async-start(bf16[32,32,256]{2,1,0:T(8,128)(2,1)} %get-tuple-element.38), calls=%async_computation | async-start | bytes 1048576 | tf_op jit(solution)/shard_map/all_to_all | solution.py:526
  29.0 0.0 copy-start.5
  29.0 0.0 copy-start.6
  29.0 0.0 copy-done.9
  29.0 0.0 copy-done.10
  29.0 0.0 copy-done.7
  29.0 0.0 copy-done.8
  29.0 0.0 copy-done.1
  29.0 0.0 copy-done.4
  29.0 11.7 %section_one_012.1 = (f32[3,32,64,128]{3,2,1,0:T(8,128)S(1)}, bf16[3,3,64,128]{3,2,1,0:T(8,128)(2,1)}, bf16[3,3,64,128]{3,2,1,0:T(8,128)(2,1)}, bf16[3,2,64,128]{3,2,1,0:T(8,128)(2,1)S(1)}) custom-call(f32[3,32,64,128]{3,2,1,0:T(8,128)} %refs_10_.3, bf16[3,3,64,128]{3,2,1,0:T(8,128)(2,1)} %copy-done.7, bf16[3,3,64,128]{3,2,1,0:T(8,128)(2,1)} %copy-done.8, ...), custom_call_target="tpu_custom_call" | custom-call | flops 60000000 | bytes 24000000 | tf_op jit(solution)/shard_map/section_one_012/pallas_call | solution.py:350
  40.8 1.3 %collective-permute-start.7 = (bf16[3,2,64,128]{3,2,1,0:T(8,128)(2,1)S(1)}, bf16[3,2,64,128]{3,2,1,0:T(8,128)(2,1)}, u32[]{:S(2)}, u32[]{:S(2)}) collective-permute-start(bf16[3,2,64,128]{3,2,1,0:T(8,128)(2,1)S(1)} %get-tuple-element.37), channel_id=1, source_target_pairs={{1,0},{2,1},{3,2},{4,3},{5,4},{6,5},{7,6},{9,8},{10,9},{11,10},{12... | collective-permute-start | bytes 294920 | tf_op jit(solution)/shard_map/ppermute | solution.py:492
  42.1 5.2 %collective-permute-start.6 = (bf16[3,2,64,128]{3,2,1,0:T(8,128)(2,1)S(1)}, bf16[3,2,64,128]{3,2,1,0:T(8,128)(2,1)}, u32[]{:S(2)}, u32[]{:S(2)}) collective-permute-start(bf16[3,2,64,128]{3,2,1,0:T(8,128)(2,1)S(1)} %get-tuple-element.37), channel_id=1, source_target_pairs={{0,1},{1,2},{2,3},{3,4},{4,5},{5,6},{6,7},{8,9},{9,10},{10,11},{11... | collective-permute-start | bytes 294920 | tf_op jit(solution)/shard_map/ppermute | solution.py:491
  47.3 1.9 %collective-permute-start.4 = (bf16[3,3,64,128]{3,2,1,0:T(8,128)(2,1)}, bf16[3,3,64,128]{3,2,1,0:T(8,128)(2,1)}, u32[]{:S(2)}, u32[]{:S(2)}) collective-permute-start(bf16[3,3,64,128]{3,2,1,0:T(8,128)(2,1)} %get-tuple-element.35), channel_id=1, source_target_pairs={{0,8},{8,16},{16,24},{24,32},{32,40},{40,48},{48,56},{56,64},{64,7... | collective-permute-start | bytes 442376 | tf_op jit(solution)/shard_map/ppermute | solution.py:489
  49.2 0.0 collective-permute-start.5
  49.2 0.0 copy-done.11
  49.2 0.9 copy.17
  50.1 0.6 copy.18
  50.7 0.9 copy.19.refs_12_
  51.6 0.0 all-to-all-done
  51.7 0.0 copy-done.5
  51.7 0.0 copy-done.6
  51.7 3.4 %gram_stored.1.known_ref = f32[2,8,32,1024]{3,2,1,0:T(8,128)S(1)} custom-call(f32[2,8,32,1024]{3,2,1,0:T(8,128)} %prior_ref.1, bf16[1024,256]{1,0:T(8,128)(2,1)} %bitcast.every_ref, bf16[32,256]{1,0:T(8,128)(2,1)S(1)} %copy-done.5, f32[1,256]{1,0:T(1,128)S(1)} %copy-done.6), custom_call_target="tpu_custom_call" | custom-call | flops 30000000 | bytes 12000000 | tf_op jit(solution)/shard_map/gram_stored/pallas_call | solution.py:541
  55.1 0.0 copy-start
  55.1 0.0 collective-permute-done.7.refs_4_
  55.1 0.0 collective-permute-done.6.refs_3_
  55.2 0.0 collective-permute-done.4.refs_1_
  55.2 0.0 collective-permute-done.5.refs_2_
  55.2 6.4 %section_two_0.1 = (f32[3,32,64,128]{3,2,1,0:T(8,128)}, bf16[32,8,4,128]{3,2,1,0:T(4,128)(2,1)S(1)}) custom-call(f32[3,32,64,128]{3,2,1,0:T(8,128)S(1)} %get-tuple-element.41.refs_0_, bf16[3,3,64,128]{3,2,1,0:T(8,128)(2,1)} %collective-permute-done.4.refs_1_, bf16[3,3,64,128]{3,2,1,0:T(8,128)(2,1)} %collective-permute-done.5.refs_2_, ...), custom_call_target="tpu_custom_call" | custom-call | flops 20000000 | bytes 8000000 | tf_op jit(solution)/shard_map/section_two_0/pallas_call | solution.py:350
  61.6 0.0 copy-done
  61.6 0.0 copy-start.2
  61.7 0.7 copy-done.2
  62.3 19.2 %all-to-all-start.1 = ((bf16[256,4,128]{2,1,0:T(4,128)(2,1)}), bf16[256,4,128]{2,1,0:T(4,128)(2,1)}, u32[]{:S(2)}, u32[]{:S(2)}) async-start(bf16[256,4,128]{2,1,0:T(4,128)(2,1)} %bitcast.7), calls=%async_computation.1 | async-start | bytes 524288 | tf_op jit(solution)/shard_map/all_to_all | solution.py:581
  81.6 0.0 copy-start.3
  81.6 7.6 %section_two_12.1 = f32[3,32,64,128]{3,2,1,0:T(8,128)} custom-call(f32[3,32,64,128]{3,2,1,0:T(8,128)S(1)} %get-tuple-element.41.refs_0_, bf16[3,3,64,128]{3,2,1,0:T(8,128)(2,1)} %collective-permute-done.4.refs_1_, bf16[3,3,64,128]{3,2,1,0:T(8,128)(2,1)} %collective-permute-done.5.refs_2_, ...), custom_call_target="tpu_custom_call", output_to_operand_aliasing={{}: (11, {})} | custom-call | flops 40000000 | bytes 16000000 | tf_op jit(solution)/shard_map/section_two_12/pallas_call | solution.py:350
  89.2 7.0 %all-to-all-done.1.amp_ref = bf16[256,4,128]{2,1,0:T(4,128)(2,1)} async-done(((bf16[256,4,128]{2,1,0:T(4,128)(2,1)}), bf16[256,4,128]{2,1,0:T(4,128)(2,1)}, u32[]{:S(2)}, u32[]{:S(2)}) %all-to-all-start.1) | async-done | bytes 262176 | tf_op jit(solution)/shard_map/all_to_all | solution.py:581
  96.2 0.0 copy-done.3
  96.2 4.4 %gram_amplitudes.1 = f32[2,8,32,1024]{3,2,1,0:T(8,128)} custom-call(f32[2,8,32,1024]{3,2,1,0:T(8,128)} %copy-done, bf16[256,4,128]{2,1,0:T(4,128)(2,1)} %all-to-all-done.1.amp_ref, s32[1]{0:T(128)} %bitcast.5.where_ref, bf16[2,128,128]{2,1,0:T(8,128)(2,1)S(1)} %copy-done.3), custom_call_target="tpu_custom_call" | custom-call | tf_op jit(solution)/shard_map/gram_amplitudes/pallas_call | solution.py:590
  (1 shorter events, 0.0 us)
Async XLA Ops:
  0.6 28.4 %copy-start.1 = (bf16[384,256]{1,0:T(8,128)(2,1)S(1)}, bf16[384,256]{1,0:T(8,128)(2,1)}, u32[]{:S(2)}) copy-start(bf16[384,256]{1,0:T(8,128)(2,1)} %constant.17.clone.refs_9_) | copy-start | bytes 589828
  0.6 28.4 %copy-start.4 = (f32[3,3]{1,0:T(4,128)S(1)}, f32[3,3]{1,0:T(4,128)}, u32[]{:S(2)}) copy-start(f32[3,3]{1,0:T(4,128)} %refs_8_.5) | copy-start | bytes 112
  4.3 10.6 %collective-permute-start = (bf16[3,3,64,128]{3,2,1,0:T(8,128)(2,1)}, bf16[3,3,64,128]{3,2,1,0:T(8,128)(2,1)S(1)}, u32[]{:S(2)}, u32[]{:S(2)}) collective-permute-start(bf16[3,3,64,128]{3,2,1,0:T(8,128)(2,1)} %get-tuple-element.26), channel_id=1, source_target_pairs={{0,8},{8,16},{16,24},{24,32},{32,40},{40,48},{48,56},{56,64},{64,7... | collective-permute-start | bytes 442376 | tf_op jit(solution)/shard_map/ppermute | solution.py:489
  6.9 8.0 %collective-permute-start.1 = (bf16[3,3,64,128]{3,2,1,0:T(8,128)(2,1)}, bf16[3,3,64,128]{3,2,1,0:T(8,128)(2,1)S(1)}, u32[]{:S(2)}, u32[]{:S(2)}) collective-permute-start(bf16[3,3,64,128]{3,2,1,0:T(8,128)(2,1)} %get-tuple-element.27), channel_id=1, source_target_pairs={{8,0},{16,8},{24,16},{32,24},{40,32},{48,40},{56,48},{64,56},{72,6... | collective-permute-start | bytes 442376 | tf_op jit(solution)/shard_map/ppermute | solution.py:490
  7.6 7.2 %collective-permute-start.3 = (bf16[3,2,64,128]{3,2,1,0:T(8,128)(2,1)}, bf16[3,2,64,128]{3,2,1,0:T(8,128)(2,1)S(1)}, u32[]{:S(2)}, u32[]{:S(2)}) collective-permute-start(bf16[3,2,64,128]{3,2,1,0:T(8,128)(2,1)} %get-tuple-element.28), channel_id=1, source_target_pairs={{1,0},{2,1},{3,2},{4,3},{5,4},{6,5},{7,6},{9,8},{10,9},{11,10},{12... | collective-permute-start | bytes 294920 | tf_op jit(solution)/shard_map/ppermute | solution.py:492
  8.9 6.0 %collective-permute-start.2 = (bf16[3,2,64,128]{3,2,1,0:T(8,128)(2,1)}, bf16[3,2,64,128]{3,2,1,0:T(8,128)(2,1)S(1)}, u32[]{:S(2)}, u32[]{:S(2)}) collective-permute-start(bf16[3,2,64,128]{3,2,1,0:T(8,128)(2,1)} %get-tuple-element.28), channel_id=1, source_target_pairs={{0,1},{1,2},{2,3},{3,4},{4,5},{5,6},{6,7},{8,9},{9,10},{10,11},{11... | collective-permute-start | bytes 294920 | tf_op jit(solution)/shard_map/ppermute | solution.py:491
  14.8 14.2 %copy-start.9 = (bf16[3,2,64,128]{3,2,1,0:T(8,128)(2,1)}, bf16[3,2,64,128]{3,2,1,0:T(8,128)(2,1)S(1)}, u32[]{:S(2)}) copy-start(bf16[3,2,64,128]{3,2,1,0:T(8,128)(2,1)S(1)} %collective-permute-done.3.refs_4_) | copy-start | bytes 294916
  14.8 14.2 %copy-start.10 = (bf16[3,2,64,128]{3,2,1,0:T(8,128)(2,1)}, bf16[3,2,64,128]{3,2,1,0:T(8,128)(2,1)S(1)}, u32[]{:S(2)}) copy-start(bf16[3,2,64,128]{3,2,1,0:T(8,128)(2,1)S(1)} %collective-permute-done.2.refs_3_) | copy-start | bytes 294916
  14.8 14.2 %copy-start.7 = (bf16[3,3,64,128]{3,2,1,0:T(8,128)(2,1)}, bf16[3,3,64,128]{3,2,1,0:T(8,128)(2,1)S(1)}, u32[]{:S(2)}) copy-start(bf16[3,3,64,128]{3,2,1,0:T(8,128)(2,1)S(1)} %collective-permute-done.refs_1_) | copy-start | bytes 442372
  14.9 14.1 %copy-start.8 = (bf16[3,3,64,128]{3,2,1,0:T(8,128)(2,1)}, bf16[3,3,64,128]{3,2,1,0:T(8,128)(2,1)S(1)}, u32[]{:S(2)}) copy-start(bf16[3,3,64,128]{3,2,1,0:T(8,128)(2,1)S(1)} %collective-permute-done.1.refs_2_) | copy-start | bytes 442372
  14.9 34.3 %copy-start.11 = (s32[32]{0:T(128)S(1)}, s32[32]{0:T(128)}, u32[]{:S(2)}) copy-start(s32[32]{0:T(128)} %param.18) | copy-start | bytes 388
  14.9 36.8 %all-to-all-start = ((bf16[32,32,256]{2,1,0:T(8,128)(2,1)}), bf16[32,32,256]{2,1,0:T(8,128)(2,1)}, u32[]{:S(2)}, u32[]{:S(2)}) async-start(bf16[32,32,256]{2,1,0:T(8,128)(2,1)} %get-tuple-element.38), calls=%async_computation | async-start | bytes 1048576 | tf_op jit(solution)/shard_map/all_to_all | solution.py:526
  29.0 22.7 %copy-start.5 = (bf16[32,256]{1,0:T(8,128)(2,1)S(1)}, bf16[32,256]{1,0:T(8,128)(2,1)}, u32[]{:S(2)}) copy-start(bf16[32,256]{1,0:T(8,128)(2,1)} %get-tuple-element.39.own_ref) | copy-start | bytes 49156
  29.0 22.7 %copy-start.6 = (f32[1,256]{1,0:T(1,128)S(1)}, f32[1,256]{1,0:T(1,128)}, u32[]{:S(2)}) copy-start(f32[1,256]{1,0:T(1,128)} %constant.18.clone.ramp_ref) | copy-start | bytes 3076
  40.8 14.4 %collective-permute-start.7 = (bf16[3,2,64,128]{3,2,1,0:T(8,128)(2,1)S(1)}, bf16[3,2,64,128]{3,2,1,0:T(8,128)(2,1)}, u32[]{:S(2)}, u32[]{:S(2)}) collective-permute-start(bf16[3,2,64,128]{3,2,1,0:T(8,128)(2,1)S(1)} %get-tuple-element.37), channel_id=1, source_target_pairs={{1,0},{2,1},{3,2},{4,3},{5,4},{6,5},{7,6},{9,8},{10,9},{11,10},{12... | collective-permute-start | bytes 294920 | tf_op jit(solution)/shard_map/ppermute | solution.py:492
  42.1 13.1 %collective-permute-start.6 = (bf16[3,2,64,128]{3,2,1,0:T(8,128)(2,1)S(1)}, bf16[3,2,64,128]{3,2,1,0:T(8,128)(2,1)}, u32[]{:S(2)}, u32[]{:S(2)}) collective-permute-start(bf16[3,2,64,128]{3,2,1,0:T(8,128)(2,1)S(1)} %get-tuple-element.37), channel_id=1, source_target_pairs={{0,1},{1,2},{2,3},{3,4},{4,5},{5,6},{6,7},{8,9},{9,10},{10,11},{11... | collective-permute-start | bytes 294920 | tf_op jit(solution)/shard_map/ppermute | solution.py:491
  47.3 7.9 %collective-permute-start.4 = (bf16[3,3,64,128]{3,2,1,0:T(8,128)(2,1)}, bf16[3,3,64,128]{3,2,1,0:T(8,128)(2,1)}, u32[]{:S(2)}, u32[]{:S(2)}) collective-permute-start(bf16[3,3,64,128]{3,2,1,0:T(8,128)(2,1)} %get-tuple-element.35), channel_id=1, source_target_pairs={{0,8},{8,16},{16,24},{24,32},{32,40},{40,48},{48,56},{56,64},{64,7... | collective-permute-start | bytes 442376 | tf_op jit(solution)/shard_map/ppermute | solution.py:489
  49.2 6.0 %collective-permute-start.5 = (bf16[3,3,64,128]{3,2,1,0:T(8,128)(2,1)}, bf16[3,3,64,128]{3,2,1,0:T(8,128)(2,1)}, u32[]{:S(2)}, u32[]{:S(2)}) collective-permute-start(bf16[3,3,64,128]{3,2,1,0:T(8,128)(2,1)} %get-tuple-element.36), channel_id=1, source_target_pairs={{8,0},{16,8},{24,16},{32,24},{40,32},{48,40},{56,48},{64,56},{72,6... | collective-permute-start | bytes 442376 | tf_op jit(solution)/shard_map/ppermute | solution.py:490
  55.1 6.5 %copy-start = (f32[2,8,32,1024]{3,2,1,0:T(8,128)}, f32[2,8,32,1024]{3,2,1,0:T(8,128)S(1)}, u32[]{:S(2)}) copy-start(f32[2,8,32,1024]{3,2,1,0:T(8,128)S(1)} %gram_stored.1.known_ref) | copy-start | bytes 6291460
  61.6 0.7 copy-start.2
  62.3 33.9 %all-to-all-start.1 = ((bf16[256,4,128]{2,1,0:T(4,128)(2,1)}), bf16[256,4,128]{2,1,0:T(4,128)(2,1)}, u32[]{:S(2)}, u32[]{:S(2)}) async-start(bf16[256,4,128]{2,1,0:T(4,128)(2,1)} %bitcast.7), calls=%async_computation.1 | async-start | bytes 524288 | tf_op jit(solution)/shard_map/all_to_all | solution.py:581
  81.6 14.6 %copy-start.3 = (bf16[2,128,128]{2,1,0:T(8,128)(2,1)S(1)}, bf16[2,128,128]{2,1,0:T(8,128)(2,1)}, u32[]{:S(2)}) copy-start(bf16[2,128,128]{2,1,0:T(8,128)(2,1)} %constant.19.clone.rep_ref) | copy-start | bytes 196612
